TPU v7x, 32 devices: a whole 2x2x4 slice. The times are simulated.
32 devices in a mesh: groups: 2 (over x), tm: 16 (over z, y, core).
Axes of the slice: x: 2, y: 2, z: 4, core: 2. Of those that a mesh axis runs over, the one named last changes fastest.
Arguments:
- tokens: bfloat16 [8192, 1024], P(('groups', 'tm')), parts along dimension 0, may hold values from -16 to 16
- log_decay: float32 [8, 8192], P(None, ('groups', 'tm')), parts along dimension 1, may hold values from -1.5 to 0
- mem_index: int32 [64, 8], P(('groups', 'tm')), parts along dimension 0, may hold values from 0 to 29, as said below
- mem_count: int32 [64], P(('groups', 'tm')), parts along dimension 0, may hold values from 0 to 8
- w_rq: bfloat16 [1024, 512], replicated, may hold values from -0.1875 to 0.1875
- w_rk: bfloat16 [1024, 512], replicated, may hold values from -0.1875 to 0.1875
- w_rv: bfloat16 [1024, 1024], replicated, may hold values from -0.1875 to 0.1875
- norm_gain: float32 [1024], replicated, may hold values from 0.5 to 1.5
- w_mq: bfloat16 [1024, 512], replicated, may hold values from -1 to 1
- w_mk: bfloat16 [1024, 512], replicated, may hold values from -1 to 1
- w_mv: bfloat16 [1024, 512], replicated, may hold values from -0.1875 to 0.1875
- w_out: bfloat16 [512, 1024], replicated, may hold values from -0.25 to 0.25
Outputs:
- layer_out: bfloat16 [8192, 1024], P(('groups', 'tm')), parts along dimension 0
There are 2 independent parts, one for each index of `groups`. A program takes and returns all parts, laid end to end along the dimension named above; an argument that names none is the same for every part. Nothing has to cross between parts.
Inputs may be any that keep to these rules, and one draw needn't show every extreme that they name: `mem_index`: entries i < mem_count[f] of frame f's list are distinct frames held by lower indices of tm than frame f's own; all the live entries of the 2 frames of one index of tm name at most one frame of any other index.
All inputs are finite; a program needn't handle non-finite values.
Results may differ from a plain program's by a relative error of at most 0.04.
Values may be sent and summed in bfloat16 or wider, within the bound.
No kernel may reach another device: no remote copies, remote signals or barrier semaphores. Data moves between devices by JAX's collectives and lax.ppermute only.
A program may use at most 128 MiB of HBM per device.

v0:
```python
import functools

import jax
import jax.numpy as jnp
from jax import lax
from jax.experimental import pallas as pl
from jax.experimental.pallas import tpu as pltpu
from jax.sharding import PartitionSpec as P


H = 8
DK = 64
DV = 128
MH = 4
MD = 128
MC = 512
P_SIZE = 128
BLK = 64
LANES = 4
HC = H // LANES
ROWS = HC * 2 * DK
TAIL = 16
PAIRS = HC * 2
NEG = -1e30
F32 = jnp.float32
BF16 = jnp.bfloat16


VMEM = pl.BlockSpec(memory_space=pltpu.VMEM)
SMEM = pl.BlockSpec(memory_space=pltpu.SMEM)
HBM = pl.BlockSpec(memory_space=pltpu.HBM)


def params(mib=48):
    return pltpu.CompilerParams(vmem_limit_bytes=mib << 20)


def cost(flops, nbytes):
    return pl.CostEstimate(flops=flops, bytes_accessed=nbytes, transcendentals=0)


def chain_of(iota):
    return (iota // BLK) % 2


def nn(a, b, **kw):
    return lax.dot_general(a, b, (((1,), (0,)), ((), ())), preferred_element_type=F32, **kw)


def nt(a, b, **kw):
    return lax.dot_general(a, b, (((1,), (1,)), ((), ())), preferred_element_type=F32, **kw)


def tn(a, b, **kw):
    return lax.dot_general(a, b, (((0,), (0,)), ((), ())), preferred_element_type=F32, **kw)


def by_chain(x):
    rows = x.shape[0]
    chain = chain_of(lax.broadcasted_iota(jnp.int32, (rows, DK), 0))
    zero = jnp.zeros_like(x)
    return jnp.concatenate([jnp.where(chain == 0, x, zero), jnp.where(chain == 1, x, zero)], axis=1)


def split3(x):
    hi = x.astype(BF16)
    rest = x - hi.astype(F32)
    mid = rest.astype(BF16)
    return hi, mid, (rest - mid.astype(F32)).astype(BF16)


def read_message(x):
    state = x[:ROWS].astype(F32)
    tail = x[ROWS:].astype(F32)
    total = tail[0:PAIRS] + tail[PAIRS : 2 * PAIRS] + tail[2 * PAIRS : 3 * PAIRS]
    return state, total


def spread(total):
    return jnp.concatenate(
        [jnp.broadcast_to(total[p : p + 1], (DK, total.shape[1])) for p in range(PAIRS)], axis=0
    )


def write_message(ref, state, total):
    ref[:ROWS, :] = state.astype(BF16)
    hi, mid, lo = split3(total)
    pad = jnp.zeros((TAIL - 3 * PAIRS, total.shape[1]), F32)
    ref[ROWS:, :] = jnp.concatenate(
        [hi.astype(F32), mid.astype(F32), lo.astype(F32), pad], axis=0
    ).astype(BF16)


def local_kernel(x_in, ld_in, wk_ref, wv_ref, k_ref, v_ref, *rest):
    outs, (chunks, x_ref, ld_ref, bk, bv, sems, own) = rest[:LANES], rest[LANES:]
    rows = x_ref.shape[0]
    first = [
        pltpu.make_async_copy(ld_in, ld_ref, own.at[0]),
        pltpu.make_async_copy(x_in, x_ref, own.at[1]),
    ]
    for copy in first:
        copy.start()
    copies = []
    for q in range(LANES):
        kc, vc = slice(q * HC * DK, (q + 1) * HC * DK), slice(q * HC * DV, (q + 1) * HC * DV)
        copies.append(
            (
                pltpu.make_async_copy(wk_ref.at[:, kc], bk.at[:, kc], sems.at[0, q]),
                pltpu.make_async_copy(wv_ref.at[:, vc], bv.at[:, vc], sems.at[1, q]),
            )
        )
    for pair in copies:
        for copy in pair:
            copy.start()
    first[0].wait()
    ld = ld_ref[...]
    t = lax.broadcasted_iota(jnp.int32, (rows, rows), 0)
    s = lax.broadcasted_iota(jnp.int32, (rows, rows), 1)
    after = ((s > t) & (chain_of(s) == chain_of(t))).astype(F32)
    tail = jnp.exp(nt(after, ld, precision=lax.Precision.HIGHEST))
    chain = chain_of(lax.broadcasted_iota(jnp.int32, ld.shape, 1))
    sums = [jnp.sum(jnp.where(chain == b, ld, 0.0), axis=1, keepdims=True) for b in (0, 1)]
    first[1].wait()
    x = x_ref[...]
    for q in range(LANES):
        for copy in copies[q]:
            copy.wait()
        kc, vc = slice(q * HC * DK, (q + 1) * HC * DK), slice(q * HC * DV, (q + 1) * HC * DV)
        k = nn(x, bk[:, kc]).astype(BF16)
        v = nn(x, bv[:, vc]).astype(BF16)
        k_ref[:, kc] = k
        v_ref[:, vc] = v
        states, totals = [], []
        for i in range(HC):
            h = q * HC + i
            kt = (k[:, i * DK : (i + 1) * DK].astype(F32) * tail[:, h : h + 1]).astype(BF16)
            states.append(tn(by_chain(kt), v[:, i * DV : (i + 1) * DV]))
            totals += [jnp.broadcast_to(sums[b][h : h + 1], (1, DV)) for b in (0, 1)]
        write_message(
            chunks.at[q], jnp.concatenate(states, axis=0), jnp.concatenate(totals, axis=0)
        )
    lane = lax.rem(lax.axis_index("tm"), LANES)
    for f in range(LANES):
        outs[f][...] = chunks[lane ^ f]


def local(tokens, w_rk, w_rv, ld):
    rows, d = tokens.shape
    message = jax.ShapeDtypeStruct((ROWS + TAIL, DV), BF16)
    return pl.pallas_call(
        local_kernel,
        in_specs=[HBM] * 4,
        out_specs=[VMEM] * (2 + LANES),
        out_shape=[
            jax.ShapeDtypeStruct((rows, H * DK), BF16),
            jax.ShapeDtypeStruct((rows, H * DV), BF16),
        ]
        + [message] * LANES,
        scratch_shapes=[
            pltpu.VMEM((LANES, ROWS + TAIL, DV), BF16),
            pltpu.VMEM((rows, d), BF16),
            pltpu.VMEM((H, rows), F32),
            pltpu.VMEM((d, H * DK), BF16),
            pltpu.VMEM((d, H * DV), BF16),
            pltpu.SemaphoreType.DMA((2, LANES)),
            pltpu.SemaphoreType.DMA((2,)),
        ],
        compiler_params=params(62),
        name="local",
    )(tokens, ld, w_rk, w_rv)


def list_live(frames, distances, tables, groups):
    me = lax.axis_index("tm")
    lane = lax.rem(me, LANES)
    plane = me // LANES
    spans = len(distances)
    for part in range(spans):
        table, counts, need = tables[3 * part : 3 * part + 3]

        def clear(b, _, need=need, part=part):
            need[b] = (b < frames).astype(jnp.int32) if part == 0 else jnp.int32(0)
            return 0

        lax.fori_loop(0, need.shape[0], clear, 0)
        for g in range(2):
            for f in range(frames):
                counts[g * frames + f] = jnp.int32(1 if part == 0 and g == 0 else 0)
                if part == 0 and g == 0:
                    table[f, 0] = jnp.int32(f)
    for g, (index, live) in enumerate(groups):
        slots = index.shape[1]
        for f in range(frames):
            row = g * frames + f

            def visit(i, carry, index=index, f=f, row=row):
                frame = index[f, i]
                owner = frame // frames
                its = lax.rem(owner, LANES)
                here = (its // 2) == (lane // 2)
                distance = plane - owner // LANES
                for part, (low, high) in enumerate(distances):
                    table, counts, need = tables[3 * part : 3 * part + 3]

                    @pl.when(here & (distance >= low) & (distance < high))
                    def _(table=table, counts=counts, need=need, low=low):
                        block = ((distance - low) * 2 + ((its ^ lane) & 1)) * frames
                        block = block + lax.rem(frame, frames)
                        n = counts[row]
                        table[row, n] = block
                        need[block] = 1
                        counts[row] = n + 1

                return carry

            lax.fori_loop(0, jnp.minimum(live[f], slots), visit, 0)


def inner_kernel(frames, distances, *refs):
    x_ref, ld_ref, k_ref, v_ref, idx, cnt, pidx, pcnt, wq_ref = refs[:9]
    inner_ref, qq_ref = refs[9:11]
    tables, (bq, sem) = refs[11:-2], refs[-2:]
    copy = pltpu.make_async_copy(wq_ref, bq, sem)
    copy.start()
    list_live(frames, distances, tables, ((idx, cnt), (pidx, pcnt)))
    rows = x_ref.shape[0]
    ld = ld_ref[...]
    t = lax.broadcasted_iota(jnp.int32, (rows, rows), 0)
    s = lax.broadcasted_iota(jnp.int32, (rows, rows), 1)
    upto = (s <= t) & (chain_of(s) == chain_of(t))
    ones = upto.astype(F32)
    column = nt(ones, ld, precision=lax.Precision.HIGHEST)
    row = nt(ld, ones, precision=lax.Precision.HIGHEST)
    grown = jnp.exp(column) * DK**-0.5
    copy.wait()
    q = nn(x_ref[...], bq[...]).astype(BF16)
    for h in range(H):
        qh = q[:, h * DK : (h + 1) * DK]
        gap = column[:, h : h + 1] - row[h : h + 1, :]
        weight = jnp.exp(jnp.where(upto, gap, NEG)) * DK**-0.5
        scores = nt(qh, k_ref[:, h * DK : (h + 1) * DK]) * weight
        inner_ref[:, h * DV : (h + 1) * DV] = nn(
            scores.astype(BF16), v_ref[:, h * DV : (h + 1) * DV]
        )
        scaled = qh.astype(F32) * grown[:, h : h + 1]
        qq_ref[:, h * 2 * DK : (h + 1) * 2 * DK] = by_chain(scaled.astype(BF16))


def inner(tokens, w_rq, k, v, ld, index, live, pindex, plive, distances):
    rows, d = tokens.shape
    frames = rows // P_SIZE
    slots = index.shape[1]
    table_shapes = []
    for low, high in distances:
        table_shapes += [
            jax.ShapeDtypeStruct((2 * frames, slots + 1), jnp.int32),
            jax.ShapeDtypeStruct((2 * frames,), jnp.int32),
            jax.ShapeDtypeStruct(((high - low) * 2 * frames,), jnp.int32),
        ]
    out = pl.pallas_call(
        functools.partial(inner_kernel, frames, distances),
        in_specs=[VMEM] * 4 + [SMEM] * 4 + [HBM],
        out_specs=[VMEM] * 2 + [SMEM] * len(table_shapes),
        out_shape=[
            jax.ShapeDtypeStruct((rows, H * DV), F32),
            jax.ShapeDtypeStruct((rows, H * 2 * DK), BF16),
        ]
        + table_shapes,
        scratch_shapes=[pltpu.VMEM((d, H * DK), BF16), pltpu.SemaphoreType.DMA(())],
        compiler_params=params(),
        cost_estimate=cost(2 * rows * d * H * DK, 8 << 20),
        name="inner",
    )(tokens, ld, k, v, index, live, pindex, plive, w_rq)
    return out[0], out[1], [out[2 + 3 * i : 5 + 3 * i] for i in range(len(distances))]


def plane_kernel(*refs):
    parts, out, ordered = refs[:LANES], refs[LANES], refs[LANES + 1]
    lane = lax.rem(lax.axis_index("tm"), LANES)
    for f in range(LANES):
        ordered[lane ^ f] = parts[f][...]
    state, total = read_message(ordered[0])
    for i in range(1, LANES):
        mine, decay = read_message(ordered[i])
        state = spread(jnp.exp(decay)) * state + mine
        total = total + decay
    write_message(out, state, total)


def plane_total(parts):
    return pl.pallas_call(
        plane_kernel,
        in_specs=[VMEM] * LANES,
        out_specs=VMEM,
        out_shape=jax.ShapeDtypeStruct((ROWS + TAIL, DV), BF16),
        scratch_shapes=[pltpu.VMEM((LANES, ROWS + TAIL, DV), BF16)],
        compiler_params=params(),
        name="plane",
    )(*parts)


def prefix_kernel(count, *refs):
    parts, earlier = refs[:LANES], refs[LANES : LANES + count]
    outs = refs[LANES + count : 2 * LANES + count]
    ordered, results = refs[2 * LANES + count :]
    lane = lax.rem(lax.axis_index("tm"), LANES)
    for f in range(LANES):
        ordered[lane ^ f] = parts[f][...]
    state = jnp.zeros((ROWS, DV), F32)
    for ref in reversed(earlier):
        mine, decay = read_message(ref[...])
        state = spread(jnp.exp(decay)) * state + mine
    for i in range(LANES):
        results[i] = state.astype(BF16)
        if i + 1 < LANES:
            mine, decay = read_message(ordered[i])
            state = spread(jnp.exp(decay)) * state + mine
    for f in range(LANES):
        outs[f][...] = results[lane ^ f]


def prefix(parts, earlier):
    return pl.pallas_call(
        functools.partial(prefix_kernel, len(earlier)),
        in_specs=[VMEM] * (LANES + len(earlier)),
        out_specs=[VMEM] * LANES,
        out_shape=[jax.ShapeDtypeStruct((ROWS, DV), BF16)] * LANES,
        scratch_shapes=[
            pltpu.VMEM((LANES, ROWS + TAIL, DV), BF16),
            pltpu.VMEM((LANES, ROWS, DV), BF16),
        ],
        compiler_params=params(),
        name="prefix",
    )(*parts, *earlier)


def hidden_kernel(frames, *refs):
    inner_ref, qq_ref = refs[:2]
    states = refs[2 : 2 + LANES]
    x_ref, gain_ref, wq, wk, wv = refs[2 + LANES : 7 + LANES]
    hid_ref, q_ref = refs[7 + LANES : 9 + LANES]
    kv_refs = refs[9 + LANES : 9 + LANES + frames]
    ordered, bq, bk, bv, sems = refs[9 + LANES + frames :]
    copies = [
        pltpu.make_async_copy(src, dst, sems.at[i])
        for i, (src, dst) in enumerate(((wq, bq), (wk, bk), (wv, bv)))
    ]
    for copy in copies:
        copy.start()
    lane = lax.rem(lax.axis_index("tm"), LANES)
    for f in range(LANES):
        ordered[lane ^ f] = states[f][...]
    for h in range(H):
        cols = slice(h * DV, (h + 1) * DV)
        state = ordered[h // HC, (h % HC) * 2 * DK : (h % HC + 1) * 2 * DK, :]
        o = inner_ref[:, cols] + nn(qq_ref[:, h * 2 * DK : (h + 1) * 2 * DK], state)
        scale = lax.rsqrt(jnp.mean(o * o, axis=1, keepdims=True) + 1e-05)
        y = o * scale * gain_ref[:, cols]
        hid_ref[:, cols] = (x_ref[:, cols].astype(F32) + y).astype(BF16)
    hid = hid_ref[...]
    copies[0].wait()
    q_ref[...] = nn(hid, bq[...]).astype(BF16)
    for i, buf in ((1, bk), (2, bv)):
        copies[i].wait()
        part = nn(hid, buf[...]).astype(BF16)
        for f in range(frames):
            kv_refs[f][:, (i - 1) * MC : i * MC] = part[f * P_SIZE : (f + 1) * P_SIZE]


def hidden_of(inner_out, qq, states, tokens, gain, w_mq, w_mk, w_mv):
    rows, d = tokens.shape
    frames = rows // P_SIZE
    return pl.pallas_call(
        functools.partial(hidden_kernel, frames),
        in_specs=[VMEM] * (LANES + 4) + [HBM] * 3,
        out_specs=[VMEM] * (2 + frames),
        out_shape=[
            jax.ShapeDtypeStruct((rows, d), BF16),
            jax.ShapeDtypeStruct((rows, MC), BF16),
        ]
        + [jax.ShapeDtypeStruct((P_SIZE, 2 * MC), BF16)] * frames,
        scratch_shapes=[pltpu.VMEM((LANES, ROWS, DV), BF16)]
        + [pltpu.VMEM((d, MC), BF16)] * 3
        + [pltpu.SemaphoreType.DMA((3,))],
        compiler_params=params(),
        name="hidden",
    )(inner_out, qq, *states, tokens, gain.reshape(1, d), w_mq, w_mk, w_mv)


def attend_kernel(frames, blocks, first, last, *refs):
    table, counts, need, q_ref, pq_ref = refs[:5]
    refs = refs[5:]
    if not first:
        acc_in, stat_in = refs[:2]
        refs = refs[2:]
    kv_refs = refs[:blocks]
    refs = refs[blocks:]
    if last:
        o_ref, po_ref, lse_ref, plse_ref = refs[:4]
        refs = refs[4:]
    else:
        acc_out, stat_out = refs[:2]
        refs = refs[2:]
    kv, scores, peak, total, acc, stat, sems = refs
    copies = [pltpu.make_async_copy(kv_refs[b], kv.at[b], sems.at[b]) for b in range(blocks)]
    for b in range(blocks):

        @pl.when(need[b] == 1)
        def _(b=b):
            copies[b].start()

    for b in range(blocks):

        @pl.when(need[b] == 1)
        def _(b=b):
            copies[b].wait()

    scale = MD**-0.5
    for row in range(2 * frames):
        queries = q_ref if row < frames else pq_ref
        f = row % frames
        span = slice(f * P_SIZE, (f + 1) * P_SIZE)
        held = slice(row * P_SIZE, (row + 1) * P_SIZE)
        n = counts[row]
        if first:
            stat[...] = jnp.zeros_like(stat)
            acc[...] = jnp.zeros_like(acc)
            peak[...] = jnp.full_like(peak, NEG)
        else:
            stat[...] = stat_in[held, :]
            for e in range(MH):
                acc[e] = acc_in[held, e * MD : (e + 1) * MD]

        @pl.when(n > 0)
        def _(row=row, queries=queries, span=span, n=n):
            if not first:
                for e in range(MH):
                    peak[e] = jnp.broadcast_to(stat[:, e : e + 1], (P_SIZE, P_SIZE))
            total[...] = jnp.zeros_like(total)
            half = (n + 1) // 2

            def score(i, _):
                b0 = table[row, 2 * i]
                more = 2 * i + 1 < n
                b1 = jnp.where(more, table[row, jnp.minimum(2 * i + 1, n - 1)], b0)
                for e in range(MH):
                    cols = slice(e * MD, (e + 1) * MD)
                    s0 = nt(queries[span, cols], kv[b0, :, cols])
                    s1 = nt(queries[span, cols], kv[b1, :, cols])
                    s1 = jnp.where(more, s1, NEG)
                    scores[2 * i, e] = s0
                    scores[2 * i + 1, e] = s1
                    peak[e] = jnp.maximum(peak[e], jnp.maximum(s0, s1))
                return 0

            lax.fori_loop(0, half, score, 0)
            for e in range(MH):
                top = jnp.max(peak[e], axis=1, keepdims=True)
                peak[e] = jnp.broadcast_to(top, (P_SIZE, P_SIZE))
                if not first:
                    fade = jnp.exp((stat[:, e : e + 1] - top) * scale)
                    acc[e] = acc[e] * fade
                    stat[:, MH + e : MH + e + 1] = stat[:, MH + e : MH + e + 1] * fade
                stat[:, e : e + 1] = top

            def weigh(i, _):
                b0 = table[row, 2 * i]
                b1 = table[row, jnp.minimum(2 * i + 1, n - 1)]
                for e in range(MH):
                    cols = slice(MC + e * MD, MC + (e + 1) * MD)
                    p0 = jnp.exp((scores[2 * i, e] - peak[e]) * scale)
                    p1 = jnp.exp((scores[2 * i + 1, e] - peak[e]) * scale)
                    total[e] += p0 + p1
                    acc[e] += nn(p0.astype(BF16), kv[b0, :, cols]) + nn(
                        p1.astype(BF16), kv[b1, :, cols]
                    )
                return 0

            lax.fori_loop(0, half, weigh, 0)
            for e in range(MH):
                stat[:, MH + e : MH + e + 1] += jnp.sum(total[e], axis=1, keepdims=True)

        if first:

            @pl.when(n == 0)
            def _():
                for e in range(MH):
                    stat[:, e : e + 1] = jnp.full((P_SIZE, 1), NEG, F32)

        if last:
            out, stats = (o_ref, lse_ref) if row < frames else (po_ref, plse_ref)
            for e in range(MH):
                l = jnp.maximum(stat[:, MH + e : MH + e + 1], 1e-30)
                out[span, e * MD : (e + 1) * MD] = (acc[e] / l).astype(out.dtype)
            flat = jnp.transpose(stat[...])
            low = jnp.log(jnp.maximum(flat[MH : 2 * MH], 1e-30))
            stats[:, span] = jnp.concatenate([flat[:MH] * scale + low, low], axis=0)
        else:
            stat_out[held, :] = stat[...]
            for e in range(MH):
                acc_out[held, e * MD : (e + 1) * MD] = acc[e]


def attend(tables, q, pq, kvs, state, last):
    rows = q.shape[0]
    frames = rows // P_SIZE
    blocks = len(kvs)
    slots = tables[0].shape[1]
    first = state is None
    state = [] if first else list(state)
    if last:
        out_shape = [
            jax.ShapeDtypeStruct((rows, MC), F32),
            jax.ShapeDtypeStruct((rows, MC), BF16),
            jax.ShapeDtypeStruct((2 * MH, rows), F32),
            jax.ShapeDtypeStruct((2 * MH, rows), F32),
        ]
    else:
        out_shape = [
            jax.ShapeDtypeStruct((2 * rows, MC), F32),
            jax.ShapeDtypeStruct((2 * rows, 128), F32),
        ]
    return pl.pallas_call(
        functools.partial(attend_kernel, frames, blocks, first, last),
        in_specs=[SMEM] * 3 + [VMEM] * (2 + len(state)) + [HBM] * blocks,
        out_specs=[VMEM] * len(out_shape),
        out_shape=out_shape,
        scratch_shapes=[
            pltpu.VMEM((blocks, P_SIZE, 2 * MC), BF16),
            pltpu.VMEM((slots + 2, MH, P_SIZE, P_SIZE), F32),
            pltpu.VMEM((MH, P_SIZE, P_SIZE), F32),
            pltpu.VMEM((MH, P_SIZE, P_SIZE), F32),
            pltpu.VMEM((MH, P_SIZE, MD), F32),
            pltpu.VMEM((P_SIZE, 128), F32),
            pltpu.SemaphoreType.DMA((blocks,)),
        ],
        compiler_params=params(),
        cost_estimate=cost(4 * 8 * frames * P_SIZE * P_SIZE * MC, blocks * P_SIZE * MC * 4),
        name="attend_last" if last else "attend",
    )(*tables, q, pq, *state, *kvs)


def output_kernel(o_ref, lse_ref, po_ref, plse_ref, hid_ref, w_ref, out_ref, mixed):
    rows = o_ref.shape[0]
    mine, other = lse_ref[...], plse_ref[...]
    top = jnp.maximum(mine, other)
    a, b = jnp.exp(mine - top), jnp.exp(other - top)
    inv = 1.0 / (a + b)
    both = jnp.concatenate([a * inv, b * inv, jnp.zeros((128 - 16, rows), F32)], axis=0)
    weights = jnp.transpose(both)
    for e in range(MH):
        cols = slice(e * MD, (e + 1) * MD)
        value = o_ref[:, cols] * weights[:, e : e + 1]
        value = value + po_ref[:, cols].astype(F32) * weights[:, 8 + e : 9 + e]
        mixed[:, cols] = value.astype(BF16)
    out_ref[...] = (hid_ref[...].astype(F32) + nn(mixed[...], w_ref[...])).astype(BF16)


def output(o, lse, po, plse, hid, w_out):
    rows, d = hid.shape
    return pl.pallas_call(
        output_kernel,
        in_specs=[VMEM] * 6,
        out_specs=VMEM,
        out_shape=jax.ShapeDtypeStruct((rows, d), BF16),
        scratch_shapes=[pltpu.VMEM((rows, MC), BF16)],
        compiler_params=params(),
        name="output",
    )(o, lse, po, plse, hid, w_out)


def on_device(
    tokens, log_decay, mem_index, mem_count, w_rq, w_rk, w_rv, norm_gain, w_mq, w_mk, w_mv, w_out
):
    size = lax.axis_size("tm")
    planes = size // LANES

    def flip(x, bits):
        return lax.ppermute(x, "tm", [(i, i ^ bits) for i in range(size)])

    def up(x, distance):
        step = distance * LANES
        return lax.ppermute(x, "tm", [(i, i + step) for i in range(size - step)])

    spans = ((0, planes - 1), (planes - 1, planes)) if planes > 1 else ((0, planes),)
    partner_index, partner_count = flip(mem_index, 2), flip(mem_count, 2)
    k, v, *chunks = local(tokens, w_rk, w_rv, log_decay)
    parts = [chunks[0]] + [flip(chunks[f], f) for f in range(1, LANES)]
    inner_out, qq, tables = inner(
        tokens, w_rq, k, v, log_decay, mem_index, mem_count, partner_index, partner_count, spans
    )
    total = plane_total(parts)
    earlier = [up(total, distance) for distance in range(1, planes)]
    mine = prefix(parts, earlier)
    states = [mine[0]] + [flip(mine[f], f) for f in range(1, LANES)]
    hid, q, *kv = hidden_of(inner_out, qq, states, tokens, norm_gain, w_mq, w_mk, w_mv)
    partner_q = flip(q, 2)
    held = []
    for distance in range(planes):
        if distance:
            moved = []
            for x in kv:
                moved.append(up(x, 1))
            kv = moved
        near = []
        for x in kv:
            near.append(flip(x, 1))
        held.append(kv + near)
    state = None
    for (low, high), table in zip(spans, tables):
        blocks = [x for group in held[low:high] for x in group]
        state = attend(table, q, partner_q, blocks, state, high == planes)
    o, po, lse, plse = state
    return output(o, lse, flip(po, 2), flip(plse, 2), hid, w_out)


def solution(mesh):
    placed = (
        P(("groups", "tm"), None),
        P(None, ("groups", "tm")),
        P(("groups", "tm"), None),
        P(("groups", "tm")),
        P(),
        P(),
        P(),
        P(),
        P(),
        P(),
        P(),
        P(),
    )

    return jax.shard_map(
        on_device, mesh=mesh, in_specs=placed, out_specs=P(("groups", "tm"), None), check_vma=False
    )
```

profile of v0, /device:TPU:27, one launch (start us, length us, event | category | flops | bytes accessed | tf_op | source)
XLA Modules:
  0.0 100.7 jit_solution(4398714451735188527)
XLA Ops:
  0.0 6.1 %local.1 = (bf16[256,512]{1,0:T(8,128)(2,1)}, bf16[256,1024]{1,0:T(8,128)(2,1)}, bf16[272,128]{1,0:T(8,128)(2,1)}, bf16[272,128]{1,0:T(8,128)(2,1)}, bf16[272,128]{1,0:T(8,128)(2,1)}, /*index=5*/bf16[272,128]{1,0:T(8,128)(2,1)}) custom-call(bf16[256,1024]{1,0:T(8,128)(2,1)} %refs_6_.1, f32[8,256]{1,0:T(8,128)} %refs_1_.1, bf16[1024,512]{1,0:T(8,128)(2,1)} %wk_ref.1, ...), custom_call_target="tpu_custom_call" | custom-call | tf_op jit(solution)/shard_map/local/pallas_call | solution.py:150
  8.6 2.2 %collective-permute-done.3.refs_2_ = bf16[272,128]{1,0:T(8,128)(2,1)S(1)} collective-permute-done((bf16[272,128]{1,0:T(8,128)(2,1)}, bf16[272,128]{1,0:T(8,128)(2,1)S(1)}, u32[]{:S(2)}, u32[]{:S(2)}) %collective-permute-start.3) | collective-permute-done | bytes 69664 | tf_op jit(solution)/shard_map/ppermute | solution.py:579
  10.8 1.7 %collective-permute-done.4.refs_3_ = bf16[272,128]{1,0:T(8,128)(2,1)S(1)} collective-permute-done((bf16[272,128]{1,0:T(8,128)(2,1)}, bf16[272,128]{1,0:T(8,128)(2,1)S(1)}, u32[]{:S(2)}, u32[]{:S(2)}) %collective-permute-start.4) | collective-permute-done | bytes 69664 | tf_op jit(solution)/shard_map/ppermute | solution.py:579
  13.5 1.3 %collective-permute-start.5 = (bf16[272,128]{1,0:T(8,128)(2,1)S(1)}, bf16[272,128]{1,0:T(8,128)(2,1)S(1)}, u32[]{:S(2)}, u32[]{:S(2)}) collective-permute-start(bf16[272,128]{1,0:T(8,128)(2,1)S(1)} %plane.1), channel_id=1, source_target_pairs={{0,4},{1,5},{2,6},{3,7},{4,8},{5,9},{6,10},{7,11},{8,12},{9,13},{1... | collective-permute-start | bytes 208904 | tf_op jit(solution)/shard_map/ppermute | solution.py:583
  14.8 1.3 %collective-permute-start.6 = (bf16[272,128]{1,0:T(8,128)(2,1)S(1)}, bf16[272,128]{1,0:T(8,128)(2,1)S(1)}, u32[]{:S(2)}, u32[]{:S(2)}) collective-permute-start(bf16[272,128]{1,0:T(8,128)(2,1)S(1)} %plane.1), channel_id=1, source_target_pairs={{0,8},{1,9},{2,10},{3,11},{4,12},{5,13},{6,14},{7,15},{16,24},{17,... | collective-permute-start | bytes 208904 | tf_op jit(solution)/shard_map/ppermute | solution.py:583
  16.1 1.3 %collective-permute-start.7 = (bf16[272,128]{1,0:T(8,128)(2,1)S(1)}, bf16[272,128]{1,0:T(8,128)(2,1)S(1)}, u32[]{:S(2)}, u32[]{:S(2)}) collective-permute-start(bf16[272,128]{1,0:T(8,128)(2,1)S(1)} %plane.1), channel_id=1, source_target_pairs={{0,12},{1,13},{2,14},{3,15},{16,28},{17,29},{18,30},{19,31}} | collective-permute-start | bytes 208904 | tf_op jit(solution)/shard_map/ppermute | solution.py:583
  18.6 2.2 %collective-permute-done.6.refs_5_ = bf16[272,128]{1,0:T(8,128)(2,1)S(1)} collective-permute-done((bf16[272,128]{1,0:T(8,128)(2,1)S(1)}, bf16[272,128]{1,0:T(8,128)(2,1)S(1)}, u32[]{:S(2)}, u32[]{:S(2)}) %collective-permute-start.6) | collective-permute-done | bytes 69664 | tf_op jit(solution)/shard_map/ppermute | solution.py:583
  20.8 4.1 %collective-permute-done.7.refs_6_ = bf16[272,128]{1,0:T(8,128)(2,1)S(1)} collective-permute-done((bf16[272,128]{1,0:T(8,128)(2,1)S(1)}, bf16[272,128]{1,0:T(8,128)(2,1)S(1)}, u32[]{:S(2)}, u32[]{:S(2)}) %collective-permute-start.7) | collective-permute-done | bytes 69664 | tf_op jit(solution)/shard_map/ppermute | solution.py:583
  29.3 2.1 %collective-permute-done.1.refs_7_ = s32[2]{0:T(128)S(1)} collective-permute-done((s32[2]{0:T(128)S(1)}, s32[2]{0:T(128)S(1)}, u32[]{:S(2)}, u32[]{:S(2)}) %collective-permute-start.1) | collective-permute-done | bytes 40 | tf_op jit(solution)/shard_map/ppermute | solution.py:579
  33.4 4.2 %inner.1 = (f32[256,1024]{1,0:T(8,128)S(1)}, bf16[256,1024]{1,0:T(8,128)(2,1)S(1)}, s32[4,9]{1,0:T(4,128)S(1)}, s32[4]{0:T(128)S(1)}, s32[12]{0:T(128)S(1)}, /*i...) custom-call(bf16[256,1024]{1,0:T(8,128)(2,1)S(1)} %copy-done, f32[8,256]{1,0:T(8,128)S(1)} %copy-done.8, ...), custom_call_target="tpu_custom_call" | custom-call | flops 268435456 | bytes 8388608 | tf_op jit(solution)/shard_map/inner/pallas_call | solution.py:260
  37.7 2.2 %hidden.1 = (bf16[256,1024]{1,0:T(8,128)(2,1)S(1)}, bf16[256,512]{1,0:T(8,128)(2,1)S(1)}, bf16[128,1024]{1,0:T(8,128)(2,1)S(1)}, bf16[128,1024]{1,0:T(8,128)(2,1)S(1)}) custom-call(f32[256,1024]{1,0:T(8,128)S(1)} %get-tuple-element.38.refs_0_, bf16[256,1024]{1,0:T(8,128)(2,1)S(1)} %get-tuple-element.39.refs_1_, ...), custom_call_target="tpu_custom_call" | custom-call | tf_op jit(solution)/shard_map/hidden/pallas_call | solution.py:373
  39.9 1.3 %collective-permute-start.14 = (bf16[128,1024]{1,0:T(8,128)(2,1)S(1)}, bf16[128,1024]{1,0:T(8,128)(2,1)S(1)}, u32[]{:S(2)}, u32[]{:S(2)}) collective-permute-start(bf16[128,1024]{1,0:T(8,128)(2,1)S(1)} %get-tuple-element.52.refs_5_), channel_id=1, source_target_pairs={{0,4},{1,5},{2,6},{3,7},{4,8},{5,9},{6,10},{7,11},{8,12},{9,13},{1... | collective-permute-start | bytes 786440 | tf_op jit(solution)/shard_map/ppermute | solution.py:583
  43.2 5.1 %collective-permute-done.14.refs_9_ = bf16[128,1024]{1,0:T(8,128)(2,1)S(1)} collective-permute-done((bf16[128,1024]{1,0:T(8,128)(2,1)S(1)}, bf16[128,1024]{1,0:T(8,128)(2,1)S(1)}, u32[]{:S(2)}, u32[]{:S(2)}) %collective-permute-start.14) | collective-permute-done | bytes 262176 | tf_op jit(solution)/shard_map/ppermute | solution.py:583
  49.6 4.3 %collective-permute-done.15.refs_10_ = bf16[128,1024]{1,0:T(8,128)(2,1)S(1)} collective-permute-done((bf16[128,1024]{1,0:T(8,128)(2,1)S(1)}, bf16[128,1024]{1,0:T(8,128)(2,1)S(1)}, u32[]{:S(2)}, u32[]{:S(2)}) %collective-permute-start.15) | collective-permute-done | bytes 262176 | tf_op jit(solution)/shard_map/ppermute | solution.py:583
  55.2 4.0 %collective-permute-start.12 = (bf16[128,1024]{1,0:T(8,128)(2,1)S(1)}, bf16[128,1024]{1,0:T(8,128)(2,1)S(1)}, u32[]{:S(2)}, u32[]{:S(2)}) collective-permute-start(bf16[128,1024]{1,0:T(8,128)(2,1)S(1)} %get-tuple-element.52.refs_5_), channel_id=1, source_target_pairs={{0,1},{1,0},{2,3},{3,2},{4,5},{5,4},{6,7},{7,6},{8,9},{9,8},{10,11... | collective-permute-start | bytes 786440 | tf_op jit(solution)/shard_map/ppermute | solution.py:579
  61.1 4.1 %collective-permute-done.19.refs_14_ = bf16[128,1024]{1,0:T(8,128)(2,1)S(1)} collective-permute-done((bf16[128,1024]{1,0:T(8,128)(2,1)S(1)}, bf16[128,1024]{1,0:T(8,128)(2,1)S(1)}, u32[]{:S(2)}, u32[]{:S(2)}) %collective-permute-start.19) | collective-permute-done | bytes 262176 | tf_op jit(solution)/shard_map/ppermute | solution.py:583
  66.5 3.9 %collective-permute-start.17 = (bf16[128,1024]{1,0:T(8,128)(2,1)S(1)}, bf16[128,1024]{1,0:T(8,128)(2,1)S(1)}, u32[]{:S(2)}, u32[]{:S(2)}) collective-permute-start(bf16[128,1024]{1,0:T(8,128)(2,1)S(1)} %collective-permute-done.15.refs_10_), channel_id=1, source_target_pairs={{0,1},{1,0},{2,3},{3,2},{4,5},{5,4},{6,7},{7,6},{8,9},{9,8},{10,11... | collective-permute-start | bytes 786440 | tf_op jit(solution)/shard_map/ppermute | solution.py:579
  70.9 3.7 %collective-permute-start.24 = (bf16[128,1024]{1,0:T(8,128)(2,1)S(1)}, bf16[128,1024]{1,0:T(8,128)(2,1)S(1)}, u32[]{:S(2)}, u32[]{:S(2)}) collective-permute-start(bf16[128,1024]{1,0:T(8,128)(2,1)S(1)} %collective-permute-done.22.refs_7_), channel_id=1, source_target_pairs={{0,1},{1,0},{2,3},{3,2},{4,5},{5,4},{6,7},{7,6},{8,9},{9,8},{10,11... | collective-permute-start | bytes 786440 | tf_op jit(solution)/shard_map/ppermute | solution.py:579
  74.7 1.9 %collective-permute-done.23.refs_8_ = bf16[128,1024]{1,0:T(8,128)(2,1)S(1)} collective-permute-done((bf16[128,1024]{1,0:T(8,128)(2,1)S(1)}, bf16[128,1024]{1,0:T(8,128)(2,1)S(1)}, u32[]{:S(2)}, u32[]{:S(2)}) %collective-permute-start.23) | collective-permute-done | bytes 262176 | tf_op jit(solution)/shard_map/ppermute | solution.py:583
  76.5 2.1 %collective-permute-start.25 = (bf16[128,1024]{1,0:T(8,128)(2,1)S(1)}, bf16[128,1024]{1,0:T(8,128)(2,1)S(1)}, u32[]{:S(2)}, u32[]{:S(2)}) collective-permute-start(bf16[128,1024]{1,0:T(8,128)(2,1)S(1)} %collective-permute-done.23.refs_8_), channel_id=1, source_target_pairs={{0,1},{1,0},{2,3},{3,2},{4,5},{5,4},{6,7},{7,6},{8,9},{9,8},{10,11... | collective-permute-start | bytes 786440 | tf_op jit(solution)/shard_map/ppermute | solution.py:579
  78.6 5.9 %attend.1 = (f32[512,512]{1,0:T(8,128)S(1)}, f32[512,128]{1,0:T(8,128)S(1)}) custom-call(s32[4,9]{1,0:T(4,128)S(1)} %get-tuple-element.49.refs_0_, s32[4]{0:T(128)S(1)} %get-tuple-element.50.refs_1_, s32[12]{0:T(128)S(1)} %get-tuple-element.51.refs_2_, bf16[256,512]{1,0:T(8,128)(2,1)S(1)} %get-tuple-element.48.refs_3_, ...), custom_call_target="tpu_custom_call" | custom-call | flops 536870912 | bytes 3145728 | tf_op jit(solution)/shard_map/attend/pallas_call | solution.py:523
  84.6 6.0 %attend_last.1 = (f32[256,512]{1,0:T(8,128)S(1)}, bf16[256,512]{1,0:T(8,128)(2,1)S(1)}, f32[8,256]{1,0:T(8,128)S(1)}, f32[8,256]{1,0:T(8,128)S(1)}) custom-call(s32[4,9]{1,0:T(4,128)S(1)} %get-tuple-element.35.refs_0_, s32[4]{0:T(128)S(1)} %get-tuple-element.36.refs_1_, s32[4]{0:T(128)S(1)} %get-tuple-element.37.refs_2_, ...), custom_call_target="tpu_custom_call" | custom-call | flops 536870912 | bytes 1048576 | tf_op jit(solution)/shard_map/attend_last/pallas_call | solution.py:523
  92.1 6.9 %collective-permute-done.27.plse_ref = f32[8,256]{1,0:T(8,128)S(1)} collective-permute-done((f32[8,256]{1,0:T(8,128)S(1)}, f32[8,256]{1,0:T(8,128)S(1)}, u32[]{:S(2)}, u32[]{:S(2)}) %collective-permute-start.27) | collective-permute-done | bytes 8224 | tf_op jit(solution)/shard_map/ppermute | solution.py:579
  99.0 1.7 %output.1 = bf16[256,1024]{1,0:T(8,128)(2,1)} custom-call(f32[256,512]{1,0:T(8,128)S(1)} %get-tuple-element.56.o_ref, f32[8,256]{1,0:T(8,128)S(1)} %get-tuple-element.57.lse_ref, bf16[256,512]{1,0:T(8,128)(2,1)S(1)} %collective-permute-done.26.po_ref, f32[8,256]{1,0:T(8,128)S(1)} %collective-permute-done.27.plse_ref, ...), custom_call_target="tpu_custom_call" | custom-call | tf_op jit(solution)/shard_map/output/pallas_call | solution.py:561
  (64 shorter events, 20.7 us)
Async XLA Ops:
  8.2 4.4 %collective-permute-start.4 = (bf16[272,128]{1,0:T(8,128)(2,1)}, bf16[272,128]{1,0:T(8,128)(2,1)S(1)}, u32[]{:S(2)}, u32[]{:S(2)}) collective-permute-start(bf16[272,128]{1,0:T(8,128)(2,1)} %get-tuple-element.43), channel_id=1, source_target_pairs={{0,3},{1,2},{2,1},{3,0},{4,7},{5,6},{6,5},{7,4},{8,11},{9,10},{10,... | collective-permute-start | bytes 208904 | tf_op jit(solution)/shard_map/ppermute | solution.py:579
  13.5 5.1 %collective-permute-start.5 = (bf16[272,128]{1,0:T(8,128)(2,1)S(1)}, bf16[272,128]{1,0:T(8,128)(2,1)S(1)}, u32[]{:S(2)}, u32[]{:S(2)}) collective-permute-start(bf16[272,128]{1,0:T(8,128)(2,1)S(1)} %plane.1), channel_id=1, source_target_pairs={{0,4},{1,5},{2,6},{3,7},{4,8},{5,9},{6,10},{7,11},{8,12},{9,13},{1... | collective-permute-start | bytes 208904 | tf_op jit(solution)/shard_map/ppermute | solution.py:583
  14.8 6.0 %collective-permute-start.6 = (bf16[272,128]{1,0:T(8,128)(2,1)S(1)}, bf16[272,128]{1,0:T(8,128)(2,1)S(1)}, u32[]{:S(2)}, u32[]{:S(2)}) collective-permute-start(bf16[272,128]{1,0:T(8,128)(2,1)S(1)} %plane.1), channel_id=1, source_target_pairs={{0,8},{1,9},{2,10},{3,11},{4,12},{5,13},{6,14},{7,15},{16,24},{17,... | collective-permute-start | bytes 208904 | tf_op jit(solution)/shard_map/ppermute | solution.py:583
  16.1 8.8 %collective-permute-start.7 = (bf16[272,128]{1,0:T(8,128)(2,1)S(1)}, bf16[272,128]{1,0:T(8,128)(2,1)S(1)}, u32[]{:S(2)}, u32[]{:S(2)}) collective-permute-start(bf16[272,128]{1,0:T(8,128)(2,1)S(1)} %plane.1), channel_id=1, source_target_pairs={{0,12},{1,13},{2,14},{3,15},{16,28},{17,29},{18,30},{19,31}} | collective-permute-start | bytes 208904 | tf_op jit(solution)/shard_map/ppermute | solution.py:583
  25.0 12.6 %collective-permute-start.8 = (bf16[256,128]{1,0:T(8,128)(2,1)S(1)}, bf16[256,128]{1,0:T(8,128)(2,1)S(1)}, u32[]{:S(2)}, u32[]{:S(2)}) collective-permute-start(bf16[256,128]{1,0:T(8,128)(2,1)S(1)} %get-tuple-element.45), channel_id=1, source_target_pairs={{0,1},{1,0},{2,3},{3,2},{4,5},{5,4},{6,7},{7,6},{8,9},{9,8},{10,11... | collective-permute-start | bytes 196616 | tf_op jit(solution)/shard_map/ppermute | solution.py:579
  26.1 11.6 %collective-permute-start.9 = (bf16[256,128]{1,0:T(8,128)(2,1)S(1)}, bf16[256,128]{1,0:T(8,128)(2,1)S(1)}, u32[]{:S(2)}, u32[]{:S(2)}) collective-permute-start(bf16[256,128]{1,0:T(8,128)(2,1)S(1)} %get-tuple-element.46), channel_id=1, source_target_pairs={{0,2},{1,3},{2,0},{3,1},{4,6},{5,7},{6,4},{7,5},{8,10},{9,11},{10,... | collective-permute-start | bytes 196616 | tf_op jit(solution)/shard_map/ppermute | solution.py:579
  27.1 10.5 %collective-permute-start.10 = (bf16[256,128]{1,0:T(8,128)(2,1)S(1)}, bf16[256,128]{1,0:T(8,128)(2,1)S(1)}, u32[]{:S(2)}, u32[]{:S(2)}) collective-permute-start(bf16[256,128]{1,0:T(8,128)(2,1)S(1)} %get-tuple-element.47), channel_id=1, source_target_pairs={{0,3},{1,2},{2,1},{3,0},{4,7},{5,6},{6,5},{7,4},{8,11},{9,10},{10,... | collective-permute-start | bytes 196616 | tf_op jit(solution)/shard_map/ppermute | solution.py:579
  39.9 8.4 %collective-permute-start.14 = (bf16[128,1024]{1,0:T(8,128)(2,1)S(1)}, bf16[128,1024]{1,0:T(8,128)(2,1)S(1)}, u32[]{:S(2)}, u32[]{:S(2)}) collective-permute-start(bf16[128,1024]{1,0:T(8,128)(2,1)S(1)} %get-tuple-element.52.refs_5_), channel_id=1, source_target_pairs={{0,4},{1,5},{2,6},{3,7},{4,8},{5,9},{6,10},{7,11},{8,12},{9,13},{1... | collective-permute-start | bytes 786440 | tf_op jit(solution)/shard_map/ppermute | solution.py:583
  41.2 12.7 %collective-permute-start.15 = (bf16[128,1024]{1,0:T(8,128)(2,1)S(1)}, bf16[128,1024]{1,0:T(8,128)(2,1)S(1)}, u32[]{:S(2)}, u32[]{:S(2)}) collective-permute-start(bf16[128,1024]{1,0:T(8,128)(2,1)S(1)} %get-tuple-element.53.refs_6_), channel_id=1, source_target_pairs={{0,4},{1,5},{2,6},{3,7},{4,8},{5,9},{6,10},{7,11},{8,12},{9,13},{1... | collective-permute-start | bytes 786440 | tf_op jit(solution)/shard_map/ppermute | solution.py:583
  42.5 16.9 %collective-permute-start.11 = (bf16[256,512]{1,0:T(8,128)(2,1)S(1)}, bf16[256,512]{1,0:T(8,128)(2,1)S(1)}, u32[]{:S(2)}, u32[]{:S(2)}) collective-permute-start(bf16[256,512]{1,0:T(8,128)(2,1)S(1)} %get-tuple-element.48.refs_3_), channel_id=1, source_target_pairs={{0,2},{1,3},{2,0},{3,1},{4,6},{5,7},{6,4},{7,5},{8,10},{9,11},{10,... | collective-permute-start | bytes 786440 | tf_op jit(solution)/shard_map/ppermute | solution.py:579
  48.3 11.5 %collective-permute-start.18 = (bf16[128,1024]{1,0:T(8,128)(2,1)S(1)}, bf16[128,1024]{1,0:T(8,128)(2,1)S(1)}, u32[]{:S(2)}, u32[]{:S(2)}) collective-permute-start(bf16[128,1024]{1,0:T(8,128)(2,1)S(1)} %collective-permute-done.14.refs_9_), channel_id=1, source_target_pairs={{0,4},{1,5},{2,6},{3,7},{4,8},{5,9},{6,10},{7,11},{8,12},{9,13},{1... | collective-permute-start | bytes 786440 | tf_op jit(solution)/shard_map/ppermute | solution.py:583
  53.9 11.2 %collective-permute-start.19 = (bf16[128,1024]{1,0:T(8,128)(2,1)S(1)}, bf16[128,1024]{1,0:T(8,128)(2,1)S(1)}, u32[]{:S(2)}, u32[]{:S(2)}) collective-permute-start(bf16[128,1024]{1,0:T(8,128)(2,1)S(1)} %collective-permute-done.15.refs_10_), channel_id=1, source_target_pairs={{0,4},{1,5},{2,6},{3,7},{4,8},{5,9},{6,10},{7,11},{8,12},{9,13},{1... | collective-permute-start | bytes 786440 | tf_op jit(solution)/shard_map/ppermute | solution.py:583
  55.2 11.2 %collective-permute-start.12 = (bf16[128,1024]{1,0:T(8,128)(2,1)S(1)}, bf16[128,1024]{1,0:T(8,128)(2,1)S(1)}, u32[]{:S(2)}, u32[]{:S(2)}) collective-permute-start(bf16[128,1024]{1,0:T(8,128)(2,1)S(1)} %get-tuple-element.52.refs_5_), channel_id=1, source_target_pairs={{0,1},{1,0},{2,3},{3,2},{4,5},{5,4},{6,7},{7,6},{8,9},{9,8},{10,11... | collective-permute-start | bytes 786440 | tf_op jit(solution)/shard_map/ppermute | solution.py:579
  59.3 11.1 %collective-permute-start.13 = (bf16[128,1024]{1,0:T(8,128)(2,1)S(1)}, bf16[128,1024]{1,0:T(8,128)(2,1)S(1)}, u32[]{:S(2)}, u32[]{:S(2)}) collective-permute-start(bf16[128,1024]{1,0:T(8,128)(2,1)S(1)} %get-tuple-element.53.refs_6_), channel_id=1, source_target_pairs={{0,1},{1,0},{2,3},{3,2},{4,5},{5,4},{6,7},{7,6},{8,9},{9,8},{10,11... | collective-permute-start | bytes 786440 | tf_op jit(solution)/shard_map/ppermute | solution.py:579
  59.3 11.1 %collective-permute-start.16 = (bf16[128,1024]{1,0:T(8,128)(2,1)S(1)}, bf16[128,1024]{1,0:T(8,128)(2,1)S(1)}, u32[]{:S(2)}, u32[]{:S(2)}) collective-permute-start(bf16[128,1024]{1,0:T(8,128)(2,1)S(1)} %collective-permute-done.14.refs_9_), channel_id=1, source_target_pairs={{0,1},{1,0},{2,3},{3,2},{4,5},{5,4},{6,7},{7,6},{8,9},{9,8},{10,11... | collective-permute-start | bytes 786440 | tf_op jit(solution)/shard_map/ppermute | solution.py:579
  59.8 11.1 %collective-permute-start.22 = (bf16[128,1024]{1,0:T(8,128)(2,1)S(1)}, bf16[128,1024]{1,0:T(8,128)(2,1)S(1)}, u32[]{:S(2)}, u32[]{:S(2)}) collective-permute-start(bf16[128,1024]{1,0:T(8,128)(2,1)S(1)} %collective-permute-done.18.refs_13_), channel_id=1, source_target_pairs={{0,4},{1,5},{2,6},{3,7},{4,8},{5,9},{6,10},{7,11},{8,12},{9,13},{1... | collective-permute-start | bytes 786440 | tf_op jit(solution)/shard_map/ppermute | solution.py:583
  65.2 11.3 %collective-permute-start.23 = (bf16[128,1024]{1,0:T(8,128)(2,1)S(1)}, bf16[128,1024]{1,0:T(8,128)(2,1)S(1)}, u32[]{:S(2)}, u32[]{:S(2)}) collective-permute-start(bf16[128,1024]{1,0:T(8,128)(2,1)S(1)} %collective-permute-done.19.refs_14_), channel_id=1, source_target_pairs={{0,4},{1,5},{2,6},{3,7},{4,8},{5,9},{6,10},{7,11},{8,12},{9,13},{1... | collective-permute-start | bytes 786440 | tf_op jit(solution)/shard_map/ppermute | solution.py:583
  66.5 12.1 %collective-permute-start.17 = (bf16[128,1024]{1,0:T(8,128)(2,1)S(1)}, bf16[128,1024]{1,0:T(8,128)(2,1)S(1)}, u32[]{:S(2)}, u32[]{:S(2)}) collective-permute-start(bf16[128,1024]{1,0:T(8,128)(2,1)S(1)} %collective-permute-done.15.refs_10_), channel_id=1, source_target_pairs={{0,1},{1,0},{2,3},{3,2},{4,5},{5,4},{6,7},{7,6},{8,9},{9,8},{10,11... | collective-permute-start | bytes 786440 | tf_op jit(solution)/shard_map/ppermute | solution.py:579
  70.4 8.2 %collective-permute-start.20 = (bf16[128,1024]{1,0:T(8,128)(2,1)S(1)}, bf16[128,1024]{1,0:T(8,128)(2,1)S(1)}, u32[]{:S(2)}, u32[]{:S(2)}) collective-permute-start(bf16[128,1024]{1,0:T(8,128)(2,1)S(1)} %collective-permute-done.18.refs_13_), channel_id=1, source_target_pairs={{0,1},{1,0},{2,3},{3,2},{4,5},{5,4},{6,7},{7,6},{8,9},{9,8},{10,11... | collective-permute-start | bytes 786440 | tf_op jit(solution)/shard_map/ppermute | solution.py:579
  70.5 8.1 %collective-permute-start.21 = (bf16[128,1024]{1,0:T(8,128)(2,1)S(1)}, bf16[128,1024]{1,0:T(8,128)(2,1)S(1)}, u32[]{:S(2)}, u32[]{:S(2)}) collective-permute-start(bf16[128,1024]{1,0:T(8,128)(2,1)S(1)} %collective-permute-done.19.refs_14_), channel_id=1, source_target_pairs={{0,1},{1,0},{2,3},{3,2},{4,5},{5,4},{6,7},{7,6},{8,9},{9,8},{10,11... | collective-permute-start | bytes 786440 | tf_op jit(solution)/shard_map/ppermute | solution.py:579
  70.9 13.6 %collective-permute-start.24 = (bf16[128,1024]{1,0:T(8,128)(2,1)S(1)}, bf16[128,1024]{1,0:T(8,128)(2,1)S(1)}, u32[]{:S(2)}, u32[]{:S(2)}) collective-permute-start(bf16[128,1024]{1,0:T(8,128)(2,1)S(1)} %collective-permute-done.22.refs_7_), channel_id=1, source_target_pairs={{0,1},{1,0},{2,3},{3,2},{4,5},{5,4},{6,7},{7,6},{8,9},{9,8},{10,11... | collective-permute-start | bytes 786440 | tf_op jit(solution)/shard_map/ppermute | solution.py:579
  76.5 8.1 %collective-permute-start.25 = (bf16[128,1024]{1,0:T(8,128)(2,1)S(1)}, bf16[128,1024]{1,0:T(8,128)(2,1)S(1)}, u32[]{:S(2)}, u32[]{:S(2)}) collective-permute-start(bf16[128,1024]{1,0:T(8,128)(2,1)S(1)} %collective-permute-done.23.refs_8_), channel_id=1, source_target_pairs={{0,1},{1,0},{2,3},{3,2},{4,5},{5,4},{6,7},{7,6},{8,9},{9,8},{10,11... | collective-permute-start | bytes 786440 | tf_op jit(solution)/shard_map/ppermute | solution.py:579
  90.6 8.4 %collective-permute-start.26 = (bf16[256,512]{1,0:T(8,128)(2,1)S(1)}, bf16[256,512]{1,0:T(8,128)(2,1)S(1)}, u32[]{:S(2)}, u32[]{:S(2)}) collective-permute-start(bf16[256,512]{1,0:T(8,128)(2,1)S(1)} %get-tuple-element.58), channel_id=1, source_target_pairs={{0,2},{1,3},{2,0},{3,1},{4,6},{5,7},{6,4},{7,5},{8,10},{9,11},{10,... | collective-permute-start | bytes 786440 | tf_op jit(solution)/shard_map/ppermute | solution.py:579
  91.0 8.0 %collective-permute-start.27 = (f32[8,256]{1,0:T(8,128)S(1)}, f32[8,256]{1,0:T(8,128)S(1)}, u32[]{:S(2)}, u32[]{:S(2)}) collective-permute-start(f32[8,256]{1,0:T(8,128)S(1)} %get-tuple-element.59), channel_id=1, source_target_pairs={{0,2},{1,3},{2,0},{3,1},{4,6},{5,7},{6,4},{7,5},{8,10},{9,11},{10,... | collective-permute-start | bytes 24584 | tf_op jit(solution)/shard_map/ppermute | solution.py:579
  (16 other events, 281.1 us)
where the time goes:
time: 101 us
  waiting for transfers between devices  35.8 us (35%)
  starting transfers between devices  35.3 us (35%)
  Pallas kernels  26.4 us (26%)
  local copies, waits for them, and re-layouts  2.91 us (3%)
    ppermute x19, starting transfers between devices, flip(): return lax.ppermute(x, 'tm', [(i, i ^ bits) for i in range(size)])  23.7 us
    ppermute x9, waiting for transfers between devices, up(): return lax.ppermute(x, 'tm', [(i, i + step) for i in range(size - step)])  22.8 us
    ppermute x19, waiting for transfers between devices, flip(): return lax.ppermute(x, 'tm', [(i, i ^ bits) for i in range(size)])  12.9 us
    pallas_call x2, Pallas kernels, attend(): pl.pallas_call(functools.partial(attend_kernel, frames, blocks, first, la...  11.9 us
    ppermute x9, starting transfers between devices, up(): return lax.ppermute(x, 'tm', [(i, i + step) for i in range(size - step)])  11.6 us
    pallas_call x1, Pallas kernels, local(): pl.pallas_call(local_kernel, in_specs=[HBM] * 4, out_specs=[VMEM] * (2 +...  6.11 us
    pallas_call x1, Pallas kernels, inner(): pl.pallas_call(functools.partial(inner_kernel, frames, distances), in_spe...  4.2 us
    unnamed x24, local copies, waits for them, and re-layouts  2.91 us
  transfers between devices with their start and end apart: 28, of which 11 were waited for; matrix products, arithmetic and copies ran while one was open for 0% of the time, Pallas kernels for 10%

commit v1 on v0

--- a/solution.py
+++ b/solution.py
@@ -91,83 +91,99 @@
     ).astype(BF16)
 
 
-def local_kernel(x_in, ld_in, wk_ref, wv_ref, k_ref, v_ref, *rest):
-    outs, (chunks, x_ref, ld_ref, bk, bv, sems, own) = rest[:LANES], rest[LANES:]
+def decay_terms(ld):
+    return jnp.concatenate([t.astype(F32) for t in split3(ld)], axis=0).astype(BF16)
+
+
+def column_sums(mask, ld):
+    x = nt(mask.astype(BF16), decay_terms(ld))
+    return x[:, :H] + x[:, H : 2 * H] + x[:, 2 * H : 3 * H]
+
+
+def row_sums(mask, ld):
+    x = nt(decay_terms(ld), mask.astype(BF16))
+    return x[:H] + x[H : 2 * H] + x[2 * H : 3 * H]
+
+
+def position():
+    lane = lax.rem(lax.axis_index("tm"), LANES)
+    return lane // 2, lane & 1
+
+
+def local_kernel(x_in, ld_in, wk_in, wv_in, idx, cnt, k_ref, v_ref, keep, give, pack, *rest):
+    chunks, x_ref, ld_ref, bk, bv, sems = rest
     rows = x_ref.shape[0]
-    first = [
-        pltpu.make_async_copy(ld_in, ld_ref, own.at[0]),
-        pltpu.make_async_copy(x_in, x_ref, own.at[1]),
+    copies = [
+        pltpu.make_async_copy(src, dst, sems.at[i])
+        for i, (src, dst) in enumerate(
+            ((ld_in, ld_ref), (x_in, x_ref), (wk_in, bk), (wv_in, bv))
+        )
     ]
-    for copy in first:
+    for copy in copies:
         copy.start()
-    copies = []
-    for q in range(LANES):
-        kc, vc = slice(q * HC * DK, (q + 1) * HC * DK), slice(q * HC * DV, (q + 1) * HC * DV)
-        copies.append(
-            (
-                pltpu.make_async_copy(wk_ref.at[:, kc], bk.at[:, kc], sems.at[0, q]),
-                pltpu.make_async_copy(wv_ref.at[:, vc], bv.at[:, vc], sems.at[1, q]),
-            )
-        )
-    for pair in copies:
-        for copy in pair:
-            copy.start()
-    first[0].wait()
-    ld = ld_ref[...]
+    frames, slots = idx.shape
+    for f in range(frames):
+        for i in range(slots):
+            pack[f, i] = idx[f, i]
+        pack[f, slots] = cnt[f]
     t = lax.broadcasted_iota(jnp.int32, (rows, rows), 0)
     s = lax.broadcasted_iota(jnp.int32, (rows, rows), 1)
     after = ((s > t) & (chain_of(s) == chain_of(t))).astype(F32)
-    tail = jnp.exp(nt(after, ld, precision=lax.Precision.HIGHEST))
+    copies[0].wait()
+    ld = ld_ref[...]
+    tail = jnp.exp(column_sums(after, ld))
     chain = chain_of(lax.broadcasted_iota(jnp.int32, ld.shape, 1))
     sums = [jnp.sum(jnp.where(chain == b, ld, 0.0), axis=1, keepdims=True) for b in (0, 1)]
-    first[1].wait()
+    for copy in copies[1:]:
+        copy.wait()
     x = x_ref[...]
+    k = nn(x, bk[...]).astype(BF16)
+    k_ref[...] = k
     for q in range(LANES):
-        for copy in copies[q]:
-            copy.wait()
-        kc, vc = slice(q * HC * DK, (q + 1) * HC * DK), slice(q * HC * DV, (q + 1) * HC * DV)
-        k = nn(x, bk[:, kc]).astype(BF16)
+        vc = slice(q * HC * DV, (q + 1) * HC * DV)
         v = nn(x, bv[:, vc]).astype(BF16)
-        k_ref[:, kc] = k
         v_ref[:, vc] = v
         states, totals = [], []
         for i in range(HC):
             h = q * HC + i
-            kt = (k[:, i * DK : (i + 1) * DK].astype(F32) * tail[:, h : h + 1]).astype(BF16)
+            kt = (k[:, h * DK : (h + 1) * DK].astype(F32) * tail[:, h : h + 1]).astype(BF16)
             states.append(tn(by_chain(kt), v[:, i * DV : (i + 1) * DV]))
             totals += [jnp.broadcast_to(sums[b][h : h + 1], (1, DV)) for b in (0, 1)]
         write_message(
             chunks.at[q], jnp.concatenate(states, axis=0), jnp.concatenate(totals, axis=0)
         )
-    lane = lax.rem(lax.axis_index("tm"), LANES)
-    for f in range(LANES):
-        outs[f][...] = chunks[lane ^ f]
-
-
-def local(tokens, w_rk, w_rv, ld):
+    _, core = position()
+    for y in range(2):
+        keep[y] = chunks[2 * y + core]
+        give[y] = chunks[2 * y + 1 - core]
+
+
+def local(tokens, w_rk, w_rv, ld, index, live):
     rows, d = tokens.shape
-    message = jax.ShapeDtypeStruct((ROWS + TAIL, DV), BF16)
+    message = jax.ShapeDtypeStruct((2, ROWS + TAIL, DV), BF16)
+    frames, slots = index.shape
     return pl.pallas_call(
         local_kernel,
-        in_specs=[HBM] * 4,
-        out_specs=[VMEM] * (2 + LANES),
+        in_specs=[HBM] * 4 + [SMEM] * 2,
+        out_specs=[VMEM] * 4 + [SMEM],
         out_shape=[
             jax.ShapeDtypeStruct((rows, H * DK), BF16),
             jax.ShapeDtypeStruct((rows, H * DV), BF16),
-        ]
-        + [message] * LANES,
+            message,
+            message,
+            jax.ShapeDtypeStruct((frames, slots + 1), jnp.int32),
+        ],
         scratch_shapes=[
             pltpu.VMEM((LANES, ROWS + TAIL, DV), BF16),
             pltpu.VMEM((rows, d), BF16),
             pltpu.VMEM((H, rows), F32),
             pltpu.VMEM((d, H * DK), BF16),
             pltpu.VMEM((d, H * DV), BF16),
-            pltpu.SemaphoreType.DMA((2, LANES)),
-            pltpu.SemaphoreType.DMA((2,)),
+            pltpu.SemaphoreType.DMA((4,)),
         ],
         compiler_params=params(62),
         name="local",
-    )(tokens, ld, w_rk, w_rv)
+    )(tokens, ld, w_rk, w_rv, index, live)
 
 
 def list_live(frames, distances, tables, groups):
@@ -188,8 +204,8 @@
                 counts[g * frames + f] = jnp.int32(1 if part == 0 and g == 0 else 0)
                 if part == 0 and g == 0:
                     table[f, 0] = jnp.int32(f)
-    for g, (index, live) in enumerate(groups):
-        slots = index.shape[1]
+    for g, index in enumerate(groups):
+        slots = index.shape[1] - 1
         for f in range(frames):
             row = g * frames + f
 
@@ -213,26 +229,33 @@
 
                 return carry
 
-            lax.fori_loop(0, jnp.minimum(live[f], slots), visit, 0)
+            lax.fori_loop(0, jnp.minimum(index[f, slots], slots), visit, 0)
 
 
 def inner_kernel(frames, distances, *refs):
-    x_ref, ld_ref, k_ref, v_ref, idx, cnt, pidx, pcnt, wq_ref = refs[:9]
-    inner_ref, qq_ref = refs[9:11]
-    tables, (bq, sem) = refs[11:-2], refs[-2:]
-    copy = pltpu.make_async_copy(wq_ref, bq, sem)
-    copy.start()
-    list_live(frames, distances, tables, ((idx, cnt), (pidx, pcnt)))
-    rows = x_ref.shape[0]
+    x_in, ld_ref, k_in, v_in, pack, other, wq_in = refs[:7]
+    inner_ref, qq_ref = refs[7:9]
+    tables, (x_ref, k_ref, v_ref, bq, sems) = refs[9:-5], refs[-5:]
+    copies = [
+        pltpu.make_async_copy(src, dst, sems.at[i])
+        for i, (src, dst) in enumerate(
+            ((x_in, x_ref), (wq_in, bq), (k_in, k_ref), (v_in, v_ref))
+        )
+    ]
+    for copy in copies:
+        copy.start()
+    list_live(frames, distances, tables, (pack, other))
+    rows = x_in.shape[0]
     ld = ld_ref[...]
     t = lax.broadcasted_iota(jnp.int32, (rows, rows), 0)
     s = lax.broadcasted_iota(jnp.int32, (rows, rows), 1)
     upto = (s <= t) & (chain_of(s) == chain_of(t))
     ones = upto.astype(F32)
-    column = nt(ones, ld, precision=lax.Precision.HIGHEST)
-    row = nt(ld, ones, precision=lax.Precision.HIGHEST)
+    column = column_sums(ones, ld)
+    row = row_sums(ones, ld)
     grown = jnp.exp(column) * DK**-0.5
-    copy.wait()
+    for copy in copies:
+        copy.wait()
     q = nn(x_ref[...], bq[...]).astype(BF16)
     for h in range(H):
         qh = q[:, h * DK : (h + 1) * DK]
@@ -246,10 +269,10 @@
         qq_ref[:, h * 2 * DK : (h + 1) * 2 * DK] = by_chain(scaled.astype(BF16))
 
 
-def inner(tokens, w_rq, k, v, ld, index, live, pindex, plive, distances):
+def inner(tokens, w_rq, k, v, ld, pack, other, distances):
     rows, d = tokens.shape
     frames = rows // P_SIZE
-    slots = index.shape[1]
+    slots = pack.shape[1] - 1
     table_shapes = []
     for low, high in distances:
         table_shapes += [
@@ -259,97 +282,109 @@
         ]
     out = pl.pallas_call(
         functools.partial(inner_kernel, frames, distances),
-        in_specs=[VMEM] * 4 + [SMEM] * 4 + [HBM],
+        in_specs=[HBM, VMEM, HBM, HBM, SMEM, SMEM, HBM],
         out_specs=[VMEM] * 2 + [SMEM] * len(table_shapes),
         out_shape=[
             jax.ShapeDtypeStruct((rows, H * DV), F32),
             jax.ShapeDtypeStruct((rows, H * 2 * DK), BF16),
         ]
         + table_shapes,
-        scratch_shapes=[pltpu.VMEM((d, H * DK), BF16), pltpu.SemaphoreType.DMA(())],
-        compiler_params=params(),
+        scratch_shapes=[
+            pltpu.VMEM((rows, d), BF16),
+            pltpu.VMEM((rows, H * DK), BF16),
+            pltpu.VMEM((rows, H * DV), BF16),
+            pltpu.VMEM((d, H * DK), BF16),
+            pltpu.SemaphoreType.DMA((4,)),
+        ],
+        compiler_params=params(48),
         cost_estimate=cost(2 * rows * d * H * DK, 8 << 20),
         name="inner",
-    )(tokens, ld, k, v, index, live, pindex, plive, w_rq)
+    )(tokens, ld, k, v, pack, other, w_rq)
     return out[0], out[1], [out[2 + 3 * i : 5 + 3 * i] for i in range(len(distances))]
 
 
-def plane_kernel(*refs):
-    parts, out, ordered = refs[:LANES], refs[LANES], refs[LANES + 1]
-    lane = lax.rem(lax.axis_index("tm"), LANES)
-    for f in range(LANES):
-        ordered[lane ^ f] = parts[f][...]
-    state, total = read_message(ordered[0])
-    for i in range(1, LANES):
-        mine, decay = read_message(ordered[i])
-        state = spread(jnp.exp(decay)) * state + mine
-        total = total + decay
-    write_message(out, state, total)
-
-
-def plane_total(parts):
+def join(first, second):
+    return spread(jnp.exp(second[1])) * first[0] + second[0], first[1] + second[1]
+
+
+def chip_kernel(keep, got, stay, send, ordered, results):
+    y, core = position()
+    ordered[core] = keep[...]
+    ordered[1 - core] = got[...]
+    for q in range(2):
+        write_message(
+            results.at[q], *join(read_message(ordered[0, q]), read_message(ordered[1, q]))
+        )
+    stay[...] = results[y]
+    send[...] = results[1 - y]
+
+
+def plane_kernel(stay, got, out, ordered):
+    y, _ = position()
+    ordered[y] = stay[...]
+    ordered[1 - y] = got[...]
+    write_message(out, *join(read_message(ordered[0]), read_message(ordered[1])))
+
+
+def prefix_kernel(count, *refs):
+    (stay, got), earlier = refs[:2], refs[2 : 2 + count]
+    mine, send, ordered, results = refs[2 + count :]
+    y, _ = position()
+    plane = lax.axis_index("tm") // LANES
+    ordered[y] = stay[...]
+    ordered[1 - y] = got[...]
+    state = jnp.zeros((ROWS, DV), F32)
+    for distance in range(count, 0, -1):
+        step, _ = join((state, 0.0), read_message(earlier[distance - 1][...]))
+        state = jnp.where(plane >= distance, step, 0.0)
+    results[0] = state.astype(BF16)
+    results[1] = join((state, 0.0), read_message(ordered[0]))[0].astype(BF16)
+    mine[...] = results[y]
+    send[...] = results[1 - y]
+
+
+def split_kernel(keep, local_got, mine, got, kept, give, ordered, both, results):
+    y, core = position()
+    ordered[core] = keep[...]
+    ordered[1 - core] = local_got[...]
+    both[y] = mine[...]
+    both[1 - y] = got[...]
+    for q in range(2):
+        state = both[q]
+        results[0, q] = state
+        results[1, q] = join((state.astype(F32), 0.0), read_message(ordered[0, q]))[0].astype(BF16)
+    kept[...] = results[core]
+    give[...] = results[1 - core]
+
+
+def small(kernel, outs, scratch, *args):
     return pl.pallas_call(
-        plane_kernel,
-        in_specs=[VMEM] * LANES,
-        out_specs=VMEM,
-        out_shape=jax.ShapeDtypeStruct((ROWS + TAIL, DV), BF16),
-        scratch_shapes=[pltpu.VMEM((LANES, ROWS + TAIL, DV), BF16)],
-        compiler_params=params(),
-        name="plane",
-    )(*parts)
-
-
-def prefix_kernel(count, *refs):
-    parts, earlier = refs[:LANES], refs[LANES : LANES + count]
-    outs = refs[LANES + count : 2 * LANES + count]
-    ordered, results = refs[2 * LANES + count :]
-    lane = lax.rem(lax.axis_index("tm"), LANES)
-    for f in range(LANES):
-        ordered[lane ^ f] = parts[f][...]
-    state = jnp.zeros((ROWS, DV), F32)
-    for ref in reversed(earlier):
-        mine, decay = read_message(ref[...])
-        state = spread(jnp.exp(decay)) * state + mine
-    for i in range(LANES):
-        results[i] = state.astype(BF16)
-        if i + 1 < LANES:
-            mine, decay = read_message(ordered[i])
-            state = spread(jnp.exp(decay)) * state + mine
-    for f in range(LANES):
-        outs[f][...] = results[lane ^ f]
-
-
-def prefix(parts, earlier):
-    return pl.pallas_call(
-        functools.partial(prefix_kernel, len(earlier)),
-        in_specs=[VMEM] * (LANES + len(earlier)),
-        out_specs=[VMEM] * LANES,
-        out_shape=[jax.ShapeDtypeStruct((ROWS, DV), BF16)] * LANES,
-        scratch_shapes=[
-            pltpu.VMEM((LANES, ROWS + TAIL, DV), BF16),
-            pltpu.VMEM((LANES, ROWS, DV), BF16),
-        ],
-        compiler_params=params(),
-        name="prefix",
-    )(*parts, *earlier)
+        kernel,
+        in_specs=[VMEM] * len(args),
+        out_specs=[VMEM] * len(outs),
+        out_shape=[jax.ShapeDtypeStruct(shape, BF16) for shape in outs],
+        scratch_shapes=[pltpu.VMEM(shape, BF16) for shape in scratch],
+        compiler_params=params(8),
+    )(*args)
 
 
 def hidden_kernel(frames, *refs):
     inner_ref, qq_ref = refs[:2]
-    states = refs[2 : 2 + LANES]
-    x_ref, gain_ref, wq, wk, wv = refs[2 + LANES : 7 + LANES]
-    hid_ref, q_ref = refs[7 + LANES : 9 + LANES]
-    kv_refs = refs[9 + LANES : 9 + LANES + frames]
-    ordered, bq, bk, bv, sems = refs[9 + LANES + frames :]
+    kept, got = refs[2:4]
+    x_ref, gain_ref, wq, wk, wv = refs[4:9]
+    hid_ref, q_ref = refs[9:11]
+    kv_refs = refs[11 : 11 + frames]
+    ordered, bq, bk, bv, sems = refs[11 + frames :]
     copies = [
         pltpu.make_async_copy(src, dst, sems.at[i])
         for i, (src, dst) in enumerate(((wq, bq), (wk, bk), (wv, bv)))
     ]
     for copy in copies:
         copy.start()
-    lane = lax.rem(lax.axis_index("tm"), LANES)
-    for f in range(LANES):
-        ordered[lane ^ f] = states[f][...]
+    _, core = position()
+    for y in range(2):
+        ordered[2 * y + core] = kept[y]
+        ordered[2 * y + 1 - core] = got[y]
     for h in range(H):
         cols = slice(h * DV, (h + 1) * DV)
         state = ordered[h // HC, (h % HC) * 2 * DK : (h % HC + 1) * 2 * DK, :]
@@ -372,7 +407,7 @@
     frames = rows // P_SIZE
     return pl.pallas_call(
         functools.partial(hidden_kernel, frames),
-        in_specs=[VMEM] * (LANES + 4) + [HBM] * 3,
+        in_specs=[VMEM] * 6 + [HBM] * 3,
         out_specs=[VMEM] * (2 + frames),
         out_shape=[
             jax.ShapeDtypeStruct((rows, d), BF16),
@@ -580,19 +615,39 @@
 
     def up(x, distance):
         step = distance * LANES
-        return lax.ppermute(x, "tm", [(i, i + step) for i in range(size - step)])
-
+        return lax.ppermute(x, "tm", [(i, (i + step) % size) for i in range(size)])
+
+    message, chunk = (ROWS + TAIL, DV), (ROWS, DV)
     spans = ((0, planes - 1), (planes - 1, planes)) if planes > 1 else ((0, planes),)
-    partner_index, partner_count = flip(mem_index, 2), flip(mem_count, 2)
-    k, v, *chunks = local(tokens, w_rk, w_rv, log_decay)
-    parts = [chunks[0]] + [flip(chunks[f], f) for f in range(1, LANES)]
-    inner_out, qq, tables = inner(
-        tokens, w_rq, k, v, log_decay, mem_index, mem_count, partner_index, partner_count, spans
+    k, v, keep, give, pack = local(tokens, w_rk, w_rv, log_decay, mem_index, mem_count)
+    core_got = flip(give, 1)
+    other = flip(pack, 2)
+    stay, send = small(
+        chip_kernel, [message] * 2, [(2, 2) + message, (2,) + message], keep, core_got
     )
-    total = plane_total(parts)
-    earlier = [up(total, distance) for distance in range(1, planes)]
-    mine = prefix(parts, earlier)
-    states = [mine[0]] + [flip(mine[f], f) for f in range(1, LANES)]
+    column_got = flip(send, 2)
+    (total,) = small(plane_kernel, [message], [(2,) + message], stay, column_got)
+    earlier = [up(total, d) for d in range(1, planes)]
+    inner_out, qq, tables = inner(tokens, w_rq, k, v, log_decay, pack, other, spans)
+    mine, send = small(
+        functools.partial(prefix_kernel, len(earlier)),
+        [chunk] * 2,
+        [(2,) + message, (2,) + chunk],
+        stay,
+        column_got,
+        *earlier,
+    )
+    column_back = flip(send, 2)
+    kept, give = small(
+        split_kernel,
+        [(2,) + chunk] * 2,
+        [(2, 2) + message, (2,) + chunk, (2, 2) + chunk],
+        keep,
+        core_got,
+        mine,
+        column_back,
+    )
+    states = (kept, flip(give, 1))
     hid, q, *kv = hidden_of(inner_out, qq, states, tokens, norm_gain, w_mq, w_mk, w_mv)
     partner_q = flip(q, 2)
     held = []

time: 101 us -> 97.7 us (0.967)
  waiting for transfers between devices: 35.8 us -> 31.8 us
  local copies, waits for them, and re-layouts: 2.91 us -> 4.52 us
    ppermute x9, waiting for transfers between devices: 22.8 us -> 18.5 us  [up(): return lax.ppermute(x, 'tm', [(i, (i + step) % size) for i in range(size)])]
    unnamed x24, local copies, waits for them, and re-layouts: 2.91 us -> 4.52 us
    ppermute x9, starting transfers between devices: 11.6 us -> 10.1 us  [up(): return lax.ppermute(x, 'tm', [(i, (i + step) % size) for i in range(size)])]
    ppermute x19 -> x16, starting transfers between devices: 23.7 us -> 25.1 us  [flip(): return lax.ppermute(x, 'tm', [(i, i ^ bits) for i in range(size)])]
    ppermute x19 -> x16, waiting for transfers between devices: 12.9 us -> 13.3 us  [flip(): return lax.ppermute(x, 'tm', [(i, i ^ bits) for i in range(size)])]
    pallas_call x3 -> x5, Pallas kernels: 6.35 us -> 6.35 us  [the longest x1 5.97 us: local(): pl.pallas_call(local_kernel, in_specs=[HBM] * 4 + [SMEM] * 2, out_specs=[...]
  transfers between devices with their start and end apart: 28 -> 25, of which waited for: 11 -> 12; matrix products, arithmetic and copies ran while one was open for 0% -> 0% of each run, Pallas kernels for 10% -> 10%
where the time goes in v1:
time: 97.7 us; the launch traced here: 97.5 us
  starting transfers between devices  35.3 us (36%)
  waiting for transfers between devices  31.8 us (33%)
  Pallas kernels  25.7 us (26%)
  local copies, waits for them, and re-layouts  4.52 us (5%)
    ppermute x16, starting transfers between devices, flip(): return lax.ppermute(x, 'tm', [(i, i ^ bits) for i in range(size)])  25.1 us
    ppermute x9, waiting for transfers between devices, up(): return lax.ppermute(x, 'tm', [(i, (i + step) % size) for i in range(size)])  18.5 us
    ppermute x16, waiting for transfers between devices, flip(): return lax.ppermute(x, 'tm', [(i, i ^ bits) for i in range(size)])  13.3 us
    pallas_call x2, Pallas kernels, attend(): pl.pallas_call(functools.partial(attend_kernel, frames, blocks, first, la...  11.9 us
    ppermute x9, starting transfers between devices, up(): return lax.ppermute(x, 'tm', [(i, (i + step) % size) for i in range(size)])  10.1 us
    pallas_call x1, Pallas kernels, local(): pl.pallas_call(local_kernel, in_specs=[HBM] * 4 + [SMEM] * 2, out_specs=[...  5.97 us
    unnamed x24, local copies, waits for them, and re-layouts  4.52 us
    pallas_call x1, Pallas kernels, inner(): pl.pallas_call(functools.partial(inner_kernel, frames, distances), in_spe...  3.53 us
  transfers between devices with their start and end apart: 25, of which 12 were waited for; matrix products, arithmetic and copies ran while one was open for 0% of the time, Pallas kernels for 10%

profile of v1, /device:TPU:27, one launch (start us, length us, event | category | flops | bytes accessed | tf_op | source)
XLA Modules:
  0.0 97.5 jit_solution(9085358952502757351)
XLA Ops:
  0.0 6.0 %local.1 = (bf16[256,512]{1,0:T(8,128)(2,1)}, bf16[256,1024]{1,0:T(8,128)(2,1)}, bf16[2,272,128]{2,1,0:T(8,128)(2,1)}, bf16[2,272,128]{2,1,0:T(8,128)(2,1)}, s32[2,9]{1,0:T(2,128)}) custom-call(bf16[256,1024]{1,0:T(8,128)(2,1)} %refs_4_.1, f32[8,256]{1,0:T(8,128)} %refs_1_.1, bf16[1024,512]{1,0:T(8,128)(2,1)} %wk_in.1, bf16[1024,1024]{1,0:T(8,128)(2,1)} %wv_in.1, ...), custom_call_target="tpu_custom_call" | custom-call | tf_op jit(solution)/shard_map/local/pallas_call | solution.py:165
  10.3 1.9 %collective-permute-done.2.got.refs_1_ = bf16[272,128]{1,0:T(8,128)(2,1)S(1)} collective-permute-done((bf16[272,128]{1,0:T(8,128)(2,1)S(1)}, bf16[272,128]{1,0:T(8,128)(2,1)S(1)}, u32[]{:S(2)}, u32[]{:S(2)}) %collective-permute-start.2) | collective-permute-done | bytes 69664 | tf_op jit(solution)/shard_map/ppermute | solution.py:614
  13.8 1.6 %collective-permute-done.3.refs_2_ = bf16[272,128]{1,0:T(8,128)(2,1)S(1)} collective-permute-done((bf16[272,128]{1,0:T(8,128)(2,1)S(1)}, bf16[272,128]{1,0:T(8,128)(2,1)S(1)}, u32[]{:S(2)}, u32[]{:S(2)}) %collective-permute-start.3) | collective-permute-done | bytes 69664 | tf_op jit(solution)/shard_map/ppermute | solution.py:618
  16.4 2.4 %collective-permute-done.5.refs_4_ = bf16[272,128]{1,0:T(8,128)(2,1)S(1)} collective-permute-done((bf16[272,128]{1,0:T(8,128)(2,1)S(1)}, bf16[272,128]{1,0:T(8,128)(2,1)S(1)}, u32[]{:S(2)}, u32[]{:S(2)}) %collective-permute-start.5) | collective-permute-done | bytes 69664 | tf_op jit(solution)/shard_map/ppermute | solution.py:618
  20.2 1.9 %collective-permute-done.6.got = bf16[256,128]{1,0:T(8,128)(2,1)S(1)} collective-permute-done((bf16[256,128]{1,0:T(8,128)(2,1)S(1)}, bf16[256,128]{1,0:T(8,128)(2,1)S(1)}, u32[]{:S(2)}, u32[]{:S(2)}) %collective-permute-start.6) | collective-permute-done | bytes 65568 | tf_op jit(solution)/shard_map/ppermute | solution.py:614
  23.1 4.2 %collective-permute-start.7 = (bf16[2,256,128]{2,1,0:T(8,128)(2,1)S(1)}, bf16[2,256,128]{2,1,0:T(8,128)(2,1)S(1)}, u32[]{:S(2)}, u32[]{:S(2)}) collective-permute-start(bf16[2,256,128]{2,1,0:T(8,128)(2,1)S(1)} %get-tuple-element.49), channel_id=1, source_target_pairs={{0,1},{1,0},{2,3},{3,2},{4,5},{5,4},{6,7},{7,6},{8,9},{9,8},{10,11... | collective-permute-start | bytes 393224 | tf_op jit(solution)/shard_map/ppermute | solution.py:614
  28.6 1.4 %collective-permute-done.refs_5_ = s32[2,9]{1,0:T(2,128)S(1)} collective-permute-done((s32[2,9]{1,0:T(2,128)}, s32[2,9]{1,0:T(2,128)S(1)}, u32[]{:S(2)}, u32[]{:S(2)}) %collective-permute-start) | collective-permute-done | bytes 104 | tf_op jit(solution)/shard_map/ppermute | solution.py:614
  32.7 3.5 %inner.1 = (f32[256,1024]{1,0:T(8,128)S(1)}, bf16[256,1024]{1,0:T(8,128)(2,1)S(1)}, s32[4,9]{1,0:T(4,128)S(1)}, s32[4]{0:T(128)S(1)}, s32[12]{0:T(128)S(1)}, /*i...) custom-call(bf16[256,1024]{1,0:T(8,128)(2,1)S(1)} %copy-done, f32[8,256]{1,0:T(8,128)S(1)} %copy-done.9, ...), custom_call_target="tpu_custom_call" | custom-call | flops 268435456 | bytes 8388608 | tf_op jit(solution)/shard_map/inner/pallas_call | solution.py:283
  36.3 2.2 %hidden.1 = (bf16[256,1024]{1,0:T(8,128)(2,1)S(1)}, bf16[256,512]{1,0:T(8,128)(2,1)S(1)}, bf16[128,1024]{1,0:T(8,128)(2,1)S(1)}, bf16[128,1024]{1,0:T(8,128)(2,1)S(1)}) custom-call(f32[256,1024]{1,0:T(8,128)S(1)} %get-tuple-element.40.refs_0_, bf16[256,1024]{1,0:T(8,128)(2,1)S(1)} %get-tuple-element.41.refs_1_, ...), custom_call_target="tpu_custom_call" | custom-call | tf_op jit(solution)/shard_map/hidden/pallas_call | solution.py:408
  41.2 4.1 %collective-permute-done.11.refs_9_ = bf16[128,1024]{1,0:T(8,128)(2,1)S(1)} collective-permute-done((bf16[128,1024]{1,0:T(8,128)(2,1)S(1)}, bf16[128,1024]{1,0:T(8,128)(2,1)S(1)}, u32[]{:S(2)}, u32[]{:S(2)}) %collective-permute-start.11) | collective-permute-done | bytes 262176 | tf_op jit(solution)/shard_map/ppermute | solution.py:618
  45.3 1.9 %collective-permute-start.15 = (bf16[128,1024]{1,0:T(8,128)(2,1)S(1)}, bf16[128,1024]{1,0:T(8,128)(2,1)S(1)}, u32[]{:S(2)}, u32[]{:S(2)}) collective-permute-start(bf16[128,1024]{1,0:T(8,128)(2,1)S(1)} %collective-permute-done.11.refs_9_), channel_id=1, source_target_pairs={{0,4},{1,5},{2,6},{3,7},{4,8},{5,9},{6,10},{7,11},{8,12},{9,13},{1... | collective-permute-start | bytes 786440 | tf_op jit(solution)/shard_map/ppermute | solution.py:618
  47.2 3.7 %collective-permute-done.12.refs_10_ = bf16[128,1024]{1,0:T(8,128)(2,1)S(1)} collective-permute-done((bf16[128,1024]{1,0:T(8,128)(2,1)S(1)}, bf16[128,1024]{1,0:T(8,128)(2,1)S(1)}, u32[]{:S(2)}, u32[]{:S(2)}) %collective-permute-start.12) | collective-permute-done | bytes 262176 | tf_op jit(solution)/shard_map/ppermute | solution.py:618
  50.9 1.9 %collective-permute-start.16 = (bf16[128,1024]{1,0:T(8,128)(2,1)S(1)}, bf16[128,1024]{1,0:T(8,128)(2,1)S(1)}, u32[]{:S(2)}, u32[]{:S(2)}) collective-permute-start(bf16[128,1024]{1,0:T(8,128)(2,1)S(1)} %collective-permute-done.12.refs_10_), channel_id=1, source_target_pairs={{0,4},{1,5},{2,6},{3,7},{4,8},{5,9},{6,10},{7,11},{8,12},{9,13},{1... | collective-permute-start | bytes 786440 | tf_op jit(solution)/shard_map/ppermute | solution.py:618
  52.8 3.8 %collective-permute-start.9 = (bf16[128,1024]{1,0:T(8,128)(2,1)S(1)}, bf16[128,1024]{1,0:T(8,128)(2,1)S(1)}, u32[]{:S(2)}, u32[]{:S(2)}) collective-permute-start(bf16[128,1024]{1,0:T(8,128)(2,1)S(1)} %get-tuple-element.54.refs_5_), channel_id=1, source_target_pairs={{0,1},{1,0},{2,3},{3,2},{4,5},{5,4},{6,7},{7,6},{8,9},{9,8},{10,11... | collective-permute-start | bytes 786440 | tf_op jit(solution)/shard_map/ppermute | solution.py:614
  58.4 3.7 %collective-permute-done.16.refs_14_ = bf16[128,1024]{1,0:T(8,128)(2,1)S(1)} collective-permute-done((bf16[128,1024]{1,0:T(8,128)(2,1)S(1)}, bf16[128,1024]{1,0:T(8,128)(2,1)S(1)}, u32[]{:S(2)}, u32[]{:S(2)}) %collective-permute-start.16) | collective-permute-done | bytes 262176 | tf_op jit(solution)/shard_map/ppermute | solution.py:618
  62.1 1.9 %collective-permute-start.20 = (bf16[128,1024]{1,0:T(8,128)(2,1)S(1)}, bf16[128,1024]{1,0:T(8,128)(2,1)S(1)}, u32[]{:S(2)}, u32[]{:S(2)}) collective-permute-start(bf16[128,1024]{1,0:T(8,128)(2,1)S(1)} %collective-permute-done.16.refs_14_), channel_id=1, source_target_pairs={{0,4},{1,5},{2,6},{3,7},{4,8},{5,9},{6,10},{7,11},{8,12},{9,13},{1... | collective-permute-start | bytes 786440 | tf_op jit(solution)/shard_map/ppermute | solution.py:618
  64.1 3.8 %collective-permute-start.14 = (bf16[128,1024]{1,0:T(8,128)(2,1)S(1)}, bf16[128,1024]{1,0:T(8,128)(2,1)S(1)}, u32[]{:S(2)}, u32[]{:S(2)}) collective-permute-start(bf16[128,1024]{1,0:T(8,128)(2,1)S(1)} %collective-permute-done.12.refs_10_), channel_id=1, source_target_pairs={{0,1},{1,0},{2,3},{3,2},{4,5},{5,4},{6,7},{7,6},{8,9},{9,8},{10,11... | collective-permute-start | bytes 786440 | tf_op jit(solution)/shard_map/ppermute | solution.py:614
  68.4 2.9 %collective-permute-start.21 = (bf16[128,1024]{1,0:T(8,128)(2,1)S(1)}, bf16[128,1024]{1,0:T(8,128)(2,1)S(1)}, u32[]{:S(2)}, u32[]{:S(2)}) collective-permute-start(bf16[128,1024]{1,0:T(8,128)(2,1)S(1)} %collective-permute-done.19.refs_7_), channel_id=1, source_target_pairs={{0,1},{1,0},{2,3},{3,2},{4,5},{5,4},{6,7},{7,6},{8,9},{9,8},{10,11... | collective-permute-start | bytes 786440 | tf_op jit(solution)/shard_map/ppermute | solution.py:614
  71.3 2.0 %collective-permute-done.20.refs_8_ = bf16[128,1024]{1,0:T(8,128)(2,1)S(1)} collective-permute-done((bf16[128,1024]{1,0:T(8,128)(2,1)S(1)}, bf16[128,1024]{1,0:T(8,128)(2,1)S(1)}, u32[]{:S(2)}, u32[]{:S(2)}) %collective-permute-start.20) | collective-permute-done | bytes 262176 | tf_op jit(solution)/shard_map/ppermute | solution.py:618
  73.4 2.0 %collective-permute-start.22 = (bf16[128,1024]{1,0:T(8,128)(2,1)S(1)}, bf16[128,1024]{1,0:T(8,128)(2,1)S(1)}, u32[]{:S(2)}, u32[]{:S(2)}) collective-permute-start(bf16[128,1024]{1,0:T(8,128)(2,1)S(1)} %collective-permute-done.20.refs_8_), channel_id=1, source_target_pairs={{0,1},{1,0},{2,3},{3,2},{4,5},{5,4},{6,7},{7,6},{8,9},{9,8},{10,11... | collective-permute-start | bytes 786440 | tf_op jit(solution)/shard_map/ppermute | solution.py:614
  75.4 5.9 %attend.1 = (f32[512,512]{1,0:T(8,128)S(1)}, f32[512,128]{1,0:T(8,128)S(1)}) custom-call(s32[4,9]{1,0:T(4,128)S(1)} %get-tuple-element.51.refs_0_, s32[4]{0:T(128)S(1)} %get-tuple-element.52.refs_1_, s32[12]{0:T(128)S(1)} %get-tuple-element.53.refs_2_, bf16[256,512]{1,0:T(8,128)(2,1)S(1)} %get-tuple-element.50.refs_3_, ...), custom_call_target="tpu_custom_call" | custom-call | flops 536870912 | bytes 3145728 | tf_op jit(solution)/shard_map/attend/pallas_call | solution.py:558
  81.3 6.0 %attend_last.1 = (f32[256,512]{1,0:T(8,128)S(1)}, bf16[256,512]{1,0:T(8,128)(2,1)S(1)}, f32[8,256]{1,0:T(8,128)S(1)}, f32[8,256]{1,0:T(8,128)S(1)}) custom-call(s32[4,9]{1,0:T(4,128)S(1)} %get-tuple-element.37.refs_0_, s32[4]{0:T(128)S(1)} %get-tuple-element.38.refs_1_, s32[4]{0:T(128)S(1)} %get-tuple-element.39.refs_2_, ...), custom_call_target="tpu_custom_call" | custom-call | flops 536870912 | bytes 1048576 | tf_op jit(solution)/shard_map/attend_last/pallas_call | solution.py:558
  88.9 6.9 %collective-permute-done.24.plse_ref = f32[8,256]{1,0:T(8,128)S(1)} collective-permute-done((f32[8,256]{1,0:T(8,128)S(1)}, f32[8,256]{1,0:T(8,128)S(1)}, u32[]{:S(2)}, u32[]{:S(2)}) %collective-permute-start.24) | collective-permute-done | bytes 8224 | tf_op jit(solution)/shard_map/ppermute | solution.py:614
  95.7 1.7 %output.1 = bf16[256,1024]{1,0:T(8,128)(2,1)} custom-call(f32[256,512]{1,0:T(8,128)S(1)} %get-tuple-element.58.o_ref, f32[8,256]{1,0:T(8,128)S(1)} %get-tuple-element.59.lse_ref, bf16[256,512]{1,0:T(8,128)(2,1)S(1)} %collective-permute-done.23.po_ref, f32[8,256]{1,0:T(8,128)S(1)} %collective-permute-done.24.plse_ref, ...), custom_call_target="tpu_custom_call" | custom-call | tf_op jit(solution)/shard_map/output/pallas_call | solution.py:596
  (60 shorter events, 19.8 us)
Async XLA Ops:
  9.0 3.2 %collective-permute-start.2 = (bf16[272,128]{1,0:T(8,128)(2,1)S(1)}, bf16[272,128]{1,0:T(8,128)(2,1)S(1)}, u32[]{:S(2)}, u32[]{:S(2)}) collective-permute-start(bf16[272,128]{1,0:T(8,128)(2,1)S(1)} %get-tuple-element.45), channel_id=1, source_target_pairs={{0,2},{1,3},{2,0},{3,1},{4,6},{5,7},{6,4},{7,5},{8,10},{9,11},{10,... | collective-permute-start | bytes 208904 | tf_op jit(solution)/shard_map/ppermute | solution.py:614
  12.2 3.2 %collective-permute-start.3 = (bf16[272,128]{1,0:T(8,128)(2,1)S(1)}, bf16[272,128]{1,0:T(8,128)(2,1)S(1)}, u32[]{:S(2)}, u32[]{:S(2)}) collective-permute-start(bf16[272,128]{1,0:T(8,128)(2,1)S(1)} %shard_map.119), channel_id=1, source_target_pairs={{0,4},{1,5},{2,6},{3,7},{4,8},{5,9},{6,10},{7,11},{8,12},{9,13},{1... | collective-permute-start | bytes 208904 | tf_op jit(solution)/shard_map/ppermute | solution.py:618
  12.3 4.1 %collective-permute-start.4 = (bf16[272,128]{1,0:T(8,128)(2,1)S(1)}, bf16[272,128]{1,0:T(8,128)(2,1)S(1)}, u32[]{:S(2)}, u32[]{:S(2)}) collective-permute-start(bf16[272,128]{1,0:T(8,128)(2,1)S(1)} %shard_map.119), channel_id=1, source_target_pairs={{0,8},{1,9},{2,10},{3,11},{4,12},{5,13},{6,14},{7,15},{8,0},{9,1},... | collective-permute-start | bytes 208904 | tf_op jit(solution)/shard_map/ppermute | solution.py:618
  13.7 5.1 %collective-permute-start.5 = (bf16[272,128]{1,0:T(8,128)(2,1)S(1)}, bf16[272,128]{1,0:T(8,128)(2,1)S(1)}, u32[]{:S(2)}, u32[]{:S(2)}) collective-permute-start(bf16[272,128]{1,0:T(8,128)(2,1)S(1)} %shard_map.119), channel_id=1, source_target_pairs={{0,12},{1,13},{2,14},{3,15},{4,0},{5,1},{6,2},{7,3},{8,4},{9,5},{1... | collective-permute-start | bytes 208904 | tf_op jit(solution)/shard_map/ppermute | solution.py:618
  18.9 3.2 %collective-permute-start.6 = (bf16[256,128]{1,0:T(8,128)(2,1)S(1)}, bf16[256,128]{1,0:T(8,128)(2,1)S(1)}, u32[]{:S(2)}, u32[]{:S(2)}) collective-permute-start(bf16[256,128]{1,0:T(8,128)(2,1)S(1)} %get-tuple-element.47), channel_id=1, source_target_pairs={{0,2},{1,3},{2,0},{3,1},{4,6},{5,7},{6,4},{7,5},{8,10},{9,11},{10,... | collective-permute-start | bytes 196616 | tf_op jit(solution)/shard_map/ppermute | solution.py:614
  23.1 13.1 %collective-permute-start.7 = (bf16[2,256,128]{2,1,0:T(8,128)(2,1)S(1)}, bf16[2,256,128]{2,1,0:T(8,128)(2,1)S(1)}, u32[]{:S(2)}, u32[]{:S(2)}) collective-permute-start(bf16[2,256,128]{2,1,0:T(8,128)(2,1)S(1)} %get-tuple-element.49), channel_id=1, source_target_pairs={{0,1},{1,0},{2,3},{3,2},{4,5},{5,4},{6,7},{7,6},{8,9},{9,8},{10,11... | collective-permute-start | bytes 393224 | tf_op jit(solution)/shard_map/ppermute | solution.py:614
  27.4 2.6 %collective-permute-start = (s32[2,9]{1,0:T(2,128)}, s32[2,9]{1,0:T(2,128)S(1)}, u32[]{:S(2)}, u32[]{:S(2)}) collective-permute-start(s32[2,9]{1,0:T(2,128)} %get-tuple-element.36.refs_4_), channel_id=1, source_target_pairs={{0,2},{1,3},{2,0},{3,1},{4,6},{5,7},{6,4},{7,5},{8,10},{9,11},{10,... | collective-permute-start | bytes 224 | tf_op jit(solution)/shard_map/ppermute | solution.py:614
  38.5 6.8 %collective-permute-start.11 = (bf16[128,1024]{1,0:T(8,128)(2,1)S(1)}, bf16[128,1024]{1,0:T(8,128)(2,1)S(1)}, u32[]{:S(2)}, u32[]{:S(2)}) collective-permute-start(bf16[128,1024]{1,0:T(8,128)(2,1)S(1)} %get-tuple-element.54.refs_5_), channel_id=1, source_target_pairs={{0,4},{1,5},{2,6},{3,7},{4,8},{5,9},{6,10},{7,11},{8,12},{9,13},{1... | collective-permute-start | bytes 786440 | tf_op jit(solution)/shard_map/ppermute | solution.py:618
  38.6 12.3 %collective-permute-start.12 = (bf16[128,1024]{1,0:T(8,128)(2,1)S(1)}, bf16[128,1024]{1,0:T(8,128)(2,1)S(1)}, u32[]{:S(2)}, u32[]{:S(2)}) collective-permute-start(bf16[128,1024]{1,0:T(8,128)(2,1)S(1)} %get-tuple-element.55.refs_6_), channel_id=1, source_target_pairs={{0,4},{1,5},{2,6},{3,7},{4,8},{5,9},{6,10},{7,11},{8,12},{9,13},{1... | collective-permute-start | bytes 786440 | tf_op jit(solution)/shard_map/ppermute | solution.py:618
  40.0 16.7 %collective-permute-start.8 = (bf16[256,512]{1,0:T(8,128)(2,1)S(1)}, bf16[256,512]{1,0:T(8,128)(2,1)S(1)}, u32[]{:S(2)}, u32[]{:S(2)}) collective-permute-start(bf16[256,512]{1,0:T(8,128)(2,1)S(1)} %get-tuple-element.50.refs_3_), channel_id=1, source_target_pairs={{0,2},{1,3},{2,0},{3,1},{4,6},{5,7},{6,4},{7,5},{8,10},{9,11},{10,... | collective-permute-start | bytes 786440 | tf_op jit(solution)/shard_map/ppermute | solution.py:614
  45.3 11.9 %collective-permute-start.15 = (bf16[128,1024]{1,0:T(8,128)(2,1)S(1)}, bf16[128,1024]{1,0:T(8,128)(2,1)S(1)}, u32[]{:S(2)}, u32[]{:S(2)}) collective-permute-start(bf16[128,1024]{1,0:T(8,128)(2,1)S(1)} %collective-permute-done.11.refs_9_), channel_id=1, source_target_pairs={{0,4},{1,5},{2,6},{3,7},{4,8},{5,9},{6,10},{7,11},{8,12},{9,13},{1... | collective-permute-start | bytes 786440 | tf_op jit(solution)/shard_map/ppermute | solution.py:618
  50.9 11.2 %collective-permute-start.16 = (bf16[128,1024]{1,0:T(8,128)(2,1)S(1)}, bf16[128,1024]{1,0:T(8,128)(2,1)S(1)}, u32[]{:S(2)}, u32[]{:S(2)}) collective-permute-start(bf16[128,1024]{1,0:T(8,128)(2,1)S(1)} %collective-permute-done.12.refs_10_), channel_id=1, source_target_pairs={{0,4},{1,5},{2,6},{3,7},{4,8},{5,9},{6,10},{7,11},{8,12},{9,13},{1... | collective-permute-start | bytes 786440 | tf_op jit(solution)/shard_map/ppermute | solution.py:618
  52.8 11.2 %collective-permute-start.9 = (bf16[128,1024]{1,0:T(8,128)(2,1)S(1)}, bf16[128,1024]{1,0:T(8,128)(2,1)S(1)}, u32[]{:S(2)}, u32[]{:S(2)}) collective-permute-start(bf16[128,1024]{1,0:T(8,128)(2,1)S(1)} %get-tuple-element.54.refs_5_), channel_id=1, source_target_pairs={{0,1},{1,0},{2,3},{3,2},{4,5},{5,4},{6,7},{7,6},{8,9},{9,8},{10,11... | collective-permute-start | bytes 786440 | tf_op jit(solution)/shard_map/ppermute | solution.py:614
  56.6 11.2 %collective-permute-start.10 = (bf16[128,1024]{1,0:T(8,128)(2,1)S(1)}, bf16[128,1024]{1,0:T(8,128)(2,1)S(1)}, u32[]{:S(2)}, u32[]{:S(2)}) collective-permute-start(bf16[128,1024]{1,0:T(8,128)(2,1)S(1)} %get-tuple-element.55.refs_6_), channel_id=1, source_target_pairs={{0,1},{1,0},{2,3},{3,2},{4,5},{5,4},{6,7},{7,6},{8,9},{9,8},{10,11... | collective-permute-start | bytes 786440 | tf_op jit(solution)/shard_map/ppermute | solution.py:614
  56.6 11.3 %collective-permute-start.13 = (bf16[128,1024]{1,0:T(8,128)(2,1)S(1)}, bf16[128,1024]{1,0:T(8,128)(2,1)S(1)}, u32[]{:S(2)}, u32[]{:S(2)}) collective-permute-start(bf16[128,1024]{1,0:T(8,128)(2,1)S(1)} %collective-permute-done.11.refs_9_), channel_id=1, source_target_pairs={{0,1},{1,0},{2,3},{3,2},{4,5},{5,4},{6,7},{7,6},{8,9},{9,8},{10,11... | collective-permute-start | bytes 786440 | tf_op jit(solution)/shard_map/ppermute | solution.py:614
  57.1 11.2 %collective-permute-start.19 = (bf16[128,1024]{1,0:T(8,128)(2,1)S(1)}, bf16[128,1024]{1,0:T(8,128)(2,1)S(1)}, u32[]{:S(2)}, u32[]{:S(2)}) collective-permute-start(bf16[128,1024]{1,0:T(8,128)(2,1)S(1)} %collective-permute-done.15.refs_13_), channel_id=1, source_target_pairs={{0,4},{1,5},{2,6},{3,7},{4,8},{5,9},{6,10},{7,11},{8,12},{9,13},{1... | collective-permute-start | bytes 786440 | tf_op jit(solution)/shard_map/ppermute | solution.py:618
  62.1 11.2 %collective-permute-start.20 = (bf16[128,1024]{1,0:T(8,128)(2,1)S(1)}, bf16[128,1024]{1,0:T(8,128)(2,1)S(1)}, u32[]{:S(2)}, u32[]{:S(2)}) collective-permute-start(bf16[128,1024]{1,0:T(8,128)(2,1)S(1)} %collective-permute-done.16.refs_14_), channel_id=1, source_target_pairs={{0,4},{1,5},{2,6},{3,7},{4,8},{5,9},{6,10},{7,11},{8,12},{9,13},{1... | collective-permute-start | bytes 786440 | tf_op jit(solution)/shard_map/ppermute | solution.py:618
  64.1 11.3 %collective-permute-start.14 = (bf16[128,1024]{1,0:T(8,128)(2,1)S(1)}, bf16[128,1024]{1,0:T(8,128)(2,1)S(1)}, u32[]{:S(2)}, u32[]{:S(2)}) collective-permute-start(bf16[128,1024]{1,0:T(8,128)(2,1)S(1)} %collective-permute-done.12.refs_10_), channel_id=1, source_target_pairs={{0,1},{1,0},{2,3},{3,2},{4,5},{5,4},{6,7},{7,6},{8,9},{9,8},{10,11... | collective-permute-start | bytes 786440 | tf_op jit(solution)/shard_map/ppermute | solution.py:614
  67.9 7.5 %collective-permute-start.17 = (bf16[128,1024]{1,0:T(8,128)(2,1)S(1)}, bf16[128,1024]{1,0:T(8,128)(2,1)S(1)}, u32[]{:S(2)}, u32[]{:S(2)}) collective-permute-start(bf16[128,1024]{1,0:T(8,128)(2,1)S(1)} %collective-permute-done.15.refs_13_), channel_id=1, source_target_pairs={{0,1},{1,0},{2,3},{3,2},{4,5},{5,4},{6,7},{7,6},{8,9},{9,8},{10,11... | collective-permute-start | bytes 786440 | tf_op jit(solution)/shard_map/ppermute | solution.py:614
  67.9 7.4 %collective-permute-start.18 = (bf16[128,1024]{1,0:T(8,128)(2,1)S(1)}, bf16[128,1024]{1,0:T(8,128)(2,1)S(1)}, u32[]{:S(2)}, u32[]{:S(2)}) collective-permute-start(bf16[128,1024]{1,0:T(8,128)(2,1)S(1)} %collective-permute-done.16.refs_14_), channel_id=1, source_target_pairs={{0,1},{1,0},{2,3},{3,2},{4,5},{5,4},{6,7},{7,6},{8,9},{9,8},{10,11... | collective-permute-start | bytes 786440 | tf_op jit(solution)/shard_map/ppermute | solution.py:614
  68.4 12.9 %collective-permute-start.21 = (bf16[128,1024]{1,0:T(8,128)(2,1)S(1)}, bf16[128,1024]{1,0:T(8,128)(2,1)S(1)}, u32[]{:S(2)}, u32[]{:S(2)}) collective-permute-start(bf16[128,1024]{1,0:T(8,128)(2,1)S(1)} %collective-permute-done.19.refs_7_), channel_id=1, source_target_pairs={{0,1},{1,0},{2,3},{3,2},{4,5},{5,4},{6,7},{7,6},{8,9},{9,8},{10,11... | collective-permute-start | bytes 786440 | tf_op jit(solution)/shard_map/ppermute | solution.py:614
  73.4 8.0 %collective-permute-start.22 = (bf16[128,1024]{1,0:T(8,128)(2,1)S(1)}, bf16[128,1024]{1,0:T(8,128)(2,1)S(1)}, u32[]{:S(2)}, u32[]{:S(2)}) collective-permute-start(bf16[128,1024]{1,0:T(8,128)(2,1)S(1)} %collective-permute-done.20.refs_8_), channel_id=1, source_target_pairs={{0,1},{1,0},{2,3},{3,2},{4,5},{5,4},{6,7},{7,6},{8,9},{9,8},{10,11... | collective-permute-start | bytes 786440 | tf_op jit(solution)/shard_map/ppermute | solution.py:614
  87.3 8.4 %collective-permute-start.23 = (bf16[256,512]{1,0:T(8,128)(2,1)S(1)}, bf16[256,512]{1,0:T(8,128)(2,1)S(1)}, u32[]{:S(2)}, u32[]{:S(2)}) collective-permute-start(bf16[256,512]{1,0:T(8,128)(2,1)S(1)} %get-tuple-element.60), channel_id=1, source_target_pairs={{0,2},{1,3},{2,0},{3,1},{4,6},{5,7},{6,4},{7,5},{8,10},{9,11},{10,... | collective-permute-start | bytes 786440 | tf_op jit(solution)/shard_map/ppermute | solution.py:614
  88.3 7.4 %collective-permute-start.24 = (f32[8,256]{1,0:T(8,128)S(1)}, f32[8,256]{1,0:T(8,128)S(1)}, u32[]{:S(2)}, u32[]{:S(2)}) collective-permute-start(f32[8,256]{1,0:T(8,128)S(1)} %get-tuple-element.61), channel_id=1, source_target_pairs={{0,2},{1,3},{2,0},{3,1},{4,6},{5,7},{6,4},{7,5},{8,10},{9,11},{10,... | collective-permute-start | bytes 24584 | tf_op jit(solution)/shard_map/ppermute | solution.py:614
  (13 other events, 207.7 us)

commit v2 on v1

--- a/solution.py
+++ b/solution.py
@@ -51,10 +51,6 @@
     return lax.dot_general(a, b, (((1,), (1,)), ((), ())), preferred_element_type=F32, **kw)
 
 
-def tn(a, b, **kw):
-    return lax.dot_general(a, b, (((0,), (0,)), ((), ())), preferred_element_type=F32, **kw)
-
-
 def by_chain(x):
     rows = x.shape[0]
     chain = chain_of(lax.broadcasted_iota(jnp.int32, (rows, DK), 0))
@@ -110,44 +106,52 @@
     return lane // 2, lane & 1
 
 
-def local_kernel(x_in, ld_in, wk_in, wv_in, idx, cnt, k_ref, v_ref, keep, give, pack, *rest):
-    chunks, x_ref, ld_ref, bk, bv, sems = rest
+def local_kernel(x_in, ld_in, wk_in, wv_in, idx_in, cnt_in, k_ref, v_ref, keep, give, pack, *rest):
+    chunks, x_ref, ld_ref, bk, bv, idx, cnt, sems = rest
     rows = x_ref.shape[0]
     copies = [
         pltpu.make_async_copy(src, dst, sems.at[i])
         for i, (src, dst) in enumerate(
-            ((ld_in, ld_ref), (x_in, x_ref), (wk_in, bk), (wv_in, bv))
+            (
+                (ld_in, ld_ref),
+                (x_in, x_ref),
+                (wk_in, bk),
+                (wv_in, bv),
+                (idx_in, idx),
+                (cnt_in, cnt),
+            )
         )
     ]
     for copy in copies:
         copy.start()
-    frames, slots = idx.shape
-    for f in range(frames):
-        for i in range(slots):
-            pack[f, i] = idx[f, i]
-        pack[f, slots] = cnt[f]
     t = lax.broadcasted_iota(jnp.int32, (rows, rows), 0)
     s = lax.broadcasted_iota(jnp.int32, (rows, rows), 1)
     after = ((s > t) & (chain_of(s) == chain_of(t))).astype(F32)
     copies[0].wait()
     ld = ld_ref[...]
-    tail = jnp.exp(column_sums(after, ld))
+    tail = jnp.exp(row_sums(after, ld))
     chain = chain_of(lax.broadcasted_iota(jnp.int32, ld.shape, 1))
     sums = [jnp.sum(jnp.where(chain == b, ld, 0.0), axis=1, keepdims=True) for b in (0, 1)]
-    for copy in copies[1:]:
-        copy.wait()
+    tails = [jnp.where(chain == b, tail, 0.0) for b in (0, 1)]
+    copies[1].wait()
+    copies[2].wait()
     x = x_ref[...]
     k = nn(x, bk[...]).astype(BF16)
     k_ref[...] = k
+    turned = [
+        jnp.transpose(k[:, q * HC * DK : (q + 1) * HC * DK].astype(F32)) for q in range(LANES)
+    ]
+    for copy in copies[3:]:
+        copy.wait()
+    v = nn(x, bv[...]).astype(BF16)
+    v_ref[...] = v
     for q in range(LANES):
-        vc = slice(q * HC * DV, (q + 1) * HC * DV)
-        v = nn(x, bv[:, vc]).astype(BF16)
-        v_ref[:, vc] = v
         states, totals = [], []
         for i in range(HC):
             h = q * HC + i
-            kt = (k[:, h * DK : (h + 1) * DK].astype(F32) * tail[:, h : h + 1]).astype(BF16)
-            states.append(tn(by_chain(kt), v[:, i * DV : (i + 1) * DV]))
+            kt = turned[q][i * DK : (i + 1) * DK]
+            both = jnp.concatenate([(kt * tails[b][h : h + 1]).astype(BF16) for b in (0, 1)], axis=0)
+            states.append(nn(both, v[:, h * DV : (h + 1) * DV]))
             totals += [jnp.broadcast_to(sums[b][h : h + 1], (1, DV)) for b in (0, 1)]
         write_message(
             chunks.at[q], jnp.concatenate(states, axis=0), jnp.concatenate(totals, axis=0)
@@ -156,6 +160,11 @@
     for y in range(2):
         keep[y] = chunks[2 * y + core]
         give[y] = chunks[2 * y + 1 - core]
+    frames, slots = idx.shape
+    for f in range(frames):
+        for i in range(slots):
+            pack[f, i] = idx[f, i]
+        pack[f, slots] = cnt[f]
 
 
 def local(tokens, w_rk, w_rv, ld, index, live):
@@ -164,7 +173,7 @@
     frames, slots = index.shape
     return pl.pallas_call(
         local_kernel,
-        in_specs=[HBM] * 4 + [SMEM] * 2,
+        in_specs=[HBM] * 6,
         out_specs=[VMEM] * 4 + [SMEM],
         out_shape=[
             jax.ShapeDtypeStruct((rows, H * DK), BF16),
@@ -179,7 +188,9 @@
             pltpu.VMEM((H, rows), F32),
             pltpu.VMEM((d, H * DK), BF16),
             pltpu.VMEM((d, H * DV), BF16),
-            pltpu.SemaphoreType.DMA((4,)),
+            pltpu.SMEM((frames, slots), jnp.int32),
+            pltpu.SMEM((frames,), jnp.int32),
+            pltpu.SemaphoreType.DMA((6,)),
         ],
         compiler_params=params(62),
         name="local",

time: 97.7 us -> 95.7 us (0.980)
  Pallas kernels: 25.7 us -> 23.7 us
    pallas_call x1, Pallas kernels: 5.97 us -> 3.93 us  [local(): pl.pallas_call(local_kernel, in_specs=[HBM] * 6, out_specs=[VMEM] * 4 + [...]
where the time goes in v2:
time: 95.7 us; the launch traced here: 95.4 us
  starting transfers between devices  35.2 us (37%)
  waiting for transfers between devices  31.8 us (33%)
  Pallas kernels  23.7 us (25%)
  local copies, waits for them, and re-layouts  4.52 us (5%)
    ppermute x16, starting transfers between devices, flip(): return lax.ppermute(x, 'tm', [(i, i ^ bits) for i in range(size)])  25.2 us
    ppermute x9, waiting for transfers between devices, up(): return lax.ppermute(x, 'tm', [(i, (i + step) % size) for i in range(size)])  18.5 us
    ppermute x16, waiting for transfers between devices, flip(): return lax.ppermute(x, 'tm', [(i, i ^ bits) for i in range(size)])  13.3 us
    pallas_call x2, Pallas kernels, attend(): pl.pallas_call(functools.partial(attend_kernel, frames, blocks, first, la...  11.9 us
    ppermute x9, starting transfers between devices, up(): return lax.ppermute(x, 'tm', [(i, (i + step) % size) for i in range(size)])  10.1 us
    unnamed x24, local copies, waits for them, and re-layouts  4.52 us
    pallas_call x1, Pallas kernels, local(): pl.pallas_call(local_kernel, in_specs=[HBM] * 6, out_specs=[VMEM] * 4 + [...  3.93 us
    pallas_call x1, Pallas kernels, inner(): pl.pallas_call(functools.partial(inner_kernel, frames, distances), in_spe...  3.53 us
  transfers between devices with their start and end apart: 25, of which 12 were waited for; matrix products, arithmetic and copies ran while one was open for 0% of the time, Pallas kernels for 10%

profile of v2, /device:TPU:27, one launch (start us, length us, event | category | flops | bytes accessed | tf_op | source)
XLA Modules:
  0.0 95.4 jit_solution(14932030596737602299)
XLA Ops:
  0.0 3.9 %local.1 = (bf16[256,512]{1,0:T(8,128)(2,1)}, bf16[256,1024]{1,0:T(8,128)(2,1)}, bf16[2,272,128]{2,1,0:T(8,128)(2,1)}, bf16[2,272,128]{2,1,0:T(8,128)(2,1)}, s32[2,9]{1,0:T(2,128)}) custom-call(bf16[256,1024]{1,0:T(8,128)(2,1)} %refs_4_.1, f32[8,256]{1,0:T(8,128)} %refs_1_.1, bf16[1024,512]{1,0:T(8,128)(2,1)} %wk_in.1, bf16[1024,1024]{1,0:T(8,128)(2,1)} %wv_in.1, ...), custom_call_target="tpu_custom_call" | custom-call | tf_op jit(solution)/shard_map/local/pallas_call | solution.py:174
  8.2 1.9 %collective-permute-done.2.got.refs_1_ = bf16[272,128]{1,0:T(8,128)(2,1)S(1)} collective-permute-done((bf16[272,128]{1,0:T(8,128)(2,1)S(1)}, bf16[272,128]{1,0:T(8,128)(2,1)S(1)}, u32[]{:S(2)}, u32[]{:S(2)}) %collective-permute-start.2) | collective-permute-done | bytes 69664 | tf_op jit(solution)/shard_map/ppermute | solution.py:625
  11.8 1.6 %collective-permute-done.3.refs_2_ = bf16[272,128]{1,0:T(8,128)(2,1)S(1)} collective-permute-done((bf16[272,128]{1,0:T(8,128)(2,1)S(1)}, bf16[272,128]{1,0:T(8,128)(2,1)S(1)}, u32[]{:S(2)}, u32[]{:S(2)}) %collective-permute-start.3) | collective-permute-done | bytes 69664 | tf_op jit(solution)/shard_map/ppermute | solution.py:629
  14.4 2.4 %collective-permute-done.5.refs_4_ = bf16[272,128]{1,0:T(8,128)(2,1)S(1)} collective-permute-done((bf16[272,128]{1,0:T(8,128)(2,1)S(1)}, bf16[272,128]{1,0:T(8,128)(2,1)S(1)}, u32[]{:S(2)}, u32[]{:S(2)}) %collective-permute-start.5) | collective-permute-done | bytes 69664 | tf_op jit(solution)/shard_map/ppermute | solution.py:629
  18.2 1.9 %collective-permute-done.6.got = bf16[256,128]{1,0:T(8,128)(2,1)S(1)} collective-permute-done((bf16[256,128]{1,0:T(8,128)(2,1)S(1)}, bf16[256,128]{1,0:T(8,128)(2,1)S(1)}, u32[]{:S(2)}, u32[]{:S(2)}) %collective-permute-start.6) | collective-permute-done | bytes 65568 | tf_op jit(solution)/shard_map/ppermute | solution.py:625
  21.1 4.2 %collective-permute-start.7 = (bf16[2,256,128]{2,1,0:T(8,128)(2,1)S(1)}, bf16[2,256,128]{2,1,0:T(8,128)(2,1)S(1)}, u32[]{:S(2)}, u32[]{:S(2)}) collective-permute-start(bf16[2,256,128]{2,1,0:T(8,128)(2,1)S(1)} %get-tuple-element.49), channel_id=1, source_target_pairs={{0,1},{1,0},{2,3},{3,2},{4,5},{5,4},{6,7},{7,6},{8,9},{9,8},{10,11... | collective-permute-start | bytes 393224 | tf_op jit(solution)/shard_map/ppermute | solution.py:625
  26.6 1.4 %collective-permute-done.refs_5_ = s32[2,9]{1,0:T(2,128)S(1)} collective-permute-done((s32[2,9]{1,0:T(2,128)}, s32[2,9]{1,0:T(2,128)S(1)}, u32[]{:S(2)}, u32[]{:S(2)}) %collective-permute-start) | collective-permute-done | bytes 104 | tf_op jit(solution)/shard_map/ppermute | solution.py:625
  30.7 3.5 %inner.1 = (f32[256,1024]{1,0:T(8,128)S(1)}, bf16[256,1024]{1,0:T(8,128)(2,1)S(1)}, s32[4,9]{1,0:T(4,128)S(1)}, s32[4]{0:T(128)S(1)}, s32[12]{0:T(128)S(1)}, /*i...) custom-call(bf16[256,1024]{1,0:T(8,128)(2,1)S(1)} %copy-done, f32[8,256]{1,0:T(8,128)S(1)} %copy-done.9, ...), custom_call_target="tpu_custom_call" | custom-call | flops 268435456 | bytes 8388608 | tf_op jit(solution)/shard_map/inner/pallas_call | solution.py:294
  34.2 2.2 %hidden.1 = (bf16[256,1024]{1,0:T(8,128)(2,1)S(1)}, bf16[256,512]{1,0:T(8,128)(2,1)S(1)}, bf16[128,1024]{1,0:T(8,128)(2,1)S(1)}, bf16[128,1024]{1,0:T(8,128)(2,1)S(1)}) custom-call(f32[256,1024]{1,0:T(8,128)S(1)} %get-tuple-element.40.refs_0_, bf16[256,1024]{1,0:T(8,128)(2,1)S(1)} %get-tuple-element.41.refs_1_, ...), custom_call_target="tpu_custom_call" | custom-call | tf_op jit(solution)/shard_map/hidden/pallas_call | solution.py:419
  39.2 4.1 %collective-permute-done.11.refs_9_ = bf16[128,1024]{1,0:T(8,128)(2,1)S(1)} collective-permute-done((bf16[128,1024]{1,0:T(8,128)(2,1)S(1)}, bf16[128,1024]{1,0:T(8,128)(2,1)S(1)}, u32[]{:S(2)}, u32[]{:S(2)}) %collective-permute-start.11) | collective-permute-done | bytes 262176 | tf_op jit(solution)/shard_map/ppermute | solution.py:629
  43.3 1.9 %collective-permute-start.15 = (bf16[128,1024]{1,0:T(8,128)(2,1)S(1)}, bf16[128,1024]{1,0:T(8,128)(2,1)S(1)}, u32[]{:S(2)}, u32[]{:S(2)}) collective-permute-start(bf16[128,1024]{1,0:T(8,128)(2,1)S(1)} %collective-permute-done.11.refs_9_), channel_id=1, source_target_pairs={{0,4},{1,5},{2,6},{3,7},{4,8},{5,9},{6,10},{7,11},{8,12},{9,13},{1... | collective-permute-start | bytes 786440 | tf_op jit(solution)/shard_map/ppermute | solution.py:629
  45.2 3.7 %collective-permute-done.12.refs_10_ = bf16[128,1024]{1,0:T(8,128)(2,1)S(1)} collective-permute-done((bf16[128,1024]{1,0:T(8,128)(2,1)S(1)}, bf16[128,1024]{1,0:T(8,128)(2,1)S(1)}, u32[]{:S(2)}, u32[]{:S(2)}) %collective-permute-start.12) | collective-permute-done | bytes 262176 | tf_op jit(solution)/shard_map/ppermute | solution.py:629
  48.9 1.9 %collective-permute-start.16 = (bf16[128,1024]{1,0:T(8,128)(2,1)S(1)}, bf16[128,1024]{1,0:T(8,128)(2,1)S(1)}, u32[]{:S(2)}, u32[]{:S(2)}) collective-permute-start(bf16[128,1024]{1,0:T(8,128)(2,1)S(1)} %collective-permute-done.12.refs_10_), channel_id=1, source_target_pairs={{0,4},{1,5},{2,6},{3,7},{4,8},{5,9},{6,10},{7,11},{8,12},{9,13},{1... | collective-permute-start | bytes 786440 | tf_op jit(solution)/shard_map/ppermute | solution.py:629
  50.8 3.8 %collective-permute-start.9 = (bf16[128,1024]{1,0:T(8,128)(2,1)S(1)}, bf16[128,1024]{1,0:T(8,128)(2,1)S(1)}, u32[]{:S(2)}, u32[]{:S(2)}) collective-permute-start(bf16[128,1024]{1,0:T(8,128)(2,1)S(1)} %get-tuple-element.54.refs_5_), channel_id=1, source_target_pairs={{0,1},{1,0},{2,3},{3,2},{4,5},{5,4},{6,7},{7,6},{8,9},{9,8},{10,11... | collective-permute-start | bytes 786440 | tf_op jit(solution)/shard_map/ppermute | solution.py:625
  56.4 3.7 %collective-permute-done.16.refs_14_ = bf16[128,1024]{1,0:T(8,128)(2,1)S(1)} collective-permute-done((bf16[128,1024]{1,0:T(8,128)(2,1)S(1)}, bf16[128,1024]{1,0:T(8,128)(2,1)S(1)}, u32[]{:S(2)}, u32[]{:S(2)}) %collective-permute-start.16) | collective-permute-done | bytes 262176 | tf_op jit(solution)/shard_map/ppermute | solution.py:629
  60.1 1.9 %collective-permute-start.20 = (bf16[128,1024]{1,0:T(8,128)(2,1)S(1)}, bf16[128,1024]{1,0:T(8,128)(2,1)S(1)}, u32[]{:S(2)}, u32[]{:S(2)}) collective-permute-start(bf16[128,1024]{1,0:T(8,128)(2,1)S(1)} %collective-permute-done.16.refs_14_), channel_id=1, source_target_pairs={{0,4},{1,5},{2,6},{3,7},{4,8},{5,9},{6,10},{7,11},{8,12},{9,13},{1... | collective-permute-start | bytes 786440 | tf_op jit(solution)/shard_map/ppermute | solution.py:629
  62.0 3.8 %collective-permute-start.14 = (bf16[128,1024]{1,0:T(8,128)(2,1)S(1)}, bf16[128,1024]{1,0:T(8,128)(2,1)S(1)}, u32[]{:S(2)}, u32[]{:S(2)}) collective-permute-start(bf16[128,1024]{1,0:T(8,128)(2,1)S(1)} %collective-permute-done.12.refs_10_), channel_id=1, source_target_pairs={{0,1},{1,0},{2,3},{3,2},{4,5},{5,4},{6,7},{7,6},{8,9},{9,8},{10,11... | collective-permute-start | bytes 786440 | tf_op jit(solution)/shard_map/ppermute | solution.py:625
  66.3 2.9 %collective-permute-start.21 = (bf16[128,1024]{1,0:T(8,128)(2,1)S(1)}, bf16[128,1024]{1,0:T(8,128)(2,1)S(1)}, u32[]{:S(2)}, u32[]{:S(2)}) collective-permute-start(bf16[128,1024]{1,0:T(8,128)(2,1)S(1)} %collective-permute-done.19.refs_7_), channel_id=1, source_target_pairs={{0,1},{1,0},{2,3},{3,2},{4,5},{5,4},{6,7},{7,6},{8,9},{9,8},{10,11... | collective-permute-start | bytes 786440 | tf_op jit(solution)/shard_map/ppermute | solution.py:625
  69.3 2.1 %collective-permute-done.20.refs_8_ = bf16[128,1024]{1,0:T(8,128)(2,1)S(1)} collective-permute-done((bf16[128,1024]{1,0:T(8,128)(2,1)S(1)}, bf16[128,1024]{1,0:T(8,128)(2,1)S(1)}, u32[]{:S(2)}, u32[]{:S(2)}) %collective-permute-start.20) | collective-permute-done | bytes 262176 | tf_op jit(solution)/shard_map/ppermute | solution.py:629
  71.3 2.0 %collective-permute-start.22 = (bf16[128,1024]{1,0:T(8,128)(2,1)S(1)}, bf16[128,1024]{1,0:T(8,128)(2,1)S(1)}, u32[]{:S(2)}, u32[]{:S(2)}) collective-permute-start(bf16[128,1024]{1,0:T(8,128)(2,1)S(1)} %collective-permute-done.20.refs_8_), channel_id=1, source_target_pairs={{0,1},{1,0},{2,3},{3,2},{4,5},{5,4},{6,7},{7,6},{8,9},{9,8},{10,11... | collective-permute-start | bytes 786440 | tf_op jit(solution)/shard_map/ppermute | solution.py:625
  73.3 5.9 %attend.1 = (f32[512,512]{1,0:T(8,128)S(1)}, f32[512,128]{1,0:T(8,128)S(1)}) custom-call(s32[4,9]{1,0:T(4,128)S(1)} %get-tuple-element.51.refs_0_, s32[4]{0:T(128)S(1)} %get-tuple-element.52.refs_1_, s32[12]{0:T(128)S(1)} %get-tuple-element.53.refs_2_, bf16[256,512]{1,0:T(8,128)(2,1)S(1)} %get-tuple-element.50.refs_3_, ...), custom_call_target="tpu_custom_call" | custom-call | flops 536870912 | bytes 3145728 | tf_op jit(solution)/shard_map/attend/pallas_call | solution.py:569
  79.3 6.0 %attend_last.1 = (f32[256,512]{1,0:T(8,128)S(1)}, bf16[256,512]{1,0:T(8,128)(2,1)S(1)}, f32[8,256]{1,0:T(8,128)S(1)}, f32[8,256]{1,0:T(8,128)S(1)}) custom-call(s32[4,9]{1,0:T(4,128)S(1)} %get-tuple-element.37.refs_0_, s32[4]{0:T(128)S(1)} %get-tuple-element.38.refs_1_, s32[4]{0:T(128)S(1)} %get-tuple-element.39.refs_2_, ...), custom_call_target="tpu_custom_call" | custom-call | flops 536870912 | bytes 1048576 | tf_op jit(solution)/shard_map/attend_last/pallas_call | solution.py:569
  86.8 6.9 %collective-permute-done.24.plse_ref = f32[8,256]{1,0:T(8,128)S(1)} collective-permute-done((f32[8,256]{1,0:T(8,128)S(1)}, f32[8,256]{1,0:T(8,128)S(1)}, u32[]{:S(2)}, u32[]{:S(2)}) %collective-permute-start.24) | collective-permute-done | bytes 8224 | tf_op jit(solution)/shard_map/ppermute | solution.py:625
  93.7 1.7 %output.1 = bf16[256,1024]{1,0:T(8,128)(2,1)} custom-call(f32[256,512]{1,0:T(8,128)S(1)} %get-tuple-element.58.o_ref, f32[8,256]{1,0:T(8,128)S(1)} %get-tuple-element.59.lse_ref, bf16[256,512]{1,0:T(8,128)(2,1)S(1)} %collective-permute-done.23.po_ref, f32[8,256]{1,0:T(8,128)S(1)} %collective-permute-done.24.plse_ref, ...), custom_call_target="tpu_custom_call" | custom-call | tf_op jit(solution)/shard_map/output/pallas_call | solution.py:607
  (60 shorter events, 19.8 us)
Async XLA Ops:
  6.9 3.2 %collective-permute-start.2 = (bf16[272,128]{1,0:T(8,128)(2,1)S(1)}, bf16[272,128]{1,0:T(8,128)(2,1)S(1)}, u32[]{:S(2)}, u32[]{:S(2)}) collective-permute-start(bf16[272,128]{1,0:T(8,128)(2,1)S(1)} %get-tuple-element.45), channel_id=1, source_target_pairs={{0,2},{1,3},{2,0},{3,1},{4,6},{5,7},{6,4},{7,5},{8,10},{9,11},{10,... | collective-permute-start | bytes 208904 | tf_op jit(solution)/shard_map/ppermute | solution.py:625
  10.2 3.2 %collective-permute-start.3 = (bf16[272,128]{1,0:T(8,128)(2,1)S(1)}, bf16[272,128]{1,0:T(8,128)(2,1)S(1)}, u32[]{:S(2)}, u32[]{:S(2)}) collective-permute-start(bf16[272,128]{1,0:T(8,128)(2,1)S(1)} %shard_map.119), channel_id=1, source_target_pairs={{0,4},{1,5},{2,6},{3,7},{4,8},{5,9},{6,10},{7,11},{8,12},{9,13},{1... | collective-permute-start | bytes 208904 | tf_op jit(solution)/shard_map/ppermute | solution.py:629
  10.3 4.1 %collective-permute-start.4 = (bf16[272,128]{1,0:T(8,128)(2,1)S(1)}, bf16[272,128]{1,0:T(8,128)(2,1)S(1)}, u32[]{:S(2)}, u32[]{:S(2)}) collective-permute-start(bf16[272,128]{1,0:T(8,128)(2,1)S(1)} %shard_map.119), channel_id=1, source_target_pairs={{0,8},{1,9},{2,10},{3,11},{4,12},{5,13},{6,14},{7,15},{8,0},{9,1},... | collective-permute-start | bytes 208904 | tf_op jit(solution)/shard_map/ppermute | solution.py:629
  11.6 5.1 %collective-permute-start.5 = (bf16[272,128]{1,0:T(8,128)(2,1)S(1)}, bf16[272,128]{1,0:T(8,128)(2,1)S(1)}, u32[]{:S(2)}, u32[]{:S(2)}) collective-permute-start(bf16[272,128]{1,0:T(8,128)(2,1)S(1)} %shard_map.119), channel_id=1, source_target_pairs={{0,12},{1,13},{2,14},{3,15},{4,0},{5,1},{6,2},{7,3},{8,4},{9,5},{1... | collective-permute-start | bytes 208904 | tf_op jit(solution)/shard_map/ppermute | solution.py:629
  16.9 3.2 %collective-permute-start.6 = (bf16[256,128]{1,0:T(8,128)(2,1)S(1)}, bf16[256,128]{1,0:T(8,128)(2,1)S(1)}, u32[]{:S(2)}, u32[]{:S(2)}) collective-permute-start(bf16[256,128]{1,0:T(8,128)(2,1)S(1)} %get-tuple-element.47), channel_id=1, source_target_pairs={{0,2},{1,3},{2,0},{3,1},{4,6},{5,7},{6,4},{7,5},{8,10},{9,11},{10,... | collective-permute-start | bytes 196616 | tf_op jit(solution)/shard_map/ppermute | solution.py:625
  21.1 13.1 %collective-permute-start.7 = (bf16[2,256,128]{2,1,0:T(8,128)(2,1)S(1)}, bf16[2,256,128]{2,1,0:T(8,128)(2,1)S(1)}, u32[]{:S(2)}, u32[]{:S(2)}) collective-permute-start(bf16[2,256,128]{2,1,0:T(8,128)(2,1)S(1)} %get-tuple-element.49), channel_id=1, source_target_pairs={{0,1},{1,0},{2,3},{3,2},{4,5},{5,4},{6,7},{7,6},{8,9},{9,8},{10,11... | collective-permute-start | bytes 393224 | tf_op jit(solution)/shard_map/ppermute | solution.py:625
  25.3 2.6 %collective-permute-start = (s32[2,9]{1,0:T(2,128)}, s32[2,9]{1,0:T(2,128)S(1)}, u32[]{:S(2)}, u32[]{:S(2)}) collective-permute-start(s32[2,9]{1,0:T(2,128)} %get-tuple-element.36.refs_4_), channel_id=1, source_target_pairs={{0,2},{1,3},{2,0},{3,1},{4,6},{5,7},{6,4},{7,5},{8,10},{9,11},{10,... | collective-permute-start | bytes 224 | tf_op jit(solution)/shard_map/ppermute | solution.py:625
  36.5 6.8 %collective-permute-start.11 = (bf16[128,1024]{1,0:T(8,128)(2,1)S(1)}, bf16[128,1024]{1,0:T(8,128)(2,1)S(1)}, u32[]{:S(2)}, u32[]{:S(2)}) collective-permute-start(bf16[128,1024]{1,0:T(8,128)(2,1)S(1)} %get-tuple-element.54.refs_5_), channel_id=1, source_target_pairs={{0,4},{1,5},{2,6},{3,7},{4,8},{5,9},{6,10},{7,11},{8,12},{9,13},{1... | collective-permute-start | bytes 786440 | tf_op jit(solution)/shard_map/ppermute | solution.py:629
  36.6 12.3 %collective-permute-start.12 = (bf16[128,1024]{1,0:T(8,128)(2,1)S(1)}, bf16[128,1024]{1,0:T(8,128)(2,1)S(1)}, u32[]{:S(2)}, u32[]{:S(2)}) collective-permute-start(bf16[128,1024]{1,0:T(8,128)(2,1)S(1)} %get-tuple-element.55.refs_6_), channel_id=1, source_target_pairs={{0,4},{1,5},{2,6},{3,7},{4,8},{5,9},{6,10},{7,11},{8,12},{9,13},{1... | collective-permute-start | bytes 786440 | tf_op jit(solution)/shard_map/ppermute | solution.py:629
  37.9 16.7 %collective-permute-start.8 = (bf16[256,512]{1,0:T(8,128)(2,1)S(1)}, bf16[256,512]{1,0:T(8,128)(2,1)S(1)}, u32[]{:S(2)}, u32[]{:S(2)}) collective-permute-start(bf16[256,512]{1,0:T(8,128)(2,1)S(1)} %get-tuple-element.50.refs_3_), channel_id=1, source_target_pairs={{0,2},{1,3},{2,0},{3,1},{4,6},{5,7},{6,4},{7,5},{8,10},{9,11},{10,... | collective-permute-start | bytes 786440 | tf_op jit(solution)/shard_map/ppermute | solution.py:625
  43.3 11.8 %collective-permute-start.15 = (bf16[128,1024]{1,0:T(8,128)(2,1)S(1)}, bf16[128,1024]{1,0:T(8,128)(2,1)S(1)}, u32[]{:S(2)}, u32[]{:S(2)}) collective-permute-start(bf16[128,1024]{1,0:T(8,128)(2,1)S(1)} %collective-permute-done.11.refs_9_), channel_id=1, source_target_pairs={{0,4},{1,5},{2,6},{3,7},{4,8},{5,9},{6,10},{7,11},{8,12},{9,13},{1... | collective-permute-start | bytes 786440 | tf_op jit(solution)/shard_map/ppermute | solution.py:629
  48.9 11.2 %collective-permute-start.16 = (bf16[128,1024]{1,0:T(8,128)(2,1)S(1)}, bf16[128,1024]{1,0:T(8,128)(2,1)S(1)}, u32[]{:S(2)}, u32[]{:S(2)}) collective-permute-start(bf16[128,1024]{1,0:T(8,128)(2,1)S(1)} %collective-permute-done.12.refs_10_), channel_id=1, source_target_pairs={{0,4},{1,5},{2,6},{3,7},{4,8},{5,9},{6,10},{7,11},{8,12},{9,13},{1... | collective-permute-start | bytes 786440 | tf_op jit(solution)/shard_map/ppermute | solution.py:629
  50.8 11.2 %collective-permute-start.9 = (bf16[128,1024]{1,0:T(8,128)(2,1)S(1)}, bf16[128,1024]{1,0:T(8,128)(2,1)S(1)}, u32[]{:S(2)}, u32[]{:S(2)}) collective-permute-start(bf16[128,1024]{1,0:T(8,128)(2,1)S(1)} %get-tuple-element.54.refs_5_), channel_id=1, source_target_pairs={{0,1},{1,0},{2,3},{3,2},{4,5},{5,4},{6,7},{7,6},{8,9},{9,8},{10,11... | collective-permute-start | bytes 786440 | tf_op jit(solution)/shard_map/ppermute | solution.py:625
  54.6 11.2 %collective-permute-start.10 = (bf16[128,1024]{1,0:T(8,128)(2,1)S(1)}, bf16[128,1024]{1,0:T(8,128)(2,1)S(1)}, u32[]{:S(2)}, u32[]{:S(2)}) collective-permute-start(bf16[128,1024]{1,0:T(8,128)(2,1)S(1)} %get-tuple-element.55.refs_6_), channel_id=1, source_target_pairs={{0,1},{1,0},{2,3},{3,2},{4,5},{5,4},{6,7},{7,6},{8,9},{9,8},{10,11... | collective-permute-start | bytes 786440 | tf_op jit(solution)/shard_map/ppermute | solution.py:625
  54.6 11.3 %collective-permute-start.13 = (bf16[128,1024]{1,0:T(8,128)(2,1)S(1)}, bf16[128,1024]{1,0:T(8,128)(2,1)S(1)}, u32[]{:S(2)}, u32[]{:S(2)}) collective-permute-start(bf16[128,1024]{1,0:T(8,128)(2,1)S(1)} %collective-permute-done.11.refs_9_), channel_id=1, source_target_pairs={{0,1},{1,0},{2,3},{3,2},{4,5},{5,4},{6,7},{7,6},{8,9},{9,8},{10,11... | collective-permute-start | bytes 786440 | tf_op jit(solution)/shard_map/ppermute | solution.py:625
  55.1 11.2 %collective-permute-start.19 = (bf16[128,1024]{1,0:T(8,128)(2,1)S(1)}, bf16[128,1024]{1,0:T(8,128)(2,1)S(1)}, u32[]{:S(2)}, u32[]{:S(2)}) collective-permute-start(bf16[128,1024]{1,0:T(8,128)(2,1)S(1)} %collective-permute-done.15.refs_13_), channel_id=1, source_target_pairs={{0,4},{1,5},{2,6},{3,7},{4,8},{5,9},{6,10},{7,11},{8,12},{9,13},{1... | collective-permute-start | bytes 786440 | tf_op jit(solution)/shard_map/ppermute | solution.py:629
  60.1 11.2 %collective-permute-start.20 = (bf16[128,1024]{1,0:T(8,128)(2,1)S(1)}, bf16[128,1024]{1,0:T(8,128)(2,1)S(1)}, u32[]{:S(2)}, u32[]{:S(2)}) collective-permute-start(bf16[128,1024]{1,0:T(8,128)(2,1)S(1)} %collective-permute-done.16.refs_14_), channel_id=1, source_target_pairs={{0,4},{1,5},{2,6},{3,7},{4,8},{5,9},{6,10},{7,11},{8,12},{9,13},{1... | collective-permute-start | bytes 786440 | tf_op jit(solution)/shard_map/ppermute | solution.py:629
  62.0 11.3 %collective-permute-start.14 = (bf16[128,1024]{1,0:T(8,128)(2,1)S(1)}, bf16[128,1024]{1,0:T(8,128)(2,1)S(1)}, u32[]{:S(2)}, u32[]{:S(2)}) collective-permute-start(bf16[128,1024]{1,0:T(8,128)(2,1)S(1)} %collective-permute-done.12.refs_10_), channel_id=1, source_target_pairs={{0,1},{1,0},{2,3},{3,2},{4,5},{5,4},{6,7},{7,6},{8,9},{9,8},{10,11... | collective-permute-start | bytes 786440 | tf_op jit(solution)/shard_map/ppermute | solution.py:625
  65.8 7.5 %collective-permute-start.17 = (bf16[128,1024]{1,0:T(8,128)(2,1)S(1)}, bf16[128,1024]{1,0:T(8,128)(2,1)S(1)}, u32[]{:S(2)}, u32[]{:S(2)}) collective-permute-start(bf16[128,1024]{1,0:T(8,128)(2,1)S(1)} %collective-permute-done.15.refs_13_), channel_id=1, source_target_pairs={{0,1},{1,0},{2,3},{3,2},{4,5},{5,4},{6,7},{7,6},{8,9},{9,8},{10,11... | collective-permute-start | bytes 786440 | tf_op jit(solution)/shard_map/ppermute | solution.py:625
  65.9 7.4 %collective-permute-start.18 = (bf16[128,1024]{1,0:T(8,128)(2,1)S(1)}, bf16[128,1024]{1,0:T(8,128)(2,1)S(1)}, u32[]{:S(2)}, u32[]{:S(2)}) collective-permute-start(bf16[128,1024]{1,0:T(8,128)(2,1)S(1)} %collective-permute-done.16.refs_14_), channel_id=1, source_target_pairs={{0,1},{1,0},{2,3},{3,2},{4,5},{5,4},{6,7},{7,6},{8,9},{9,8},{10,11... | collective-permute-start | bytes 786440 | tf_op jit(solution)/shard_map/ppermute | solution.py:625
  66.3 13.0 %collective-permute-start.21 = (bf16[128,1024]{1,0:T(8,128)(2,1)S(1)}, bf16[128,1024]{1,0:T(8,128)(2,1)S(1)}, u32[]{:S(2)}, u32[]{:S(2)}) collective-permute-start(bf16[128,1024]{1,0:T(8,128)(2,1)S(1)} %collective-permute-done.19.refs_7_), channel_id=1, source_target_pairs={{0,1},{1,0},{2,3},{3,2},{4,5},{5,4},{6,7},{7,6},{8,9},{9,8},{10,11... | collective-permute-start | bytes 786440 | tf_op jit(solution)/shard_map/ppermute | solution.py:625
  71.3 8.0 %collective-permute-start.22 = (bf16[128,1024]{1,0:T(8,128)(2,1)S(1)}, bf16[128,1024]{1,0:T(8,128)(2,1)S(1)}, u32[]{:S(2)}, u32[]{:S(2)}) collective-permute-start(bf16[128,1024]{1,0:T(8,128)(2,1)S(1)} %collective-permute-done.20.refs_8_), channel_id=1, source_target_pairs={{0,1},{1,0},{2,3},{3,2},{4,5},{5,4},{6,7},{7,6},{8,9},{9,8},{10,11... | collective-permute-start | bytes 786440 | tf_op jit(solution)/shard_map/ppermute | solution.py:625
  85.3 8.4 %collective-permute-start.23 = (bf16[256,512]{1,0:T(8,128)(2,1)S(1)}, bf16[256,512]{1,0:T(8,128)(2,1)S(1)}, u32[]{:S(2)}, u32[]{:S(2)}) collective-permute-start(bf16[256,512]{1,0:T(8,128)(2,1)S(1)} %get-tuple-element.60), channel_id=1, source_target_pairs={{0,2},{1,3},{2,0},{3,1},{4,6},{5,7},{6,4},{7,5},{8,10},{9,11},{10,... | collective-permute-start | bytes 786440 | tf_op jit(solution)/shard_map/ppermute | solution.py:625
  86.3 7.4 %collective-permute-start.24 = (f32[8,256]{1,0:T(8,128)S(1)}, f32[8,256]{1,0:T(8,128)S(1)}, u32[]{:S(2)}, u32[]{:S(2)}) collective-permute-start(f32[8,256]{1,0:T(8,128)S(1)} %get-tuple-element.61), channel_id=1, source_target_pairs={{0,2},{1,3},{2,0},{3,1},{4,6},{5,7},{6,4},{7,5},{8,10},{9,11},{10,... | collective-permute-start | bytes 24584 | tf_op jit(solution)/shard_map/ppermute | solution.py:625
  (13 other events, 199.5 us)

commit v3 on v2

--- a/solution.py
+++ b/solution.py
@@ -433,17 +433,55 @@
     )(inner_out, qq, *states, tokens, gain.reshape(1, d), w_mq, w_mk, w_mv)
 
 
-def attend_kernel(frames, blocks, first, last, *refs):
-    table, counts, need, q_ref, pq_ref = refs[:5]
-    refs = refs[5:]
+def list_assist(frames, reach, steps, planes, pack, table, counts, need):
+    me = lax.axis_index("tm")
+    lane = lax.rem(me, LANES)
+    plane = me // LANES
+    slots = pack.shape[1] - 1
+
+    def clear(b, _):
+        need[b] = jnp.int32(0)
+        return 0
+
+    lax.fori_loop(0, need.shape[0], clear, 0)
+    for f in range(frames):
+        counts[f] = jnp.int32(0)
+
+        def visit(i, carry, f=f):
+            frame = pack[f, i]
+            owner = frame // frames
+            distance = plane - owner // LANES
+
+            @pl.when((distance >= 1) & (distance <= reach) & (plane + steps < planes))
+            def _():
+                block = ((distance - 1) * LANES + (lax.rem(owner, LANES) ^ lane)) * frames
+                block = block + lax.rem(frame, frames)
+                n = counts[f]
+                table[f, n] = block
+                need[block] = 1
+                counts[f] = n + 1
+
+            return carry
+
+        lax.fori_loop(0, jnp.minimum(pack[f, slots], slots), visit, 0)
+
+
+def attend_kernel(frames, blocks, groups, first, last, assist, *refs):
+    if assist is None:
+        table, counts, need = refs[:3]
+        refs = refs[3:]
+    else:
+        pack, refs = refs[0], refs[1:]
+        table, counts, need = refs[-3:]
+        refs = refs[:-3]
+        list_assist(frames, *assist, pack, table, counts, need)
+    asked, refs = refs[:groups], refs[groups:]
     if not first:
         acc_in, stat_in = refs[:2]
         refs = refs[2:]
-    kv_refs = refs[:blocks]
-    refs = refs[blocks:]
+    kv_refs, refs = refs[:blocks], refs[blocks:]
     if last:
-        o_ref, po_ref, lse_ref, plse_ref = refs[:4]
-        refs = refs[4:]
+        outs, refs = refs[: 2 * groups], refs[2 * groups :]
     else:
         acc_out, stat_out = refs[:2]
         refs = refs[2:]
@@ -462,8 +500,8 @@
             copies[b].wait()
 
     scale = MD**-0.5
-    for row in range(2 * frames):
-        queries = q_ref if row < frames else pq_ref
+    for row in range(groups * frames):
+        queries = asked[row // frames]
         f = row % frames
         span = slice(f * P_SIZE, (f + 1) * P_SIZE)
         held = slice(row * P_SIZE, (row + 1) * P_SIZE)
@@ -534,7 +572,7 @@
                     stat[:, e : e + 1] = jnp.full((P_SIZE, 1), NEG, F32)
 
         if last:
-            out, stats = (o_ref, lse_ref) if row < frames else (po_ref, plse_ref)
+            out, stats = outs[2 * (row // frames) : 2 * (row // frames) + 2]
             for e in range(MH):
                 l = jnp.maximum(stat[:, MH + e : MH + e + 1], 1e-30)
                 out[span, e * MD : (e + 1) * MD] = (acc[e] / l).astype(out.dtype)
@@ -547,72 +585,86 @@
                 acc_out[held, e * MD : (e + 1) * MD] = acc[e]
 
 
-def attend(tables, q, pq, kvs, state, last):
-    rows = q.shape[0]
+def attend(lists, asked, kvs, state, last, assist=None):
+    rows = asked[0].shape[0]
     frames = rows // P_SIZE
     blocks = len(kvs)
-    slots = tables[0].shape[1]
+    groups = len(asked)
+    slots = lists[0].shape[1] - 1
     first = state is None
     state = [] if first else list(state)
+    out_shape = []
     if last:
-        out_shape = [
-            jax.ShapeDtypeStruct((rows, MC), F32),
-            jax.ShapeDtypeStruct((rows, MC), BF16),
-            jax.ShapeDtypeStruct((2 * MH, rows), F32),
-            jax.ShapeDtypeStruct((2 * MH, rows), F32),
-        ]
+        for g in range(groups):
+            stays = g == 0 and assist is None
+            out_shape += [
+                jax.ShapeDtypeStruct((rows, MC), F32 if stays else BF16),
+                jax.ShapeDtypeStruct((2 * MH, rows), F32),
+            ]
     else:
         out_shape = [
-            jax.ShapeDtypeStruct((2 * rows, MC), F32),
-            jax.ShapeDtypeStruct((2 * rows, 128), F32),
+            jax.ShapeDtypeStruct((groups * rows, MC), F32),
+            jax.ShapeDtypeStruct((groups * rows, 128), F32),
+        ]
+    scratch = [
+        pltpu.VMEM((blocks, P_SIZE, 2 * MC), BF16),
+        pltpu.VMEM((slots + 3, MH, P_SIZE, P_SIZE), F32),
+        pltpu.VMEM((MH, P_SIZE, P_SIZE), F32),
+        pltpu.VMEM((MH, P_SIZE, P_SIZE), F32),
+        pltpu.VMEM((MH, P_SIZE, MD), F32),
+        pltpu.VMEM((P_SIZE, 128), F32),
+        pltpu.SemaphoreType.DMA((blocks,)),
+    ]
+    if assist is not None:
+        scratch += [
+            pltpu.SMEM((frames, slots + 1), jnp.int32),
+            pltpu.SMEM((frames,), jnp.int32),
+            pltpu.SMEM((blocks,), jnp.int32),
         ]
     return pl.pallas_call(
-        functools.partial(attend_kernel, frames, blocks, first, last),
-        in_specs=[SMEM] * 3 + [VMEM] * (2 + len(state)) + [HBM] * blocks,
+        functools.partial(attend_kernel, frames, blocks, groups, first, last, assist),
+        in_specs=[SMEM] * len(lists) + [VMEM] * (groups + len(state)) + [HBM] * blocks,
         out_specs=[VMEM] * len(out_shape),
         out_shape=out_shape,
-        scratch_shapes=[
-            pltpu.VMEM((blocks, P_SIZE, 2 * MC), BF16),
-            pltpu.VMEM((slots + 2, MH, P_SIZE, P_SIZE), F32),
-            pltpu.VMEM((MH, P_SIZE, P_SIZE), F32),
-            pltpu.VMEM((MH, P_SIZE, P_SIZE), F32),
-            pltpu.VMEM((MH, P_SIZE, MD), F32),
-            pltpu.VMEM((P_SIZE, 128), F32),
-            pltpu.SemaphoreType.DMA((blocks,)),
-        ],
+        scratch_shapes=scratch,
         compiler_params=params(),
         cost_estimate=cost(4 * 8 * frames * P_SIZE * P_SIZE * MC, blocks * P_SIZE * MC * 4),
-        name="attend_last" if last else "attend",
-    )(*tables, q, pq, *state, *kvs)
-
-
-def output_kernel(o_ref, lse_ref, po_ref, plse_ref, hid_ref, w_ref, out_ref, mixed):
-    rows = o_ref.shape[0]
-    mine, other = lse_ref[...], plse_ref[...]
-    top = jnp.maximum(mine, other)
-    a, b = jnp.exp(mine - top), jnp.exp(other - top)
-    inv = 1.0 / (a + b)
-    both = jnp.concatenate([a * inv, b * inv, jnp.zeros((128 - 16, rows), F32)], axis=0)
-    weights = jnp.transpose(both)
+        name="assist" if assist is not None else "attend_last" if last else "attend",
+    )(*lists, *asked, *state, *kvs)
+
+
+def output_kernel(parts, *refs):
+    values, stats = refs[0 : 2 * parts : 2], refs[1 : 2 * parts : 2]
+    hid_ref, w_ref, out_ref, mixed = refs[2 * parts :]
+    rows = hid_ref.shape[0]
+    logs = [ref[...] for ref in stats]
+    top = functools.reduce(jnp.maximum, logs)
+    shares = [jnp.exp(x - top) for x in logs]
+    inv = 1.0 / functools.reduce(jnp.add, shares)
+    pad = jnp.zeros((128 - parts * 2 * MH, rows), F32)
+    weights = jnp.transpose(jnp.concatenate([x * inv for x in shares] + [pad], axis=0))
     for e in range(MH):
         cols = slice(e * MD, (e + 1) * MD)
-        value = o_ref[:, cols] * weights[:, e : e + 1]
-        value = value + po_ref[:, cols].astype(F32) * weights[:, 8 + e : 9 + e]
+        value = 0.0
+        for i, ref in enumerate(values):
+            at = i * 2 * MH + e
+            value = value + ref[:, cols].astype(F32) * weights[:, at : at + 1]
         mixed[:, cols] = value.astype(BF16)
     out_ref[...] = (hid_ref[...].astype(F32) + nn(mixed[...], w_ref[...])).astype(BF16)
 
 
-def output(o, lse, po, plse, hid, w_out):
+def output(parts, hid, w_out):
     rows, d = hid.shape
+    flat = [x for part in parts for x in part]
     return pl.pallas_call(
-        output_kernel,
-        in_specs=[VMEM] * 6,
+        functools.partial(output_kernel, len(parts)),
+        in_specs=[VMEM] * (len(flat) + 2),
         out_specs=VMEM,
         out_shape=jax.ShapeDtypeStruct((rows, d), BF16),
         scratch_shapes=[pltpu.VMEM((rows, MC), BF16)],
         compiler_params=params(),
         name="output",
-    )(o, lse, po, plse, hid, w_out)
+    )(*flat, hid, w_out)
 
 
 def on_device(
@@ -629,7 +681,8 @@
         return lax.ppermute(x, "tm", [(i, (i + step) % size) for i in range(size)])
 
     message, chunk = (ROWS + TAIL, DV), (ROWS, DV)
-    spans = ((0, planes - 1), (planes - 1, planes)) if planes > 1 else ((0, planes),)
+    steps, reach = reaches(planes)
+    spans = ((0, steps), (steps, steps + 1)) if steps else ((0, 1),)
     k, v, keep, give, pack = local(tokens, w_rk, w_rv, log_decay, mem_index, mem_count)
     core_got = flip(give, 1)
     other = flip(pack, 2)
@@ -660,24 +713,49 @@
     )
     states = (kept, flip(give, 1))
     hid, q, *kv = hidden_of(inner_out, qq, states, tokens, norm_gain, w_mq, w_mk, w_mv)
+
+    def between(x, pairs):
+        return lax.ppermute(
+            x, "tm", [(a * LANES + i, b * LANES + i) for a, b in pairs for i in range(LANES)]
+        )
+
+    def onward(x, distance):
+        pairs = [(p, p + 1) for p in range(distance - 1, planes - 1)]
+        return between(x, pairs + [(p, p) for p in range(distance - 1)] + [(planes - 1, distance - 1)])
+
     partner_q = flip(q, 2)
-    held = []
-    for distance in range(planes):
+    held, across = [], []
+    for distance in range(steps + 1):
         if distance:
-            moved = []
-            for x in kv:
-                moved.append(up(x, 1))
-            kv = moved
-        near = []
-        for x in kv:
-            near.append(flip(x, 1))
+            kv = [onward(x, distance) for x in kv]
+        near = [flip(x, 1) for x in kv]
         held.append(kv + near)
+        if 1 <= distance <= reach:
+            column = [flip(x, 2) for x in kv]
+            both = [flip(x, 1) for x in column]
+            across += kv + near + column + both
+    parts = []
+    if reach:
+        helped = [(p, p + steps) for p in range(1, planes - steps)]
+        down = [(b, a) for a, b in helped]
+        rest = [(p, p) for p in range(planes) if all(p not in pair for pair in helped)]
+        far_q = between(q, down)
+        far_pack = between(pack, down)
+        far = attend([far_pack], [far_q], across, None, True, (reach, steps, planes))
+        whole = helped + down + rest
+        parts = [[between(x, whole) for x in far]]
     state = None
     for (low, high), table in zip(spans, tables):
         blocks = [x for group in held[low:high] for x in group]
-        state = attend(table, q, partner_q, blocks, state, high == planes)
-    o, po, lse, plse = state
-    return output(o, lse, flip(po, 2), flip(plse, 2), hid, w_out)
+        state = attend(table, [q, partner_q], blocks, state, high == steps + 1)
+    o, lse, po, plse = state
+    back = [flip(po, 2), flip(plse, 2)]
+    return output([[o, lse], back] + parts, hid, w_out)
+
+
+def reaches(planes):
+    steps = planes // 2
+    return steps, planes - 1 - steps
 
 
 def solution(mesh):

time: 95.7 us -> 101 us (1.055)
  the two profiles are of different devices: /device:TPU:27 before, /device:TPU:10 now
where the time goes in v3:
time: 101 us
  starting transfers between devices  36.5 us (36%)
  waiting for transfers between devices  36 us (36%)
  Pallas kernels  23.4 us (23%)
  local copies, waits for them, and re-layouts  4.5 us (4%)
    ppermute x8, starting transfers between devices, between(): lax.ppermute(x, 'tm', [(a * LANES + i, b * LANES + i) for a, b in pairs f...  22 us
    ppermute x18, waiting for transfers between devices, flip(): return lax.ppermute(x, 'tm', [(i, i ^ bits) for i in range(size)])  19.4 us
    ppermute x8, waiting for transfers between devices, between(): lax.ppermute(x, 'tm', [(a * LANES + i, b * LANES + i) for a, b in pairs f...  12.8 us
    pallas_call x3, Pallas kernels, attend(): pl.pallas_call(functools.partial(attend_kernel, frames, blocks, groups, f...  11.8 us
    ppermute x18, starting transfers between devices, flip(): return lax.ppermute(x, 'tm', [(i, i ^ bits) for i in range(size)])  9.85 us
    ppermute x3, starting transfers between devices, up(): return lax.ppermute(x, 'tm', [(i, (i + step) % size) for i in range(size)])  4.67 us
    unnamed x24, local copies, waits for them, and re-layouts  4.5 us
    pallas_call x1, Pallas kernels, local(): pl.pallas_call(local_kernel, in_specs=[HBM] * 6, out_specs=[VMEM] * 4 + [...  3.93 us
  transfers between devices with their start and end apart: 29, of which 13 were waited for; matrix products, arithmetic and copies ran while one was open for 0% of the time, Pallas kernels for 15%

profile of v3, /device:TPU:10, one launch (start us, length us, event | category | flops | bytes accessed | tf_op | source)
XLA Modules:
  0.0 100.7 jit_solution(13054729199040951359)
XLA Ops:
  0.0 3.9 %local.1 = (bf16[256,512]{1,0:T(8,128)(2,1)}, bf16[256,1024]{1,0:T(8,128)(2,1)}, bf16[2,272,128]{2,1,0:T(8,128)(2,1)}, bf16[2,272,128]{2,1,0:T(8,128)(2,1)}, s32[2,9]{1,0:T(2,128)}) custom-call(bf16[256,1024]{1,0:T(8,128)(2,1)} %refs_4_.1, f32[8,256]{1,0:T(8,128)} %refs_1_.1, bf16[1024,512]{1,0:T(8,128)(2,1)} %wk_in.1, bf16[1024,1024]{1,0:T(8,128)(2,1)} %wv_in.1, ...), custom_call_target="tpu_custom_call" | custom-call | tf_op jit(solution)/shard_map/local/pallas_call | solution.py:174
  8.2 2.8 %collective-permute-done.2.got.refs_1_ = bf16[272,128]{1,0:T(8,128)(2,1)S(1)} collective-permute-done((bf16[272,128]{1,0:T(8,128)(2,1)S(1)}, bf16[272,128]{1,0:T(8,128)(2,1)S(1)}, u32[]{:S(2)}, u32[]{:S(2)}) %collective-permute-start.2) | collective-permute-done | bytes 69664 | tf_op jit(solution)/shard_map/ppermute | solution.py:677
  11.0 1.6 %collective-permute-start.3 = (bf16[272,128]{1,0:T(8,128)(2,1)S(1)}, bf16[272,128]{1,0:T(8,128)(2,1)S(1)}, u32[]{:S(2)}, u32[]{:S(2)}) collective-permute-start(bf16[272,128]{1,0:T(8,128)(2,1)S(1)} %shard_map.119), channel_id=1, source_target_pairs={{0,4},{1,5},{2,6},{3,7},{4,8},{5,9},{6,10},{7,11},{8,12},{9,13},{1... | collective-permute-start | bytes 208904 | tf_op jit(solution)/shard_map/ppermute | solution.py:681
  13.9 1.8 %collective-permute-start.5 = (bf16[272,128]{1,0:T(8,128)(2,1)S(1)}, bf16[272,128]{1,0:T(8,128)(2,1)S(1)}, u32[]{:S(2)}, u32[]{:S(2)}) collective-permute-start(bf16[272,128]{1,0:T(8,128)(2,1)S(1)} %shard_map.119), channel_id=1, source_target_pairs={{0,12},{1,13},{2,14},{3,15},{4,0},{5,1},{6,2},{7,3},{8,4},{9,5},{1... | collective-permute-start | bytes 208904 | tf_op jit(solution)/shard_map/ppermute | solution.py:681
  15.8 2.1 %collective-permute-done.4.refs_3_ = bf16[272,128]{1,0:T(8,128)(2,1)S(1)} collective-permute-done((bf16[272,128]{1,0:T(8,128)(2,1)S(1)}, bf16[272,128]{1,0:T(8,128)(2,1)S(1)}, u32[]{:S(2)}, u32[]{:S(2)}) %collective-permute-start.4) | collective-permute-done | bytes 69664 | tf_op jit(solution)/shard_map/ppermute | solution.py:681
  17.9 1.6 %collective-permute-done.5.refs_4_ = bf16[272,128]{1,0:T(8,128)(2,1)S(1)} collective-permute-done((bf16[272,128]{1,0:T(8,128)(2,1)S(1)}, bf16[272,128]{1,0:T(8,128)(2,1)S(1)}, u32[]{:S(2)}, u32[]{:S(2)}) %collective-permute-start.5) | collective-permute-done | bytes 69664 | tf_op jit(solution)/shard_map/ppermute | solution.py:681
  21.2 2.7 %collective-permute-done.6.got = bf16[256,128]{1,0:T(8,128)(2,1)S(1)} collective-permute-done((bf16[256,128]{1,0:T(8,128)(2,1)S(1)}, bf16[256,128]{1,0:T(8,128)(2,1)S(1)}, u32[]{:S(2)}, u32[]{:S(2)}) %collective-permute-start.6) | collective-permute-done | bytes 65568 | tf_op jit(solution)/shard_map/ppermute | solution.py:677
  25.1 1.6 %collective-permute-start = (s32[2,9]{1,0:T(2,128)}, s32[2,9]{1,0:T(2,128)S(1)}, u32[]{:S(2)}, u32[]{:S(2)}) collective-permute-start(s32[2,9]{1,0:T(2,128)} %get-tuple-element.38.refs_4_), channel_id=1, source_target_pairs={{0,2},{1,3},{2,0},{3,1},{4,6},{5,7},{6,4},{7,5},{8,10},{9,11},{10,... | collective-permute-start | bytes 224 | tf_op jit(solution)/shard_map/ppermute | solution.py:677
  26.7 2.3 %collective-permute-done.refs_5_ = s32[2,9]{1,0:T(2,128)S(1)} collective-permute-done((s32[2,9]{1,0:T(2,128)}, s32[2,9]{1,0:T(2,128)S(1)}, u32[]{:S(2)}, u32[]{:S(2)}) %collective-permute-start) | collective-permute-done | bytes 104 | tf_op jit(solution)/shard_map/ppermute | solution.py:677
  31.6 3.2 %inner.1 = (f32[256,1024]{1,0:T(8,128)S(1)}, bf16[256,1024]{1,0:T(8,128)(2,1)S(1)}, s32[4,9]{1,0:T(4,128)S(1)}, s32[4]{0:T(128)S(1)}, s32[8]{0:T(128)S(1)}, /*in...) custom-call(bf16[256,1024]{1,0:T(8,128)(2,1)S(1)} %copy-done, f32[8,256]{1,0:T(8,128)S(1)} %copy-done.9, ...), custom_call_target="tpu_custom_call" | custom-call | flops 268435456 | bytes 8388608 | tf_op jit(solution)/shard_map/inner/pallas_call | solution.py:294
  34.8 2.2 %hidden.1 = (bf16[256,1024]{1,0:T(8,128)(2,1)S(1)}, bf16[256,512]{1,0:T(8,128)(2,1)S(1)}, bf16[128,1024]{1,0:T(8,128)(2,1)S(1)}, bf16[128,1024]{1,0:T(8,128)(2,1)S(1)}) custom-call(f32[256,1024]{1,0:T(8,128)S(1)} %get-tuple-element.42.refs_0_, bf16[256,1024]{1,0:T(8,128)(2,1)S(1)} %get-tuple-element.43.refs_1_, ...), custom_call_target="tpu_custom_call" | custom-call | tf_op jit(solution)/shard_map/hidden/pallas_call | solution.py:419
  37.3 2.7 %collective-permute-start.12 = (bf16[128,1024]{1,0:T(8,128)(2,1)S(1)}, bf16[128,1024]{1,0:T(8,128)(2,1)S(1)}, u32[]{:S(2)}, u32[]{:S(2)}) collective-permute-start(bf16[128,1024]{1,0:T(8,128)(2,1)S(1)} %get-tuple-element.57.refs_6_), channel_id=1, source_target_pairs={{0,4},{1,5},{2,6},{3,7},{4,8},{5,9},{6,10},{7,11},{8,12},{9,13},{1... | collective-permute-start | bytes 786440 | tf_op jit(solution)/shard_map/ppermute | solution.py:718
  42.9 8.2 %collective-permute-done.21.refs_0_ = s32[2,9]{1,0:T(2,128)S(1)} collective-permute-done((s32[2,9]{1,0:T(2,128)S(1)}, s32[2,9]{1,0:T(2,128)S(1)}, u32[]{:S(2)}, u32[]{:S(2)}) %collective-permute-start.21) | collective-permute-done | bytes 104 | tf_op jit(solution)/shard_map/ppermute | solution.py:718
  53.6 1.9 %collective-permute-start.15 = (bf16[128,1024]{1,0:T(8,128)(2,1)S(1)}, bf16[128,1024]{1,0:T(8,128)(2,1)S(1)}, u32[]{:S(2)}, u32[]{:S(2)}) collective-permute-start(bf16[128,1024]{1,0:T(8,128)(2,1)S(1)} %collective-permute-done.11.refs_9_.refs_2_), channel_id=1, source_target_pairs={{4,8},{5,9},{6,10},{7,11},{8,12},{9,13},{10,14},{11,15},{0,0},{1,1... | collective-permute-start | bytes 786440 | tf_op jit(solution)/shard_map/ppermute | solution.py:718
  55.6 4.7 %collective-permute-done.23.refs_6_ = bf16[128,1024]{1,0:T(8,128)(2,1)S(1)} collective-permute-done((bf16[128,1024]{1,0:T(8,128)(2,1)S(1)}, bf16[128,1024]{1,0:T(8,128)(2,1)S(1)}, u32[]{:S(2)}, u32[]{:S(2)}) %collective-permute-start.23) | collective-permute-done | bytes 262176 | tf_op jit(solution)/shard_map/ppermute | solution.py:677
  60.3 1.9 %collective-permute-start.16 = (bf16[128,1024]{1,0:T(8,128)(2,1)S(1)}, bf16[128,1024]{1,0:T(8,128)(2,1)S(1)}, u32[]{:S(2)}, u32[]{:S(2)}) collective-permute-start(bf16[128,1024]{1,0:T(8,128)(2,1)S(1)} %collective-permute-done.12.refs_10_.refs_3_), channel_id=1, source_target_pairs={{4,8},{5,9},{6,10},{7,11},{8,12},{9,13},{10,14},{11,15},{0,0},{1,1... | collective-permute-start | bytes 786440 | tf_op jit(solution)/shard_map/ppermute | solution.py:718
  62.2 3.2 %collective-permute-done.24.refs_7_ = bf16[128,1024]{1,0:T(8,128)(2,1)S(1)} collective-permute-done((bf16[128,1024]{1,0:T(8,128)(2,1)S(1)}, bf16[128,1024]{1,0:T(8,128)(2,1)S(1)}, u32[]{:S(2)}, u32[]{:S(2)}) %collective-permute-start.24) | collective-permute-done | bytes 262176 | tf_op jit(solution)/shard_map/ppermute | solution.py:677
  67.4 3.1 %collective-permute-done.16.refs_8_ = bf16[128,1024]{1,0:T(8,128)(2,1)S(1)} collective-permute-done((bf16[128,1024]{1,0:T(8,128)(2,1)S(1)}, bf16[128,1024]{1,0:T(8,128)(2,1)S(1)}, u32[]{:S(2)}, u32[]{:S(2)}) %collective-permute-start.16) | collective-permute-done | bytes 262176 | tf_op jit(solution)/shard_map/ppermute | solution.py:718
  70.5 6.9 %attend.1 = (f32[512,512]{1,0:T(8,128)S(1)}, f32[512,128]{1,0:T(8,128)S(1)}) custom-call(s32[4,9]{1,0:T(4,128)S(1)} %get-tuple-element.53.refs_0_, s32[4]{0:T(128)S(1)} %get-tuple-element.54.refs_1_, s32[8]{0:T(128)S(1)} %get-tuple-element.55.refs_2_, bf16[256,512]{1,0:T(8,128)(2,1)S(1)} %get-tuple-element.52.refs_3_, ...), custom_call_target="tpu_custom_call" | custom-call | flops 536870912 | bytes 2097152 | tf_op jit(solution)/shard_map/attend/pallas_call | solution.py:624
  77.5 3.3 %assist.1 = (bf16[256,512]{1,0:T(8,128)(2,1)S(1)}, f32[8,256]{1,0:T(8,128)S(1)}) custom-call(s32[2,9]{1,0:T(2,128)S(1)} %collective-permute-done.21.refs_0_, bf16[256,512]{1,0:T(8,128)(2,1)S(1)} %collective-permute-done.22.refs_1_, bf16[128,1024]{1,0:T(8,128)(2,1)S(1)} %collective-permute-done.11.refs_9_.refs_2_, ...), custom_call_target="tpu_custom_call" | custom-call | flops 536870912 | bytes 2097152 | tf_op jit(solution)/shard_map/assist/pallas_call | solution.py:624
  80.8 1.9 %collective-permute-start.27 = (bf16[256,512]{1,0:T(8,128)(2,1)S(1)}, bf16[256,512]{1,0:T(8,128)(2,1)S(1)}, u32[]{:S(2)}, u32[]{:S(2)}) collective-permute-start(bf16[256,512]{1,0:T(8,128)(2,1)S(1)} %get-tuple-element.64), channel_id=1, source_target_pairs={{4,12},{5,13},{6,14},{7,15},{12,4},{13,5},{14,6},{15,7},{0,0},{1,1... | collective-permute-start | bytes 786440 | tf_op jit(solution)/shard_map/ppermute | solution.py:718
  84.5 10.6 %collective-permute-start.28 = (f32[8,256]{1,0:T(8,128)S(1)}, f32[8,256]{1,0:T(8,128)S(1)}, u32[]{:S(2)}, u32[]{:S(2)}) collective-permute-start(f32[8,256]{1,0:T(8,128)S(1)} %get-tuple-element.65), channel_id=1, source_target_pairs={{4,12},{5,13},{6,14},{7,15},{12,4},{13,5},{14,6},{15,7},{0,0},{1,1... | collective-permute-start | bytes 24584 | tf_op jit(solution)/shard_map/ppermute | solution.py:718
  96.7 2.1 %collective-permute-done.20.refs_3_ = f32[8,256]{1,0:T(8,128)S(1)} collective-permute-done((f32[8,256]{1,0:T(8,128)S(1)}, f32[8,256]{1,0:T(8,128)S(1)}, u32[]{:S(2)}, u32[]{:S(2)}) %collective-permute-start.20) | collective-permute-done | bytes 8224 | tf_op jit(solution)/shard_map/ppermute | solution.py:677
  98.8 1.9 %output.1 = bf16[256,1024]{1,0:T(8,128)(2,1)} custom-call(f32[256,512]{1,0:T(8,128)S(1)} %get-tuple-element.60.refs_0_, f32[8,256]{1,0:T(8,128)S(1)} %get-tuple-element.61.refs_1_, bf16[256,512]{1,0:T(8,128)(2,1)S(1)} %collective-permute-done.19.refs_2_, f32[8,256]{1,0:T(8,128)S(1)} %collective-permute-done.20.refs_3_, ...), custom_call_target="tpu_custom_call" | custom-call | tf_op jit(solution)/shard_map/output/pallas_call | solution.py:659
  (69 shorter events, 22.0 us)
Async XLA Ops:
  6.6 4.4 %collective-permute-start.2 = (bf16[272,128]{1,0:T(8,128)(2,1)S(1)}, bf16[272,128]{1,0:T(8,128)(2,1)S(1)}, u32[]{:S(2)}, u32[]{:S(2)}) collective-permute-start(bf16[272,128]{1,0:T(8,128)(2,1)S(1)} %get-tuple-element.47), channel_id=1, source_target_pairs={{0,2},{1,3},{2,0},{3,1},{4,6},{5,7},{6,4},{7,5},{8,10},{9,11},{10,... | collective-permute-start | bytes 208904 | tf_op jit(solution)/shard_map/ppermute | solution.py:677
  11.0 4.8 %collective-permute-start.3 = (bf16[272,128]{1,0:T(8,128)(2,1)S(1)}, bf16[272,128]{1,0:T(8,128)(2,1)S(1)}, u32[]{:S(2)}, u32[]{:S(2)}) collective-permute-start(bf16[272,128]{1,0:T(8,128)(2,1)S(1)} %shard_map.119), channel_id=1, source_target_pairs={{0,4},{1,5},{2,6},{3,7},{4,8},{5,9},{6,10},{7,11},{8,12},{9,13},{1... | collective-permute-start | bytes 208904 | tf_op jit(solution)/shard_map/ppermute | solution.py:681
  12.7 5.2 %collective-permute-start.4 = (bf16[272,128]{1,0:T(8,128)(2,1)S(1)}, bf16[272,128]{1,0:T(8,128)(2,1)S(1)}, u32[]{:S(2)}, u32[]{:S(2)}) collective-permute-start(bf16[272,128]{1,0:T(8,128)(2,1)S(1)} %shard_map.119), channel_id=1, source_target_pairs={{0,8},{1,9},{2,10},{3,11},{4,12},{5,13},{6,14},{7,15},{8,0},{9,1},... | collective-permute-start | bytes 208904 | tf_op jit(solution)/shard_map/ppermute | solution.py:681
  13.9 5.6 %collective-permute-start.5 = (bf16[272,128]{1,0:T(8,128)(2,1)S(1)}, bf16[272,128]{1,0:T(8,128)(2,1)S(1)}, u32[]{:S(2)}, u32[]{:S(2)}) collective-permute-start(bf16[272,128]{1,0:T(8,128)(2,1)S(1)} %shard_map.119), channel_id=1, source_target_pairs={{0,12},{1,13},{2,14},{3,15},{4,0},{5,1},{6,2},{7,3},{8,4},{9,5},{1... | collective-permute-start | bytes 208904 | tf_op jit(solution)/shard_map/ppermute | solution.py:681
  25.0 9.8 %collective-permute-start.7 = (bf16[2,256,128]{2,1,0:T(8,128)(2,1)S(1)}, bf16[2,256,128]{2,1,0:T(8,128)(2,1)S(1)}, u32[]{:S(2)}, u32[]{:S(2)}) collective-permute-start(bf16[2,256,128]{2,1,0:T(8,128)(2,1)S(1)} %get-tuple-element.51), channel_id=1, source_target_pairs={{0,1},{1,0},{2,3},{3,2},{4,5},{5,4},{6,7},{7,6},{8,9},{9,8},{10,11... | collective-permute-start | bytes 393224 | tf_op jit(solution)/shard_map/ppermute | solution.py:677
  37.0 14.1 %collective-permute-start.11 = (bf16[128,1024]{1,0:T(8,128)(2,1)S(1)}, bf16[128,1024]{1,0:T(8,128)(2,1)S(1)}, u32[]{:S(2)}, u32[]{:S(2)}) collective-permute-start(bf16[128,1024]{1,0:T(8,128)(2,1)S(1)} %get-tuple-element.56.refs_5_), channel_id=1, source_target_pairs={{0,4},{1,5},{2,6},{3,7},{4,8},{5,9},{6,10},{7,11},{8,12},{9,13},{1... | collective-permute-start | bytes 786440 | tf_op jit(solution)/shard_map/ppermute | solution.py:718
  37.3 15.3 %collective-permute-start.12 = (bf16[128,1024]{1,0:T(8,128)(2,1)S(1)}, bf16[128,1024]{1,0:T(8,128)(2,1)S(1)}, u32[]{:S(2)}, u32[]{:S(2)}) collective-permute-start(bf16[128,1024]{1,0:T(8,128)(2,1)S(1)} %get-tuple-element.57.refs_6_), channel_id=1, source_target_pairs={{0,4},{1,5},{2,6},{3,7},{4,8},{5,9},{6,10},{7,11},{8,12},{9,13},{1... | collective-permute-start | bytes 786440 | tf_op jit(solution)/shard_map/ppermute | solution.py:718
  40.1 13.1 %collective-permute-start.10 = (bf16[128,1024]{1,0:T(8,128)(2,1)S(1)}, bf16[128,1024]{1,0:T(8,128)(2,1)S(1)}, u32[]{:S(2)}, u32[]{:S(2)}) collective-permute-start(bf16[128,1024]{1,0:T(8,128)(2,1)S(1)} %get-tuple-element.57.refs_6_), channel_id=1, source_target_pairs={{0,1},{1,0},{2,3},{3,2},{4,5},{5,4},{6,7},{7,6},{8,9},{9,8},{10,11... | collective-permute-start | bytes 786440 | tf_op jit(solution)/shard_map/ppermute | solution.py:677
  40.1 13.1 %collective-permute-start.8 = (bf16[256,512]{1,0:T(8,128)(2,1)S(1)}, bf16[256,512]{1,0:T(8,128)(2,1)S(1)}, u32[]{:S(2)}, u32[]{:S(2)}) collective-permute-start(bf16[256,512]{1,0:T(8,128)(2,1)S(1)} %get-tuple-element.52.refs_3_), channel_id=1, source_target_pairs={{0,2},{1,3},{2,0},{3,1},{4,6},{5,7},{6,4},{7,5},{8,10},{9,11},{10,... | collective-permute-start | bytes 786440 | tf_op jit(solution)/shard_map/ppermute | solution.py:677
  41.6 9.5 %collective-permute-start.21 = (s32[2,9]{1,0:T(2,128)S(1)}, s32[2,9]{1,0:T(2,128)S(1)}, u32[]{:S(2)}, u32[]{:S(2)}) collective-permute-start(s32[2,9]{1,0:T(2,128)S(1)} %copy-done.11), channel_id=1, source_target_pairs={{12,4},{13,5},{14,6},{15,7},{28,20},{29,21},{30,22},{31,23}} | collective-permute-start | bytes 224 | tf_op jit(solution)/shard_map/ppermute | solution.py:718
  51.1 9.2 %collective-permute-start.23 = (bf16[128,1024]{1,0:T(8,128)(2,1)S(1)}, bf16[128,1024]{1,0:T(8,128)(2,1)S(1)}, u32[]{:S(2)}, u32[]{:S(2)}) collective-permute-start(bf16[128,1024]{1,0:T(8,128)(2,1)S(1)} %collective-permute-done.11.refs_9_.refs_2_), channel_id=1, source_target_pairs={{0,2},{1,3},{2,0},{3,1},{4,6},{5,7},{6,4},{7,5},{8,10},{9,11},{10,... | collective-permute-start | bytes 786440 | tf_op jit(solution)/shard_map/ppermute | solution.py:677
  52.6 12.8 %collective-permute-start.24 = (bf16[128,1024]{1,0:T(8,128)(2,1)S(1)}, bf16[128,1024]{1,0:T(8,128)(2,1)S(1)}, u32[]{:S(2)}, u32[]{:S(2)}) collective-permute-start(bf16[128,1024]{1,0:T(8,128)(2,1)S(1)} %collective-permute-done.12.refs_10_.refs_3_), channel_id=1, source_target_pairs={{0,2},{1,3},{2,0},{3,1},{4,6},{5,7},{6,4},{7,5},{8,10},{9,11},{10,... | collective-permute-start | bytes 786440 | tf_op jit(solution)/shard_map/ppermute | solution.py:677
  53.1 13.6 %collective-permute-start.13 = (bf16[128,1024]{1,0:T(8,128)(2,1)S(1)}, bf16[128,1024]{1,0:T(8,128)(2,1)S(1)}, u32[]{:S(2)}, u32[]{:S(2)}) collective-permute-start(bf16[128,1024]{1,0:T(8,128)(2,1)S(1)} %collective-permute-done.11.refs_9_.refs_2_), channel_id=1, source_target_pairs={{0,1},{1,0},{2,3},{3,2},{4,5},{5,4},{6,7},{7,6},{8,9},{9,8},{10,11... | collective-permute-start | bytes 786440 | tf_op jit(solution)/shard_map/ppermute | solution.py:677
  53.1 13.7 %collective-permute-start.14 = (bf16[128,1024]{1,0:T(8,128)(2,1)S(1)}, bf16[128,1024]{1,0:T(8,128)(2,1)S(1)}, u32[]{:S(2)}, u32[]{:S(2)}) collective-permute-start(bf16[128,1024]{1,0:T(8,128)(2,1)S(1)} %collective-permute-done.12.refs_10_.refs_3_), channel_id=1, source_target_pairs={{0,1},{1,0},{2,3},{3,2},{4,5},{5,4},{6,7},{7,6},{8,9},{9,8},{10,11... | collective-permute-start | bytes 786440 | tf_op jit(solution)/shard_map/ppermute | solution.py:677
  53.6 13.7 %collective-permute-start.15 = (bf16[128,1024]{1,0:T(8,128)(2,1)S(1)}, bf16[128,1024]{1,0:T(8,128)(2,1)S(1)}, u32[]{:S(2)}, u32[]{:S(2)}) collective-permute-start(bf16[128,1024]{1,0:T(8,128)(2,1)S(1)} %collective-permute-done.11.refs_9_.refs_2_), channel_id=1, source_target_pairs={{4,8},{5,9},{6,10},{7,11},{8,12},{9,13},{10,14},{11,15},{0,0},{1,1... | collective-permute-start | bytes 786440 | tf_op jit(solution)/shard_map/ppermute | solution.py:718
  60.3 10.2 %collective-permute-start.16 = (bf16[128,1024]{1,0:T(8,128)(2,1)S(1)}, bf16[128,1024]{1,0:T(8,128)(2,1)S(1)}, u32[]{:S(2)}, u32[]{:S(2)}) collective-permute-start(bf16[128,1024]{1,0:T(8,128)(2,1)S(1)} %collective-permute-done.12.refs_10_.refs_3_), channel_id=1, source_target_pairs={{4,8},{5,9},{6,10},{7,11},{8,12},{9,13},{10,14},{11,15},{0,0},{1,1... | collective-permute-start | bytes 786440 | tf_op jit(solution)/shard_map/ppermute | solution.py:718
  65.4 12.0 %collective-permute-start.22 = (bf16[256,512]{1,0:T(8,128)(2,1)S(1)}, bf16[256,512]{1,0:T(8,128)(2,1)S(1)}, u32[]{:S(2)}, u32[]{:S(2)}) collective-permute-start(bf16[256,512]{1,0:T(8,128)(2,1)S(1)} %get-tuple-element.52.refs_3_), channel_id=1, source_target_pairs={{12,4},{13,5},{14,6},{15,7},{28,20},{29,21},{30,22},{31,23}} | collective-permute-start | bytes 786440 | tf_op jit(solution)/shard_map/ppermute | solution.py:718
  66.7 10.7 %collective-permute-start.25 = (bf16[128,1024]{1,0:T(8,128)(2,1)S(1)}, bf16[128,1024]{1,0:T(8,128)(2,1)S(1)}, u32[]{:S(2)}, u32[]{:S(2)}) collective-permute-start(bf16[128,1024]{1,0:T(8,128)(2,1)S(1)} %collective-permute-done.23.refs_6_), channel_id=1, source_target_pairs={{0,1},{1,0},{2,3},{3,2},{4,5},{5,4},{6,7},{7,6},{8,9},{9,8},{10,11... | collective-permute-start | bytes 786440 | tf_op jit(solution)/shard_map/ppermute | solution.py:677
  66.8 10.6 %collective-permute-start.26 = (bf16[128,1024]{1,0:T(8,128)(2,1)S(1)}, bf16[128,1024]{1,0:T(8,128)(2,1)S(1)}, u32[]{:S(2)}, u32[]{:S(2)}) collective-permute-start(bf16[128,1024]{1,0:T(8,128)(2,1)S(1)} %collective-permute-done.24.refs_7_), channel_id=1, source_target_pairs={{0,1},{1,0},{2,3},{3,2},{4,5},{5,4},{6,7},{7,6},{8,9},{9,8},{10,11... | collective-permute-start | bytes 786440 | tf_op jit(solution)/shard_map/ppermute | solution.py:677
  67.3 15.4 %collective-permute-start.17 = (bf16[128,1024]{1,0:T(8,128)(2,1)S(1)}, bf16[128,1024]{1,0:T(8,128)(2,1)S(1)}, u32[]{:S(2)}, u32[]{:S(2)}) collective-permute-start(bf16[128,1024]{1,0:T(8,128)(2,1)S(1)} %collective-permute-done.15.refs_7_), channel_id=1, source_target_pairs={{0,1},{1,0},{2,3},{3,2},{4,5},{5,4},{6,7},{7,6},{8,9},{9,8},{10,11... | collective-permute-start | bytes 786440 | tf_op jit(solution)/shard_map/ppermute | solution.py:677
  70.5 12.3 %collective-permute-start.18 = (bf16[128,1024]{1,0:T(8,128)(2,1)S(1)}, bf16[128,1024]{1,0:T(8,128)(2,1)S(1)}, u32[]{:S(2)}, u32[]{:S(2)}) collective-permute-start(bf16[128,1024]{1,0:T(8,128)(2,1)S(1)} %collective-permute-done.16.refs_8_), channel_id=1, source_target_pairs={{0,1},{1,0},{2,3},{3,2},{4,5},{5,4},{6,7},{7,6},{8,9},{9,8},{10,11... | collective-permute-start | bytes 786440 | tf_op jit(solution)/shard_map/ppermute | solution.py:677
  80.8 18.0 %collective-permute-start.27 = (bf16[256,512]{1,0:T(8,128)(2,1)S(1)}, bf16[256,512]{1,0:T(8,128)(2,1)S(1)}, u32[]{:S(2)}, u32[]{:S(2)}) collective-permute-start(bf16[256,512]{1,0:T(8,128)(2,1)S(1)} %get-tuple-element.64), channel_id=1, source_target_pairs={{4,12},{5,13},{6,14},{7,15},{12,4},{13,5},{14,6},{15,7},{0,0},{1,1... | collective-permute-start | bytes 786440 | tf_op jit(solution)/shard_map/ppermute | solution.py:718
  84.3 14.5 %collective-permute-start.19 = (bf16[256,512]{1,0:T(8,128)(2,1)S(1)}, bf16[256,512]{1,0:T(8,128)(2,1)S(1)}, u32[]{:S(2)}, u32[]{:S(2)}) collective-permute-start(bf16[256,512]{1,0:T(8,128)(2,1)S(1)} %get-tuple-element.62), channel_id=1, source_target_pairs={{0,2},{1,3},{2,0},{3,1},{4,6},{5,7},{6,4},{7,5},{8,10},{9,11},{10,... | collective-permute-start | bytes 786440 | tf_op jit(solution)/shard_map/ppermute | solution.py:677
  84.5 12.3 %collective-permute-start.28 = (f32[8,256]{1,0:T(8,128)S(1)}, f32[8,256]{1,0:T(8,128)S(1)}, u32[]{:S(2)}, u32[]{:S(2)}) collective-permute-start(f32[8,256]{1,0:T(8,128)S(1)} %get-tuple-element.65), channel_id=1, source_target_pairs={{4,12},{5,13},{6,14},{7,15},{12,4},{13,5},{14,6},{15,7},{0,0},{1,1... | collective-permute-start | bytes 24584 | tf_op jit(solution)/shard_map/ppermute | solution.py:718
  (17 other events, 225.2 us)

commit v4 on v3

--- a/solution.py
+++ b/solution.py
@@ -197,50 +197,49 @@
     )(tokens, ld, w_rk, w_rv, index, live)
 
 
+def clear(flags):
+    rows, blocks = flags.shape
+
+    def one(i, _):
+        flags[i // blocks, lax.rem(i, blocks)] = jnp.int32(0)
+        return 0
+
+    lax.fori_loop(0, rows * blocks, one, 0)
+
+
+def each_live(frames, f, index, act):
+    me = lax.axis_index("tm")
+    slots = index.shape[1] - 1
+
+    def visit(i, carry):
+        frame = index[f, i]
+        owner = frame // frames
+        act(me // LANES - owner // LANES, lax.rem(owner, LANES), lax.rem(frame, frames))
+        return carry
+
+    lax.fori_loop(0, jnp.minimum(index[f, slots], slots), visit, 0)
+
+
 def list_live(frames, distances, tables, groups):
-    me = lax.axis_index("tm")
-    lane = lax.rem(me, LANES)
-    plane = me // LANES
-    spans = len(distances)
-    for part in range(spans):
-        table, counts, need = tables[3 * part : 3 * part + 3]
-
-        def clear(b, _, need=need, part=part):
-            need[b] = (b < frames).astype(jnp.int32) if part == 0 else jnp.int32(0)
-            return 0
-
-        lax.fori_loop(0, need.shape[0], clear, 0)
-        for g in range(2):
-            for f in range(frames):
-                counts[g * frames + f] = jnp.int32(1 if part == 0 and g == 0 else 0)
-                if part == 0 and g == 0:
-                    table[f, 0] = jnp.int32(f)
+    lane = lax.rem(lax.axis_index("tm"), LANES)
+    for flags in tables:
+        clear(flags)
     for g, index in enumerate(groups):
-        slots = index.shape[1] - 1
         for f in range(frames):
             row = g * frames + f
-
-            def visit(i, carry, index=index, f=f, row=row):
-                frame = index[f, i]
-                owner = frame // frames
-                its = lax.rem(owner, LANES)
+            if g == 0:
+                tables[0][row, f] = jnp.int32(1)
+
+            def act(distance, its, place, row=row):
                 here = (its // 2) == (lane // 2)
-                distance = plane - owner // LANES
-                for part, (low, high) in enumerate(distances):
-                    table, counts, need = tables[3 * part : 3 * part + 3]
+                for flags, (low, high) in zip(tables, distances):
 
                     @pl.when(here & (distance >= low) & (distance < high))
-                    def _(table=table, counts=counts, need=need, low=low):
-                        block = ((distance - low) * 2 + ((its ^ lane) & 1)) * frames
-                        block = block + lax.rem(frame, frames)
-                        n = counts[row]
-                        table[row, n] = block
-                        need[block] = 1
-                        counts[row] = n + 1
-
-                return carry
-
-            lax.fori_loop(0, jnp.minimum(index[f, slots], slots), visit, 0)
+                    def _(flags=flags, low=low):
+                        block = ((distance - low) * 2 + ((its ^ lane) & 1)) * frames + place
+                        flags[row, block] = jnp.int32(1)
+
+            each_live(frames, f, index, act)
 
 
 def inner_kernel(frames, distances, *refs):
@@ -283,14 +282,10 @@
 def inner(tokens, w_rq, k, v, ld, pack, other, distances):
     rows, d = tokens.shape
     frames = rows // P_SIZE
-    slots = pack.shape[1] - 1
-    table_shapes = []
-    for low, high in distances:
-        table_shapes += [
-            jax.ShapeDtypeStruct((2 * frames, slots + 1), jnp.int32),
-            jax.ShapeDtypeStruct((2 * frames,), jnp.int32),
-            jax.ShapeDtypeStruct(((high - low) * 2 * frames,), jnp.int32),
-        ]
+    table_shapes = [
+        jax.ShapeDtypeStruct((2 * frames, (high - low) * 2 * frames), jnp.int32)
+        for low, high in distances
+    ]
     out = pl.pallas_call(
         functools.partial(inner_kernel, frames, distances),
         in_specs=[HBM, VMEM, HBM, HBM, SMEM, SMEM, HBM],
@@ -311,7 +306,7 @@
         cost_estimate=cost(2 * rows * d * H * DK, 8 << 20),
         name="inner",
     )(tokens, ld, k, v, pack, other, w_rq)
-    return out[0], out[1], [out[2 + 3 * i : 5 + 3 * i] for i in range(len(distances))]
+    return out[0], out[1], out[2:]
 
 
 def join(first, second):
@@ -433,156 +428,90 @@
     )(inner_out, qq, *states, tokens, gain.reshape(1, d), w_mq, w_mk, w_mv)
 
 
-def list_assist(frames, reach, steps, planes, pack, table, counts, need):
+def list_assist(frames, at, steps, planes, index, flags):
     me = lax.axis_index("tm")
-    lane = lax.rem(me, LANES)
-    plane = me // LANES
-    slots = pack.shape[1] - 1
-
-    def clear(b, _):
-        need[b] = jnp.int32(0)
-        return 0
-
-    lax.fori_loop(0, need.shape[0], clear, 0)
+    clear(flags)
     for f in range(frames):
-        counts[f] = jnp.int32(0)
-
-        def visit(i, carry, f=f):
-            frame = pack[f, i]
-            owner = frame // frames
-            distance = plane - owner // LANES
-
-            @pl.when((distance >= 1) & (distance <= reach) & (plane + steps < planes))
+
+        def act(distance, its, place, f=f):
+            @pl.when((distance == at) & (me // LANES + steps < planes))
             def _():
-                block = ((distance - 1) * LANES + (lax.rem(owner, LANES) ^ lane)) * frames
-                block = block + lax.rem(frame, frames)
-                n = counts[f]
-                table[f, n] = block
-                need[block] = 1
-                counts[f] = n + 1
-
-            return carry
-
-        lax.fori_loop(0, jnp.minimum(pack[f, slots], slots), visit, 0)
+                flags[f, (its ^ lax.rem(me, LANES)) * frames + place] = jnp.int32(1)
+
+        each_live(frames, f, index, act)
 
 
 def attend_kernel(frames, blocks, groups, first, last, assist, *refs):
     if assist is None:
-        table, counts, need = refs[:3]
-        refs = refs[3:]
+        live, refs = refs[0], refs[1:]
     else:
-        pack, refs = refs[0], refs[1:]
-        table, counts, need = refs[-3:]
-        refs = refs[:-3]
-        list_assist(frames, *assist, pack, table, counts, need)
+        index, live, refs = refs[0], refs[-1], refs[1:-1]
+        list_assist(frames, *assist, index, live)
     asked, refs = refs[:groups], refs[groups:]
     if not first:
         acc_in, stat_in = refs[:2]
         refs = refs[2:]
-    kv_refs, refs = refs[:blocks], refs[blocks:]
+    kv, refs = refs[:blocks], refs[blocks:]
     if last:
         outs, refs = refs[: 2 * groups], refs[2 * groups :]
     else:
         acc_out, stat_out = refs[:2]
         refs = refs[2:]
-    kv, scores, peak, total, acc, stat, sems = refs
-    copies = [pltpu.make_async_copy(kv_refs[b], kv.at[b], sems.at[b]) for b in range(blocks)]
-    for b in range(blocks):
-
-        @pl.when(need[b] == 1)
-        def _(b=b):
-            copies[b].start()
-
-    for b in range(blocks):
-
-        @pl.when(need[b] == 1)
-        def _(b=b):
-            copies[b].wait()
-
+    scores, stat = refs
+    rows = frames * P_SIZE
     scale = MD**-0.5
-    for row in range(groups * frames):
-        queries = asked[row // frames]
-        f = row % frames
-        span = slice(f * P_SIZE, (f + 1) * P_SIZE)
-        held = slice(row * P_SIZE, (row + 1) * P_SIZE)
-        n = counts[row]
-        if first:
-            stat[...] = jnp.zeros_like(stat)
-            acc[...] = jnp.zeros_like(acc)
-            peak[...] = jnp.full_like(peak, NEG)
-        else:
-            stat[...] = stat_in[held, :]
-            for e in range(MH):
-                acc[e] = acc_in[held, e * MD : (e + 1) * MD]
-
-        @pl.when(n > 0)
-        def _(row=row, queries=queries, span=span, n=n):
+    base2 = scale * 1.4426950408889634
+    pairs = [range(i, min(i + 2, blocks)) for i in range(0, blocks, 2)]
+    spans = [slice(f * P_SIZE, (f + 1) * P_SIZE) for f in range(frames)]
+    for g in range(groups):
+        held = slice(g * rows, (g + 1) * rows)
+        stat[...] = jnp.zeros_like(stat) if first else stat_in[held, :]
+        for e in range(MH):
+            cols, vcols = slice(e * MD, (e + 1) * MD), slice(MC + e * MD, MC + (e + 1) * MD)
+            q = asked[g][:, cols]
+            tops = [None] * frames
+            for pair in pairs:
+                s = nt(q, jnp.concatenate([kv[b][:, cols] for b in pair], axis=0))
+                for j, b in enumerate(pair):
+                    for f in range(frames):
+                        part = s[spans[f], j * P_SIZE : (j + 1) * P_SIZE]
+                        part = jnp.where(live[g * frames + f, b] == 1, part, NEG)
+                        scores[spans[f], b * P_SIZE : (b + 1) * P_SIZE] = part
+                        tops[f] = part if tops[f] is None else jnp.maximum(tops[f], part)
+            top = jnp.concatenate([jnp.max(t, axis=1, keepdims=True) for t in tops], axis=0)
+            top = jnp.maximum(top, 0.1 * NEG)
             if not first:
-                for e in range(MH):
-                    peak[e] = jnp.broadcast_to(stat[:, e : e + 1], (P_SIZE, P_SIZE))
-            total[...] = jnp.zeros_like(total)
-            half = (n + 1) // 2
-
-            def score(i, _):
-                b0 = table[row, 2 * i]
-                more = 2 * i + 1 < n
-                b1 = jnp.where(more, table[row, jnp.minimum(2 * i + 1, n - 1)], b0)
-                for e in range(MH):
-                    cols = slice(e * MD, (e + 1) * MD)
-                    s0 = nt(queries[span, cols], kv[b0, :, cols])
-                    s1 = nt(queries[span, cols], kv[b1, :, cols])
-                    s1 = jnp.where(more, s1, NEG)
-                    scores[2 * i, e] = s0
-                    scores[2 * i + 1, e] = s1
-                    peak[e] = jnp.maximum(peak[e], jnp.maximum(s0, s1))
-                return 0
-
-            lax.fori_loop(0, half, score, 0)
-            for e in range(MH):
-                top = jnp.max(peak[e], axis=1, keepdims=True)
-                peak[e] = jnp.broadcast_to(top, (P_SIZE, P_SIZE))
-                if not first:
-                    fade = jnp.exp((stat[:, e : e + 1] - top) * scale)
-                    acc[e] = acc[e] * fade
-                    stat[:, MH + e : MH + e + 1] = stat[:, MH + e : MH + e + 1] * fade
-                stat[:, e : e + 1] = top
-
-            def weigh(i, _):
-                b0 = table[row, 2 * i]
-                b1 = table[row, jnp.minimum(2 * i + 1, n - 1)]
-                for e in range(MH):
-                    cols = slice(MC + e * MD, MC + (e + 1) * MD)
-                    p0 = jnp.exp((scores[2 * i, e] - peak[e]) * scale)
-                    p1 = jnp.exp((scores[2 * i + 1, e] - peak[e]) * scale)
-                    total[e] += p0 + p1
-                    acc[e] += nn(p0.astype(BF16), kv[b0, :, cols]) + nn(
-                        p1.astype(BF16), kv[b1, :, cols]
-                    )
-                return 0
-
-            lax.fori_loop(0, half, weigh, 0)
-            for e in range(MH):
-                stat[:, MH + e : MH + e + 1] += jnp.sum(total[e], axis=1, keepdims=True)
-
-        if first:
-
-            @pl.when(n == 0)
-            def _():
-                for e in range(MH):
-                    stat[:, e : e + 1] = jnp.full((P_SIZE, 1), NEG, F32)
-
+                before = stat[:, e : e + 1]
+                top = jnp.maximum(top, before)
+                fade = jnp.exp2((before - top) * base2)
+            total, acc = None, None
+            for pair in pairs:
+                ps = []
+                for b in pair:
+                    p = jnp.exp2((scores[:, b * P_SIZE : (b + 1) * P_SIZE] - top) * base2)
+                    total = p if total is None else total + p
+                    ps.append(p.astype(BF16))
+                part = nn(
+                    jnp.concatenate(ps, axis=1),
+                    jnp.concatenate([kv[b][:, vcols] for b in pair], axis=0),
+                )
+                acc = part if acc is None else acc + part
+            total = jnp.sum(total, axis=1, keepdims=True)
+            if not first:
+                total = total + fade * stat[:, MH + e : MH + e + 1]
+                acc = acc + fade * acc_in[held, cols]
+            stat[:, e : e + 1] = top
+            stat[:, MH + e : MH + e + 1] = total
+            if last:
+                outs[2 * g][:, cols] = (acc / jnp.maximum(total, 1e-30)).astype(outs[2 * g].dtype)
+            else:
+                acc_out[held, cols] = acc
         if last:
-            out, stats = outs[2 * (row // frames) : 2 * (row // frames) + 2]
-            for e in range(MH):
-                l = jnp.maximum(stat[:, MH + e : MH + e + 1], 1e-30)
-                out[span, e * MD : (e + 1) * MD] = (acc[e] / l).astype(out.dtype)
             flat = jnp.transpose(stat[...])
             low = jnp.log(jnp.maximum(flat[MH : 2 * MH], 1e-30))
-            stats[:, span] = jnp.concatenate([flat[:MH] * scale + low, low], axis=0)
+            outs[2 * g + 1][...] = jnp.concatenate([flat[:MH] * scale + low, low], axis=0)
         else:
             stat_out[held, :] = stat[...]
-            for e in range(MH):
-                acc_out[held, e * MD : (e + 1) * MD] = acc[e]
 
 
 def attend(lists, asked, kvs, state, last, assist=None):
@@ -590,7 +519,6 @@
     frames = rows // P_SIZE
     blocks = len(kvs)
     groups = len(asked)
-    slots = lists[0].shape[1] - 1
     first = state is None
     state = [] if first else list(state)
     out_shape = []
@@ -606,38 +534,28 @@
             jax.ShapeDtypeStruct((groups * rows, MC), F32),
             jax.ShapeDtypeStruct((groups * rows, 128), F32),
         ]
-    scratch = [
-        pltpu.VMEM((blocks, P_SIZE, 2 * MC), BF16),
-        pltpu.VMEM((slots + 3, MH, P_SIZE, P_SIZE), F32),
-        pltpu.VMEM((MH, P_SIZE, P_SIZE), F32),
-        pltpu.VMEM((MH, P_SIZE, P_SIZE), F32),
-        pltpu.VMEM((MH, P_SIZE, MD), F32),
-        pltpu.VMEM((P_SIZE, 128), F32),
-        pltpu.SemaphoreType.DMA((blocks,)),
-    ]
+    scratch = [pltpu.VMEM((rows, blocks * P_SIZE), F32), pltpu.VMEM((rows, 128), F32)]
     if assist is not None:
-        scratch += [
-            pltpu.SMEM((frames, slots + 1), jnp.int32),
-            pltpu.SMEM((frames,), jnp.int32),
-            pltpu.SMEM((blocks,), jnp.int32),
-        ]
+        scratch.append(pltpu.SMEM((frames, blocks), jnp.int32))
     return pl.pallas_call(
         functools.partial(attend_kernel, frames, blocks, groups, first, last, assist),
-        in_specs=[SMEM] * len(lists) + [VMEM] * (groups + len(state)) + [HBM] * blocks,
+        in_specs=[SMEM] + [VMEM] * (groups + len(state) + blocks),
         out_specs=[VMEM] * len(out_shape),
         out_shape=out_shape,
         scratch_shapes=scratch,
         compiler_params=params(),
-        cost_estimate=cost(4 * 8 * frames * P_SIZE * P_SIZE * MC, blocks * P_SIZE * MC * 4),
+        cost_estimate=cost(4 * groups * blocks * rows * P_SIZE * MC, blocks * P_SIZE * MC * 4),
         name="assist" if assist is not None else "attend_last" if last else "attend",
-    )(*lists, *asked, *state, *kvs)
-
-
-def output_kernel(parts, *refs):
+    )(lists, *asked, *state, *kvs)
+
+
+def output_kernel(parts, steps, *refs):
     values, stats = refs[0 : 2 * parts : 2], refs[1 : 2 * parts : 2]
     hid_ref, w_ref, out_ref, mixed = refs[2 * parts :]
     rows = hid_ref.shape[0]
     logs = [ref[...] for ref in stats]
+    if parts > 2:
+        logs[2] = jnp.where(lax.axis_index("tm") // LANES > steps, logs[2], NEG)
     top = functools.reduce(jnp.maximum, logs)
     shares = [jnp.exp(x - top) for x in logs]
     inv = 1.0 / functools.reduce(jnp.add, shares)
@@ -653,11 +571,11 @@
     out_ref[...] = (hid_ref[...].astype(F32) + nn(mixed[...], w_ref[...])).astype(BF16)
 
 
-def output(parts, hid, w_out):
+def output(parts, hid, w_out, steps):
     rows, d = hid.shape
     flat = [x for part in parts for x in part]
     return pl.pallas_call(
-        functools.partial(output_kernel, len(parts)),
+        functools.partial(output_kernel, len(parts), steps),
         in_specs=[VMEM] * (len(flat) + 2),
         out_specs=VMEM,
         out_shape=jax.ShapeDtypeStruct((rows, d), BF16),
@@ -682,7 +600,7 @@
 
     message, chunk = (ROWS + TAIL, DV), (ROWS, DV)
     steps, reach = reaches(planes)
-    spans = ((0, steps), (steps, steps + 1)) if steps else ((0, 1),)
+    spans = spans_of(steps)
     k, v, keep, give, pack = local(tokens, w_rk, w_rv, log_decay, mem_index, mem_count)
     core_got = flip(give, 1)
     other = flip(pack, 2)
@@ -733,24 +651,28 @@
         if 1 <= distance <= reach:
             column = [flip(x, 2) for x in kv]
             both = [flip(x, 1) for x in column]
-            across += kv + near + column + both
+            across.append(kv + near + column + both)
     parts = []
     if reach:
         helped = [(p, p + steps) for p in range(1, planes - steps)]
         down = [(b, a) for a, b in helped]
-        rest = [(p, p) for p in range(planes) if all(p not in pair for pair in helped)]
         far_q = between(q, down)
         far_pack = between(pack, down)
-        far = attend([far_pack], [far_q], across, None, True, (reach, steps, planes))
-        whole = helped + down + rest
-        parts = [[between(x, whole) for x in far]]
+        far = None
+        for at, blocks in enumerate(across, 1):
+            far = attend(far_pack, [far_q], blocks, far, at == reach, (at, steps, planes))
+        parts = [[between(x, helped) for x in far]]
     state = None
     for (low, high), table in zip(spans, tables):
         blocks = [x for group in held[low:high] for x in group]
         state = attend(table, [q, partner_q], blocks, state, high == steps + 1)
     o, lse, po, plse = state
     back = [flip(po, 2), flip(plse, 2)]
-    return output([[o, lse], back] + parts, hid, w_out)
+    return output([[o, lse], back] + parts, hid, w_out, steps)
+
+
+def spans_of(steps):
+    return [(low, min(low + 2, steps)) for low in range(0, steps, 2)] + [(steps, steps + 1)]
 
 
 def reaches(planes):

time: 101 us -> 101 us (level)
  the two profiles are of different devices: /device:TPU:10 before, /device:TPU:13 now
where the time goes in v4:
time: 101 us; the launch traced here: 100 us
  waiting for transfers between devices  33.3 us (33%)
  starting transfers between devices  32.5 us (32%)
  Pallas kernels  29.5 us (29%)
  local copies, waits for them, and re-layouts  4.5 us (4%)
    ppermute x18, waiting for transfers between devices, flip(): return lax.ppermute(x, 'tm', [(i, i ^ bits) for i in range(size)])  20.4 us
    pallas_call x3, Pallas kernels, attend(): pl.pallas_call(functools.partial(attend_kernel, frames, blocks, groups, f...  17.4 us
    ppermute x18, starting transfers between devices, flip(): return lax.ppermute(x, 'tm', [(i, i ^ bits) for i in range(size)])  16.7 us
    ppermute x8, starting transfers between devices, between(): lax.ppermute(x, 'tm', [(a * LANES + i, b * LANES + i) for a, b in pairs f...  12 us
    ppermute x8, waiting for transfers between devices, between(): lax.ppermute(x, 'tm', [(a * LANES + i, b * LANES + i) for a, b in pairs f...  8.24 us
    ppermute x3, waiting for transfers between devices, up(): return lax.ppermute(x, 'tm', [(i, (i + step) % size) for i in range(size)])  4.7 us
    unnamed x24, local copies, waits for them, and re-layouts  4.5 us
    pallas_call x1, Pallas kernels, local(): pl.pallas_call(local_kernel, in_specs=[HBM] * 6, out_specs=[VMEM] * 4 + [...  3.93 us
  transfers between devices with their start and end apart: 29, of which 11 were waited for; matrix products, arithmetic and copies ran while one was open for 0% of the time, Pallas kernels for 21%

profile of v4, /device:TPU:13, one launch (start us, length us, event | category | flops | bytes accessed | tf_op | source)
XLA Modules:
  0.0 100.1 jit_solution(7525832128378507739)
XLA Ops:
  0.0 3.9 %local.1 = (bf16[256,512]{1,0:T(8,128)(2,1)}, bf16[256,1024]{1,0:T(8,128)(2,1)}, bf16[2,272,128]{2,1,0:T(8,128)(2,1)}, bf16[2,272,128]{2,1,0:T(8,128)(2,1)}, s32[2,9]{1,0:T(2,128)}) custom-call(bf16[256,1024]{1,0:T(8,128)(2,1)} %refs_4_.1, f32[8,256]{1,0:T(8,128)} %refs_1_.1, bf16[1024,512]{1,0:T(8,128)(2,1)} %wk_in.1, bf16[1024,1024]{1,0:T(8,128)(2,1)} %wv_in.1, ...), custom_call_target="tpu_custom_call" | custom-call | tf_op jit(solution)/shard_map/local/pallas_call | solution.py:174
  7.2 2.9 %collective-permute-done.2.got.refs_1_ = bf16[272,128]{1,0:T(8,128)(2,1)S(1)} collective-permute-done((bf16[272,128]{1,0:T(8,128)(2,1)S(1)}, bf16[272,128]{1,0:T(8,128)(2,1)S(1)}, u32[]{:S(2)}, u32[]{:S(2)}) %collective-permute-start.2) | collective-permute-done | bytes 69664 | tf_op jit(solution)/shard_map/ppermute | solution.py:595
  14.0 1.9 %collective-permute-done.4.refs_3_ = bf16[272,128]{1,0:T(8,128)(2,1)S(1)} collective-permute-done((bf16[272,128]{1,0:T(8,128)(2,1)S(1)}, bf16[272,128]{1,0:T(8,128)(2,1)S(1)}, u32[]{:S(2)}, u32[]{:S(2)}) %collective-permute-start.4) | collective-permute-done | bytes 69664 | tf_op jit(solution)/shard_map/ppermute | solution.py:599
  15.9 2.8 %collective-permute-done.5.refs_4_ = bf16[272,128]{1,0:T(8,128)(2,1)S(1)} collective-permute-done((bf16[272,128]{1,0:T(8,128)(2,1)S(1)}, bf16[272,128]{1,0:T(8,128)(2,1)S(1)}, u32[]{:S(2)}, u32[]{:S(2)}) %collective-permute-start.5) | collective-permute-done | bytes 69664 | tf_op jit(solution)/shard_map/ppermute | solution.py:599
  20.0 2.0 %collective-permute-done.6.got = bf16[256,128]{1,0:T(8,128)(2,1)S(1)} collective-permute-done((bf16[256,128]{1,0:T(8,128)(2,1)S(1)}, bf16[256,128]{1,0:T(8,128)(2,1)S(1)}, u32[]{:S(2)}, u32[]{:S(2)}) %collective-permute-start.6) | collective-permute-done | bytes 65568 | tf_op jit(solution)/shard_map/ppermute | solution.py:595
  23.1 2.7 %collective-permute-start.7 = (bf16[2,256,128]{2,1,0:T(8,128)(2,1)S(1)}, bf16[2,256,128]{2,1,0:T(8,128)(2,1)S(1)}, u32[]{:S(2)}, u32[]{:S(2)}) collective-permute-start(bf16[2,256,128]{2,1,0:T(8,128)(2,1)S(1)} %get-tuple-element.45), channel_id=1, source_target_pairs={{0,1},{1,0},{2,3},{3,2},{4,5},{5,4},{6,7},{7,6},{8,9},{9,8},{10,11... | collective-permute-start | bytes 393224 | tf_op jit(solution)/shard_map/ppermute | solution.py:595
  26.2 2.2 %collective-permute-done.refs_5_ = s32[2,9]{1,0:T(2,128)S(1)} collective-permute-done((s32[2,9]{1,0:T(2,128)}, s32[2,9]{1,0:T(2,128)S(1)}, u32[]{:S(2)}, u32[]{:S(2)}) %collective-permute-start) | collective-permute-done | bytes 104 | tf_op jit(solution)/shard_map/ppermute | solution.py:595
  31.0 3.7 %inner.1 = (f32[256,1024]{1,0:T(8,128)S(1)}, bf16[256,1024]{1,0:T(8,128)(2,1)S(1)}, s32[4,8]{1,0:T(4,128)S(1)}, s32[4,4]{1,0:T(4,128)S(1)}) custom-call(bf16[256,1024]{1,0:T(8,128)(2,1)S(1)} %copy-done, f32[8,256]{1,0:T(8,128)S(1)} %copy-done.9, bf16[256,512]{1,0:T(8,128)(2,1)S(1)} %copy-done.8, bf16[256,1024]{1,0:T(8,128)(2,1)S(1)} %copy-done.7, ...), custom_call_target="tpu_custom_call" | custom-call | flops 268435456 | bytes 8388608 | tf_op jit(solution)/shard_map/inner/pallas_call | solution.py:289
  34.8 2.2 %hidden.1 = (bf16[256,1024]{1,0:T(8,128)(2,1)S(1)}, bf16[256,512]{1,0:T(8,128)(2,1)S(1)}, bf16[128,1024]{1,0:T(8,128)(2,1)S(1)}, bf16[128,1024]{1,0:T(8,128)(2,1)S(1)}) custom-call(f32[256,1024]{1,0:T(8,128)S(1)} %get-tuple-element.36.refs_0_, bf16[256,1024]{1,0:T(8,128)(2,1)S(1)} %get-tuple-element.37.refs_1_, ...), custom_call_target="tpu_custom_call" | custom-call | tf_op jit(solution)/shard_map/hidden/pallas_call | solution.py:414
  37.0 2.4 %collective-permute-start.12 = (bf16[128,1024]{1,0:T(8,128)(2,1)S(1)}, bf16[128,1024]{1,0:T(8,128)(2,1)S(1)}, u32[]{:S(2)}, u32[]{:S(2)}) collective-permute-start(bf16[128,1024]{1,0:T(8,128)(2,1)S(1)} %get-tuple-element.49.refs_4_), channel_id=1, source_target_pairs={{0,4},{1,5},{2,6},{3,7},{4,8},{5,9},{6,10},{7,11},{8,12},{9,13},{1... | collective-permute-start | bytes 786440 | tf_op jit(solution)/shard_map/ppermute | solution.py:636
  39.5 1.7 %collective-permute-start.10 = (bf16[128,1024]{1,0:T(8,128)(2,1)S(1)}, bf16[128,1024]{1,0:T(8,128)(2,1)S(1)}, u32[]{:S(2)}, u32[]{:S(2)}) collective-permute-start(bf16[128,1024]{1,0:T(8,128)(2,1)S(1)} %get-tuple-element.49.refs_4_), channel_id=1, source_target_pairs={{0,1},{1,0},{2,3},{3,2},{4,5},{5,4},{6,7},{7,6},{8,9},{9,8},{10,11... | collective-permute-start | bytes 786440 | tf_op jit(solution)/shard_map/ppermute | solution.py:595
  42.6 7.3 %collective-permute-done.21.refs_0_ = s32[2,9]{1,0:T(2,128)S(1)} collective-permute-done((s32[2,9]{1,0:T(2,128)S(1)}, s32[2,9]{1,0:T(2,128)S(1)}, u32[]{:S(2)}, u32[]{:S(2)}) %collective-permute-start.21) | collective-permute-done | bytes 104 | tf_op jit(solution)/shard_map/ppermute | solution.py:636
  49.9 2.3 %collective-permute-start.9 = (bf16[128,1024]{1,0:T(8,128)(2,1)S(1)}, bf16[128,1024]{1,0:T(8,128)(2,1)S(1)}, u32[]{:S(2)}, u32[]{:S(2)}) collective-permute-start(bf16[128,1024]{1,0:T(8,128)(2,1)S(1)} %get-tuple-element.48.refs_3_), channel_id=1, source_target_pairs={{0,1},{1,0},{2,3},{3,2},{4,5},{5,4},{6,7},{7,6},{8,9},{9,8},{10,11... | collective-permute-start | bytes 786440 | tf_op jit(solution)/shard_map/ppermute | solution.py:595
  54.3 1.9 %collective-permute-start.15 = (bf16[128,1024]{1,0:T(8,128)(2,1)S(1)}, bf16[128,1024]{1,0:T(8,128)(2,1)S(1)}, u32[]{:S(2)}, u32[]{:S(2)}) collective-permute-start(bf16[128,1024]{1,0:T(8,128)(2,1)S(1)} %collective-permute-done.11.refs_7_.refs_2_), channel_id=1, source_target_pairs={{4,8},{5,9},{6,10},{7,11},{8,12},{9,13},{10,14},{11,15},{0,0},{1,1... | collective-permute-start | bytes 786440 | tf_op jit(solution)/shard_map/ppermute | solution.py:636
  56.2 3.8 %collective-permute-done.23.refs_6_ = bf16[128,1024]{1,0:T(8,128)(2,1)S(1)} collective-permute-done((bf16[128,1024]{1,0:T(8,128)(2,1)S(1)}, bf16[128,1024]{1,0:T(8,128)(2,1)S(1)}, u32[]{:S(2)}, u32[]{:S(2)}) %collective-permute-start.23) | collective-permute-done | bytes 262176 | tf_op jit(solution)/shard_map/ppermute | solution.py:595
  60.0 1.9 %collective-permute-start.16 = (bf16[128,1024]{1,0:T(8,128)(2,1)S(1)}, bf16[128,1024]{1,0:T(8,128)(2,1)S(1)}, u32[]{:S(2)}, u32[]{:S(2)}) collective-permute-start(bf16[128,1024]{1,0:T(8,128)(2,1)S(1)} %collective-permute-done.12.refs_8_.refs_3_), channel_id=1, source_target_pairs={{4,8},{5,9},{6,10},{7,11},{8,12},{9,13},{10,14},{11,15},{0,0},{1,1... | collective-permute-start | bytes 786440 | tf_op jit(solution)/shard_map/ppermute | solution.py:636
  61.9 3.7 %collective-permute-done.24.refs_7_ = bf16[128,1024]{1,0:T(8,128)(2,1)S(1)} collective-permute-done((bf16[128,1024]{1,0:T(8,128)(2,1)S(1)}, bf16[128,1024]{1,0:T(8,128)(2,1)S(1)}, u32[]{:S(2)}, u32[]{:S(2)}) %collective-permute-start.24) | collective-permute-done | bytes 262176 | tf_op jit(solution)/shard_map/ppermute | solution.py:595
  69.3 2.2 %collective-permute-start.18 = (bf16[128,1024]{1,0:T(8,128)(2,1)S(1)}, bf16[128,1024]{1,0:T(8,128)(2,1)S(1)}, u32[]{:S(2)}, u32[]{:S(2)}) collective-permute-start(bf16[128,1024]{1,0:T(8,128)(2,1)S(1)} %collective-permute-done.16.refs_6_), channel_id=1, source_target_pairs={{0,1},{1,0},{2,3},{3,2},{4,5},{5,4},{6,7},{7,6},{8,9},{9,8},{10,11... | collective-permute-start | bytes 786440 | tf_op jit(solution)/shard_map/ppermute | solution.py:595
  71.5 5.7 %attend.1 = (f32[512,512]{1,0:T(8,128)S(1)}, f32[512,128]{1,0:T(8,128)S(1)}) custom-call(s32[4,8]{1,0:T(4,128)S(1)} %get-tuple-element.47.refs_0_, bf16[256,512]{1,0:T(8,128)(2,1)S(1)} %get-tuple-element.46.refs_1_, bf16[256,512]{1,0:T(8,128)(2,1)S(1)} %collective-permute-done.8.refs_2_, bf16[128,1024]{1,0:T(8,128)(2,1)S(1)} %get-tuple-element.48.refs_3_, ...), custom_call_target="tpu_custom_call" | custom-call | flops 1073741824 | bytes 2097152 | tf_op jit(solution)/shard_map/attend/pallas_call | solution.py:540
  77.2 4.0 %assist.1 = (bf16[256,512]{1,0:T(8,128)(2,1)S(1)}, f32[8,256]{1,0:T(8,128)S(1)}) custom-call(s32[2,9]{1,0:T(2,128)S(1)} %collective-permute-done.21.refs_0_, bf16[256,512]{1,0:T(8,128)(2,1)S(1)} %collective-permute-done.22.refs_1_, bf16[128,1024]{1,0:T(8,128)(2,1)S(1)} %collective-permute-done.11.refs_7_.refs_2_, ...), custom_call_target="tpu_custom_call" | custom-call | flops 536870912 | bytes 2097152 | tf_op jit(solution)/shard_map/assist/pallas_call | solution.py:540
  81.3 1.8 %collective-permute-start.27 = (bf16[256,512]{1,0:T(8,128)(2,1)S(1)}, bf16[256,512]{1,0:T(8,128)(2,1)S(1)}, u32[]{:S(2)}, u32[]{:S(2)}) collective-permute-start(bf16[256,512]{1,0:T(8,128)(2,1)S(1)} %get-tuple-element.56), channel_id=1, source_target_pairs={{4,12},{5,13},{6,14},{7,15},{20,28},{21,29},{22,30},{23,31}} | collective-permute-start | bytes 786440 | tf_op jit(solution)/shard_map/ppermute | solution.py:636
  83.1 7.7 %attend_last.1 = (f32[256,512]{1,0:T(8,128)S(1)}, f32[8,256]{1,0:T(8,128)S(1)}, bf16[256,512]{1,0:T(8,128)(2,1)S(1)}, f32[8,256]{1,0:T(8,128)S(1)}) custom-call(s32[4,4]{1,0:T(4,128)S(1)} %get-tuple-element.35.refs_0_, bf16[256,512]{1,0:T(8,128)(2,1)S(1)} %get-tuple-element.46.refs_1_, bf16[256,512]{1,0:T(8,128)(2,1)S(1)} %collective-permute-done.8.refs_2_, ...), custom_call_target="tpu_custom_call" | custom-call | flops 536870912 | bytes 1048576 | tf_op jit(solution)/shard_map/attend_last/pallas_call | solution.py:540
  93.7 4.5 %collective-permute-done.20.refs_3_ = f32[8,256]{1,0:T(8,128)S(1)} collective-permute-done((f32[8,256]{1,0:T(8,128)S(1)}, f32[8,256]{1,0:T(8,128)S(1)}, u32[]{:S(2)}, u32[]{:S(2)}) %collective-permute-start.20) | collective-permute-done | bytes 8224 | tf_op jit(solution)/shard_map/ppermute | solution.py:595
  98.2 1.9 %output.1 = bf16[256,1024]{1,0:T(8,128)(2,1)} custom-call(f32[256,512]{1,0:T(8,128)S(1)} %get-tuple-element.52.refs_0_, f32[8,256]{1,0:T(8,128)S(1)} %get-tuple-element.53.refs_1_, bf16[256,512]{1,0:T(8,128)(2,1)S(1)} %collective-permute-done.19.refs_2_, f32[8,256]{1,0:T(8,128)S(1)} %collective-permute-done.20.refs_3_, ...), custom_call_target="tpu_custom_call" | custom-call | tf_op jit(solution)/shard_map/output/pallas_call | solution.py:577
  (69 shorter events, 22.8 us)
Async XLA Ops:
  10.2 3.8 %collective-permute-start.3 = (bf16[272,128]{1,0:T(8,128)(2,1)S(1)}, bf16[272,128]{1,0:T(8,128)(2,1)S(1)}, u32[]{:S(2)}, u32[]{:S(2)}) collective-permute-start(bf16[272,128]{1,0:T(8,128)(2,1)S(1)} %shard_map.119), channel_id=1, source_target_pairs={{0,4},{1,5},{2,6},{3,7},{4,8},{5,9},{6,10},{7,11},{8,12},{9,13},{1... | collective-permute-start | bytes 208904 | tf_op jit(solution)/shard_map/ppermute | solution.py:599
  11.6 4.3 %collective-permute-start.4 = (bf16[272,128]{1,0:T(8,128)(2,1)S(1)}, bf16[272,128]{1,0:T(8,128)(2,1)S(1)}, u32[]{:S(2)}, u32[]{:S(2)}) collective-permute-start(bf16[272,128]{1,0:T(8,128)(2,1)S(1)} %shard_map.119), channel_id=1, source_target_pairs={{0,8},{1,9},{2,10},{3,11},{4,12},{5,13},{6,14},{7,15},{8,0},{9,1},... | collective-permute-start | bytes 208904 | tf_op jit(solution)/shard_map/ppermute | solution.py:599
  12.7 6.1 %collective-permute-start.5 = (bf16[272,128]{1,0:T(8,128)(2,1)S(1)}, bf16[272,128]{1,0:T(8,128)(2,1)S(1)}, u32[]{:S(2)}, u32[]{:S(2)}) collective-permute-start(bf16[272,128]{1,0:T(8,128)(2,1)S(1)} %shard_map.119), channel_id=1, source_target_pairs={{0,12},{1,13},{2,14},{3,15},{4,0},{5,1},{6,2},{7,3},{8,4},{9,5},{1... | collective-permute-start | bytes 208904 | tf_op jit(solution)/shard_map/ppermute | solution.py:599
  23.1 11.7 %collective-permute-start.7 = (bf16[2,256,128]{2,1,0:T(8,128)(2,1)S(1)}, bf16[2,256,128]{2,1,0:T(8,128)(2,1)S(1)}, u32[]{:S(2)}, u32[]{:S(2)}) collective-permute-start(bf16[2,256,128]{2,1,0:T(8,128)(2,1)S(1)} %get-tuple-element.45), channel_id=1, source_target_pairs={{0,1},{1,0},{2,3},{3,2},{4,5},{5,4},{6,7},{7,6},{8,9},{9,8},{10,11... | collective-permute-start | bytes 393224 | tf_op jit(solution)/shard_map/ppermute | solution.py:595
  37.0 15.2 %collective-permute-start.11 = (bf16[128,1024]{1,0:T(8,128)(2,1)S(1)}, bf16[128,1024]{1,0:T(8,128)(2,1)S(1)}, u32[]{:S(2)}, u32[]{:S(2)}) collective-permute-start(bf16[128,1024]{1,0:T(8,128)(2,1)S(1)} %get-tuple-element.48.refs_3_), channel_id=1, source_target_pairs={{0,4},{1,5},{2,6},{3,7},{4,8},{5,9},{6,10},{7,11},{8,12},{9,13},{1... | collective-permute-start | bytes 786440 | tf_op jit(solution)/shard_map/ppermute | solution.py:636
  37.0 15.3 %collective-permute-start.12 = (bf16[128,1024]{1,0:T(8,128)(2,1)S(1)}, bf16[128,1024]{1,0:T(8,128)(2,1)S(1)}, u32[]{:S(2)}, u32[]{:S(2)}) collective-permute-start(bf16[128,1024]{1,0:T(8,128)(2,1)S(1)} %get-tuple-element.49.refs_4_), channel_id=1, source_target_pairs={{0,4},{1,5},{2,6},{3,7},{4,8},{5,9},{6,10},{7,11},{8,12},{9,13},{1... | collective-permute-start | bytes 786440 | tf_op jit(solution)/shard_map/ppermute | solution.py:636
  39.5 14.2 %collective-permute-start.10 = (bf16[128,1024]{1,0:T(8,128)(2,1)S(1)}, bf16[128,1024]{1,0:T(8,128)(2,1)S(1)}, u32[]{:S(2)}, u32[]{:S(2)}) collective-permute-start(bf16[128,1024]{1,0:T(8,128)(2,1)S(1)} %get-tuple-element.49.refs_4_), channel_id=1, source_target_pairs={{0,1},{1,0},{2,3},{3,2},{4,5},{5,4},{6,7},{7,6},{8,9},{9,8},{10,11... | collective-permute-start | bytes 786440 | tf_op jit(solution)/shard_map/ppermute | solution.py:595
  41.1 13.1 %collective-permute-start.8 = (bf16[256,512]{1,0:T(8,128)(2,1)S(1)}, bf16[256,512]{1,0:T(8,128)(2,1)S(1)}, u32[]{:S(2)}, u32[]{:S(2)}) collective-permute-start(bf16[256,512]{1,0:T(8,128)(2,1)S(1)} %get-tuple-element.46.refs_1_), channel_id=1, source_target_pairs={{0,2},{1,3},{2,0},{3,1},{4,6},{5,7},{6,4},{7,5},{8,10},{9,11},{10,... | collective-permute-start | bytes 786440 | tf_op jit(solution)/shard_map/ppermute | solution.py:595
  41.4 8.5 %collective-permute-start.21 = (s32[2,9]{1,0:T(2,128)S(1)}, s32[2,9]{1,0:T(2,128)S(1)}, u32[]{:S(2)}, u32[]{:S(2)}) collective-permute-start(s32[2,9]{1,0:T(2,128)S(1)} %copy-done.11), channel_id=1, source_target_pairs={{12,4},{13,5},{14,6},{15,7},{28,20},{29,21},{30,22},{31,23}} | collective-permute-start | bytes 224 | tf_op jit(solution)/shard_map/ppermute | solution.py:636
  49.9 4.4 %collective-permute-start.9 = (bf16[128,1024]{1,0:T(8,128)(2,1)S(1)}, bf16[128,1024]{1,0:T(8,128)(2,1)S(1)}, u32[]{:S(2)}, u32[]{:S(2)}) collective-permute-start(bf16[128,1024]{1,0:T(8,128)(2,1)S(1)} %get-tuple-element.48.refs_3_), channel_id=1, source_target_pairs={{0,1},{1,0},{2,3},{3,2},{4,5},{5,4},{6,7},{7,6},{8,9},{9,8},{10,11... | collective-permute-start | bytes 786440 | tf_op jit(solution)/shard_map/ppermute | solution.py:595
  52.2 7.9 %collective-permute-start.23 = (bf16[128,1024]{1,0:T(8,128)(2,1)S(1)}, bf16[128,1024]{1,0:T(8,128)(2,1)S(1)}, u32[]{:S(2)}, u32[]{:S(2)}) collective-permute-start(bf16[128,1024]{1,0:T(8,128)(2,1)S(1)} %collective-permute-done.11.refs_7_.refs_2_), channel_id=1, source_target_pairs={{0,2},{1,3},{2,0},{3,1},{4,6},{5,7},{6,4},{7,5},{8,10},{9,11},{10,... | collective-permute-start | bytes 786440 | tf_op jit(solution)/shard_map/ppermute | solution.py:595
  52.3 13.3 %collective-permute-start.24 = (bf16[128,1024]{1,0:T(8,128)(2,1)S(1)}, bf16[128,1024]{1,0:T(8,128)(2,1)S(1)}, u32[]{:S(2)}, u32[]{:S(2)}) collective-permute-start(bf16[128,1024]{1,0:T(8,128)(2,1)S(1)} %collective-permute-done.12.refs_8_.refs_3_), channel_id=1, source_target_pairs={{0,2},{1,3},{2,0},{3,1},{4,6},{5,7},{6,4},{7,5},{8,10},{9,11},{10,... | collective-permute-start | bytes 786440 | tf_op jit(solution)/shard_map/ppermute | solution.py:595
  53.6 13.3 %collective-permute-start.13 = (bf16[128,1024]{1,0:T(8,128)(2,1)S(1)}, bf16[128,1024]{1,0:T(8,128)(2,1)S(1)}, u32[]{:S(2)}, u32[]{:S(2)}) collective-permute-start(bf16[128,1024]{1,0:T(8,128)(2,1)S(1)} %collective-permute-done.11.refs_7_.refs_2_), channel_id=1, source_target_pairs={{0,1},{1,0},{2,3},{3,2},{4,5},{5,4},{6,7},{7,6},{8,9},{9,8},{10,11... | collective-permute-start | bytes 786440 | tf_op jit(solution)/shard_map/ppermute | solution.py:595
  54.2 13.7 %collective-permute-start.14 = (bf16[128,1024]{1,0:T(8,128)(2,1)S(1)}, bf16[128,1024]{1,0:T(8,128)(2,1)S(1)}, u32[]{:S(2)}, u32[]{:S(2)}) collective-permute-start(bf16[128,1024]{1,0:T(8,128)(2,1)S(1)} %collective-permute-done.12.refs_8_.refs_3_), channel_id=1, source_target_pairs={{0,1},{1,0},{2,3},{3,2},{4,5},{5,4},{6,7},{7,6},{8,9},{9,8},{10,11... | collective-permute-start | bytes 786440 | tf_op jit(solution)/shard_map/ppermute | solution.py:595
  54.3 13.7 %collective-permute-start.15 = (bf16[128,1024]{1,0:T(8,128)(2,1)S(1)}, bf16[128,1024]{1,0:T(8,128)(2,1)S(1)}, u32[]{:S(2)}, u32[]{:S(2)}) collective-permute-start(bf16[128,1024]{1,0:T(8,128)(2,1)S(1)} %collective-permute-done.11.refs_7_.refs_2_), channel_id=1, source_target_pairs={{4,8},{5,9},{6,10},{7,11},{8,12},{9,13},{10,14},{11,15},{0,0},{1,1... | collective-permute-start | bytes 786440 | tf_op jit(solution)/shard_map/ppermute | solution.py:636
  60.0 9.3 %collective-permute-start.16 = (bf16[128,1024]{1,0:T(8,128)(2,1)S(1)}, bf16[128,1024]{1,0:T(8,128)(2,1)S(1)}, u32[]{:S(2)}, u32[]{:S(2)}) collective-permute-start(bf16[128,1024]{1,0:T(8,128)(2,1)S(1)} %collective-permute-done.12.refs_8_.refs_3_), channel_id=1, source_target_pairs={{4,8},{5,9},{6,10},{7,11},{8,12},{9,13},{10,14},{11,15},{0,0},{1,1... | collective-permute-start | bytes 786440 | tf_op jit(solution)/shard_map/ppermute | solution.py:636
  65.6 11.6 %collective-permute-start.22 = (bf16[256,512]{1,0:T(8,128)(2,1)S(1)}, bf16[256,512]{1,0:T(8,128)(2,1)S(1)}, u32[]{:S(2)}, u32[]{:S(2)}) collective-permute-start(bf16[256,512]{1,0:T(8,128)(2,1)S(1)} %get-tuple-element.46.refs_1_), channel_id=1, source_target_pairs={{12,4},{13,5},{14,6},{15,7},{28,20},{29,21},{30,22},{31,23}} | collective-permute-start | bytes 786440 | tf_op jit(solution)/shard_map/ppermute | solution.py:636
  66.9 10.3 %collective-permute-start.25 = (bf16[128,1024]{1,0:T(8,128)(2,1)S(1)}, bf16[128,1024]{1,0:T(8,128)(2,1)S(1)}, u32[]{:S(2)}, u32[]{:S(2)}) collective-permute-start(bf16[128,1024]{1,0:T(8,128)(2,1)S(1)} %collective-permute-done.23.refs_6_), channel_id=1, source_target_pairs={{0,1},{1,0},{2,3},{3,2},{4,5},{5,4},{6,7},{7,6},{8,9},{9,8},{10,11... | collective-permute-start | bytes 786440 | tf_op jit(solution)/shard_map/ppermute | solution.py:595
  67.9 9.4 %collective-permute-start.26 = (bf16[128,1024]{1,0:T(8,128)(2,1)S(1)}, bf16[128,1024]{1,0:T(8,128)(2,1)S(1)}, u32[]{:S(2)}, u32[]{:S(2)}) collective-permute-start(bf16[128,1024]{1,0:T(8,128)(2,1)S(1)} %collective-permute-done.24.refs_7_), channel_id=1, source_target_pairs={{0,1},{1,0},{2,3},{3,2},{4,5},{5,4},{6,7},{7,6},{8,9},{9,8},{10,11... | collective-permute-start | bytes 786440 | tf_op jit(solution)/shard_map/ppermute | solution.py:595
  68.0 15.2 %collective-permute-start.17 = (bf16[128,1024]{1,0:T(8,128)(2,1)S(1)}, bf16[128,1024]{1,0:T(8,128)(2,1)S(1)}, u32[]{:S(2)}, u32[]{:S(2)}) collective-permute-start(bf16[128,1024]{1,0:T(8,128)(2,1)S(1)} %collective-permute-done.15.refs_5_), channel_id=1, source_target_pairs={{0,1},{1,0},{2,3},{3,2},{4,5},{5,4},{6,7},{7,6},{8,9},{9,8},{10,11... | collective-permute-start | bytes 786440 | tf_op jit(solution)/shard_map/ppermute | solution.py:595
  69.3 13.8 %collective-permute-start.18 = (bf16[128,1024]{1,0:T(8,128)(2,1)S(1)}, bf16[128,1024]{1,0:T(8,128)(2,1)S(1)}, u32[]{:S(2)}, u32[]{:S(2)}) collective-permute-start(bf16[128,1024]{1,0:T(8,128)(2,1)S(1)} %collective-permute-done.16.refs_6_), channel_id=1, source_target_pairs={{0,1},{1,0},{2,3},{3,2},{4,5},{5,4},{6,7},{7,6},{8,9},{9,8},{10,11... | collective-permute-start | bytes 786440 | tf_op jit(solution)/shard_map/ppermute | solution.py:595
  81.3 17.0 %collective-permute-start.27 = (bf16[256,512]{1,0:T(8,128)(2,1)S(1)}, bf16[256,512]{1,0:T(8,128)(2,1)S(1)}, u32[]{:S(2)}, u32[]{:S(2)}) collective-permute-start(bf16[256,512]{1,0:T(8,128)(2,1)S(1)} %get-tuple-element.56), channel_id=1, source_target_pairs={{4,12},{5,13},{6,14},{7,15},{20,28},{21,29},{22,30},{23,31}} | collective-permute-start | bytes 786440 | tf_op jit(solution)/shard_map/ppermute | solution.py:636
  90.8 7.4 %collective-permute-start.19 = (bf16[256,512]{1,0:T(8,128)(2,1)S(1)}, bf16[256,512]{1,0:T(8,128)(2,1)S(1)}, u32[]{:S(2)}, u32[]{:S(2)}) collective-permute-start(bf16[256,512]{1,0:T(8,128)(2,1)S(1)} %get-tuple-element.54), channel_id=1, source_target_pairs={{0,2},{1,3},{2,0},{3,1},{4,6},{5,7},{6,4},{7,5},{8,10},{9,11},{10,... | collective-permute-start | bytes 786440 | tf_op jit(solution)/shard_map/ppermute | solution.py:595
  92.4 5.9 %collective-permute-start.20 = (f32[8,256]{1,0:T(8,128)S(1)}, f32[8,256]{1,0:T(8,128)S(1)}, u32[]{:S(2)}, u32[]{:S(2)}) collective-permute-start(f32[8,256]{1,0:T(8,128)S(1)} %get-tuple-element.55), channel_id=1, source_target_pairs={{0,2},{1,3},{2,0},{3,1},{4,6},{5,7},{6,4},{7,5},{8,10},{9,11},{10,... | collective-permute-start | bytes 24584 | tf_op jit(solution)/shard_map/ppermute | solution.py:595
  (17 other events, 220.6 us)

commit v5 on v4

--- a/solution.py
+++ b/solution.py
@@ -441,47 +441,46 @@
         each_live(frames, f, index, act)
 
 
-def attend_kernel(frames, blocks, groups, first, last, assist, *refs):
+def attend_kernel(frames, blocks, row, first, last, assist, *refs):
     if assist is None:
         live, refs = refs[0], refs[1:]
     else:
         index, live, refs = refs[0], refs[-1], refs[1:-1]
-        list_assist(frames, *assist, index, live)
-    asked, refs = refs[:groups], refs[groups:]
+    q_ref, refs = refs[0], refs[1:]
     if not first:
-        acc_in, stat_in = refs[:2]
-        refs = refs[2:]
+        acc_in, top_in, sum_in = refs[:3]
+        refs = refs[3:]
     kv, refs = refs[:blocks], refs[blocks:]
-    if last:
-        outs, refs = refs[: 2 * groups], refs[2 * groups :]
-    else:
-        acc_out, stat_out = refs[:2]
-        refs = refs[2:]
-    scores, stat = refs
+    outs, (scores, stat) = refs[:-2], refs[-2:]
     rows = frames * P_SIZE
     scale = MD**-0.5
     base2 = scale * 1.4426950408889634
     pairs = [range(i, min(i + 2, blocks)) for i in range(0, blocks, 2)]
     spans = [slice(f * P_SIZE, (f + 1) * P_SIZE) for f in range(frames)]
-    for g in range(groups):
-        held = slice(g * rows, (g + 1) * rows)
-        stat[...] = jnp.zeros_like(stat) if first else stat_in[held, :]
+
+    def run():
+        if assist is not None:
+            list_assist(frames, *assist, index, live)
+        lane = lax.broadcasted_iota(jnp.int32, (rows, 128), 1)
+        if last:
+            stat[...] = jnp.zeros_like(stat)
         for e in range(MH):
             cols, vcols = slice(e * MD, (e + 1) * MD), slice(MC + e * MD, MC + (e + 1) * MD)
-            q = asked[g][:, cols]
+            held = slice(e * rows, (e + 1) * rows)
+            q = q_ref[:, cols]
             tops = [None] * frames
             for pair in pairs:
                 s = nt(q, jnp.concatenate([kv[b][:, cols] for b in pair], axis=0))
                 for j, b in enumerate(pair):
                     for f in range(frames):
                         part = s[spans[f], j * P_SIZE : (j + 1) * P_SIZE]
-                        part = jnp.where(live[g * frames + f, b] == 1, part, NEG)
+                        part = jnp.where(live[row + f, b] == 1, part, NEG)
                         scores[spans[f], b * P_SIZE : (b + 1) * P_SIZE] = part
                         tops[f] = part if tops[f] is None else jnp.maximum(tops[f], part)
             top = jnp.concatenate([jnp.max(t, axis=1, keepdims=True) for t in tops], axis=0)
-            top = jnp.maximum(top, 0.1 * NEG)
+            top = jnp.broadcast_to(jnp.maximum(top, 0.1 * NEG), (rows, 128))
             if not first:
-                before = stat[:, e : e + 1]
+                before = top_in[held, :]
                 top = jnp.maximum(top, before)
                 fade = jnp.exp2((before - top) * base2)
             total, acc = None, None
@@ -496,57 +495,60 @@
                     jnp.concatenate([kv[b][:, vcols] for b in pair], axis=0),
                 )
                 acc = part if acc is None else acc + part
-            total = jnp.sum(total, axis=1, keepdims=True)
             if not first:
-                total = total + fade * stat[:, MH + e : MH + e + 1]
-                acc = acc + fade * acc_in[held, cols]
-            stat[:, e : e + 1] = top
-            stat[:, MH + e : MH + e + 1] = total
+                total = total + fade * sum_in[held, :]
+                acc = acc + fade * acc_in[:, cols]
             if last:
-                outs[2 * g][:, cols] = (acc / jnp.maximum(total, 1e-30)).astype(outs[2 * g].dtype)
+                whole = jnp.broadcast_to(jnp.sum(total, axis=1, keepdims=True), (rows, 128))
+                whole = jnp.maximum(whole, 1e-30)
+                outs[0][:, cols] = (acc / whole).astype(outs[0].dtype)
+                stat[...] = jnp.where(
+                    lane == e, top, jnp.where(lane == MH + e, whole, stat[...])
+                )
             else:
-                acc_out[held, cols] = acc
+                outs[0][:, cols] = acc
+                outs[1][held, :] = top
+                outs[2][held, :] = total
         if last:
             flat = jnp.transpose(stat[...])
-            low = jnp.log(jnp.maximum(flat[MH : 2 * MH], 1e-30))
-            outs[2 * g + 1][...] = jnp.concatenate([flat[:MH] * scale + low, low], axis=0)
-        else:
-            stat_out[held, :] = stat[...]
-
-
-def attend(lists, asked, kvs, state, last, assist=None):
-    rows = asked[0].shape[0]
+            low = jnp.log(flat[MH : 2 * MH])
+            outs[1][...] = jnp.concatenate([flat[:MH] * scale + low, low], axis=0)
+
+    if assist is None:
+        run()
+    else:
+        _, steps, planes = assist
+        plane = lax.axis_index("tm") // LANES
+        pl.when((plane >= 1) & (plane + steps < planes))(run)
+
+
+def attend(lists, row, asked, kvs, state, last, dtype, assist=None):
+    rows = asked.shape[0]
     frames = rows // P_SIZE
     blocks = len(kvs)
-    groups = len(asked)
     first = state is None
     state = [] if first else list(state)
-    out_shape = []
     if last:
-        for g in range(groups):
-            stays = g == 0 and assist is None
-            out_shape += [
-                jax.ShapeDtypeStruct((rows, MC), F32 if stays else BF16),
-                jax.ShapeDtypeStruct((2 * MH, rows), F32),
-            ]
+        out_shape = [
+            jax.ShapeDtypeStruct((rows, MC), dtype),
+            jax.ShapeDtypeStruct((2 * MH, rows), F32),
+        ]
     else:
-        out_shape = [
-            jax.ShapeDtypeStruct((groups * rows, MC), F32),
-            jax.ShapeDtypeStruct((groups * rows, 128), F32),
-        ]
+        out_shape = [jax.ShapeDtypeStruct((rows, MC), F32)]
+        out_shape += [jax.ShapeDtypeStruct((MH * rows, 128), F32)] * 2
     scratch = [pltpu.VMEM((rows, blocks * P_SIZE), F32), pltpu.VMEM((rows, 128), F32)]
     if assist is not None:
         scratch.append(pltpu.SMEM((frames, blocks), jnp.int32))
     return pl.pallas_call(
-        functools.partial(attend_kernel, frames, blocks, groups, first, last, assist),
-        in_specs=[SMEM] + [VMEM] * (groups + len(state) + blocks),
+        functools.partial(attend_kernel, frames, blocks, row, first, last, assist),
+        in_specs=[SMEM] + [VMEM] * (1 + len(state) + blocks),
         out_specs=[VMEM] * len(out_shape),
         out_shape=out_shape,
         scratch_shapes=scratch,
         compiler_params=params(),
-        cost_estimate=cost(4 * groups * blocks * rows * P_SIZE * MC, blocks * P_SIZE * MC * 4),
+        cost_estimate=cost(4 * blocks * rows * P_SIZE * MC, blocks * P_SIZE * MC * 4),
         name="assist" if assist is not None else "attend_last" if last else "attend",
-    )(lists, *asked, *state, *kvs)
+    )(lists, asked, *state, *kvs)
 
 
 def output_kernel(parts, steps, *refs):
@@ -590,6 +592,7 @@
 ):
     size = lax.axis_size("tm")
     planes = size // LANES
+    frames = tokens.shape[0] // P_SIZE
 
     def flip(x, bits):
         return lax.ppermute(x, "tm", [(i, i ^ bits) for i in range(size)])
@@ -641,6 +644,7 @@
         pairs = [(p, p + 1) for p in range(distance - 1, planes - 1)]
         return between(x, pairs + [(p, p) for p in range(distance - 1)] + [(planes - 1, distance - 1)])
 
+    frames = len(kv)
     partner_q = flip(q, 2)
     held, across = [], []
     for distance in range(steps + 1):
@@ -660,15 +664,20 @@
         far_pack = between(pack, down)
         far = None
         for at, blocks in enumerate(across, 1):
-            far = attend(far_pack, [far_q], blocks, far, at == reach, (at, steps, planes))
+            far = attend(far_pack, 0, far_q, blocks, far, at == reach, BF16, (at, steps, planes))
         parts = [[between(x, helped) for x in far]]
-    state = None
-    for (low, high), table in zip(spans, tables):
-        blocks = [x for group in held[low:high] for x in group]
-        state = attend(table, [q, partner_q], blocks, state, high == steps + 1)
-    o, lse, po, plse = state
-    back = [flip(po, 2), flip(plse, 2)]
-    return output([[o, lse], back] + parts, hid, w_out, steps)
+
+    def attended(row, asked, dtype):
+        state = None
+        for (low, high), flags in zip(spans, tables):
+            blocks = [x for group in held[low:high] for x in group]
+            state = attend(flags, row, asked, blocks, state, high == steps + 1, dtype)
+        return state
+
+    theirs = attended(frames, partner_q, BF16)
+    back = [flip(x, 2) for x in theirs]
+    mine = attended(0, q, F32)
+    return output([mine, back] + parts, hid, w_out, steps)
 
 
 def spans_of(steps):

time: 101 us -> 93.6 us (0.927)
  waiting for transfers between devices: 33.3 us -> 25 us
  starting transfers between devices: 32.5 us -> 34.8 us
  Pallas kernels: 29.5 us -> 27.3 us
    ppermute x18, waiting for transfers between devices: 20.4 us -> 10.2 us  [flip(): return lax.ppermute(x, 'tm', [(i, i ^ bits) for i in range(size)])]
    pallas_call x3 -> x5, Pallas kernels: 17.4 us -> 15.2 us  [attend(): pl.pallas_call(functools.partial(attend_kernel, frames, blocks, row, firs...]
    ppermute x8, starting transfers between devices: 12 us -> 14 us  [between(): lax.ppermute(x, 'tm', [(a * LANES + i, b * LANES + i) for a, b in pairs f...]
    ppermute x8, waiting for transfers between devices: 8.24 us -> 10.1 us  [between(): lax.ppermute(x, 'tm', [(a * LANES + i, b * LANES + i) for a, b in pairs f...]
    unnamed x24 -> x26, local copies, waits for them, and re-layouts: 4.5 us -> 4.5 us
where the time goes in v5:
time: 93.6 us; the launch traced here: 91.9 us
  starting transfers between devices  34.8 us (37%)
  Pallas kernels  27.3 us (29%)
  waiting for transfers between devices  25 us (27%)
  local copies, waits for them, and re-layouts  4.5 us (5%)
    ppermute x18, starting transfers between devices, flip(): return lax.ppermute(x, 'tm', [(i, i ^ bits) for i in range(size)])  16.9 us
    pallas_call x5, Pallas kernels, attend(): pl.pallas_call(functools.partial(attend_kernel, frames, blocks, row, firs...  15.2 us
    ppermute x8, starting transfers between devices, between(): lax.ppermute(x, 'tm', [(a * LANES + i, b * LANES + i) for a, b in pairs f...  14 us
    ppermute x18, waiting for transfers between devices, flip(): return lax.ppermute(x, 'tm', [(i, i ^ bits) for i in range(size)])  10.2 us
    ppermute x8, waiting for transfers between devices, between(): lax.ppermute(x, 'tm', [(a * LANES + i, b * LANES + i) for a, b in pairs f...  10.1 us
    ppermute x3, waiting for transfers between devices, up(): return lax.ppermute(x, 'tm', [(i, (i + step) % size) for i in range(size)])  4.7 us
    unnamed x26, local copies, waits for them, and re-layouts  4.5 us
    pallas_call x1, Pallas kernels, local(): pl.pallas_call(local_kernel, in_specs=[HBM] * 6, out_specs=[VMEM] * 4 + [...  3.94 us
  transfers between devices with their start and end apart: 29, of which 11 were waited for; matrix products, arithmetic and copies ran while one was open for 0% of the time, Pallas kernels for 21%

profile of v5, /device:TPU:13, one launch (start us, length us, event | category | flops | bytes accessed | tf_op | source)
XLA Modules:
  0.0 91.9 jit_solution(16018183444100368473)
XLA Ops:
  0.0 3.9 %local.1 = (bf16[256,512]{1,0:T(8,128)(2,1)}, bf16[256,1024]{1,0:T(8,128)(2,1)}, bf16[2,272,128]{2,1,0:T(8,128)(2,1)}, bf16[2,272,128]{2,1,0:T(8,128)(2,1)}, s32[2,9]{1,0:T(2,128)}) custom-call(bf16[256,1024]{1,0:T(8,128)(2,1)} %refs_4_.1, f32[8,256]{1,0:T(8,128)} %refs_1_.1, bf16[1024,512]{1,0:T(8,128)(2,1)} %wk_in.1, bf16[1024,1024]{1,0:T(8,128)(2,1)} %wv_in.1, ...), custom_call_target="tpu_custom_call" | custom-call | tf_op jit(solution)/shard_map/local/pallas_call | solution.py:174
  7.2 2.9 %collective-permute-done.2.got.refs_1_ = bf16[272,128]{1,0:T(8,128)(2,1)S(1)} collective-permute-done((bf16[272,128]{1,0:T(8,128)(2,1)S(1)}, bf16[272,128]{1,0:T(8,128)(2,1)S(1)}, u32[]{:S(2)}, u32[]{:S(2)}) %collective-permute-start.2) | collective-permute-done | bytes 69664 | tf_op jit(solution)/shard_map/ppermute | solution.py:598
  14.1 1.9 %collective-permute-done.4.refs_3_ = bf16[272,128]{1,0:T(8,128)(2,1)S(1)} collective-permute-done((bf16[272,128]{1,0:T(8,128)(2,1)S(1)}, bf16[272,128]{1,0:T(8,128)(2,1)S(1)}, u32[]{:S(2)}, u32[]{:S(2)}) %collective-permute-start.4) | collective-permute-done | bytes 69664 | tf_op jit(solution)/shard_map/ppermute | solution.py:602
  15.9 2.8 %collective-permute-done.5.refs_4_ = bf16[272,128]{1,0:T(8,128)(2,1)S(1)} collective-permute-done((bf16[272,128]{1,0:T(8,128)(2,1)S(1)}, bf16[272,128]{1,0:T(8,128)(2,1)S(1)}, u32[]{:S(2)}, u32[]{:S(2)}) %collective-permute-start.5) | collective-permute-done | bytes 69664 | tf_op jit(solution)/shard_map/ppermute | solution.py:602
  20.0 2.0 %collective-permute-done.6.got = bf16[256,128]{1,0:T(8,128)(2,1)S(1)} collective-permute-done((bf16[256,128]{1,0:T(8,128)(2,1)S(1)}, bf16[256,128]{1,0:T(8,128)(2,1)S(1)}, u32[]{:S(2)}, u32[]{:S(2)}) %collective-permute-start.6) | collective-permute-done | bytes 65568 | tf_op jit(solution)/shard_map/ppermute | solution.py:598
  23.1 2.7 %collective-permute-start.7 = (bf16[2,256,128]{2,1,0:T(8,128)(2,1)S(1)}, bf16[2,256,128]{2,1,0:T(8,128)(2,1)S(1)}, u32[]{:S(2)}, u32[]{:S(2)}) collective-permute-start(bf16[2,256,128]{2,1,0:T(8,128)(2,1)S(1)} %get-tuple-element.49), channel_id=1, source_target_pairs={{0,1},{1,0},{2,3},{3,2},{4,5},{5,4},{6,7},{7,6},{8,9},{9,8},{10,11... | collective-permute-start | bytes 393224 | tf_op jit(solution)/shard_map/ppermute | solution.py:598
  26.2 2.2 %collective-permute-done.refs_5_ = s32[2,9]{1,0:T(2,128)S(1)} collective-permute-done((s32[2,9]{1,0:T(2,128)}, s32[2,9]{1,0:T(2,128)S(1)}, u32[]{:S(2)}, u32[]{:S(2)}) %collective-permute-start) | collective-permute-done | bytes 104 | tf_op jit(solution)/shard_map/ppermute | solution.py:598
  31.0 3.7 %inner.1 = (f32[256,1024]{1,0:T(8,128)S(1)}, bf16[256,1024]{1,0:T(8,128)(2,1)S(1)}, s32[4,8]{1,0:T(4,128)S(1)}, s32[4,4]{1,0:T(4,128)S(1)}) custom-call(bf16[256,1024]{1,0:T(8,128)(2,1)S(1)} %copy-done, f32[8,256]{1,0:T(8,128)S(1)} %copy-done.9, bf16[256,512]{1,0:T(8,128)(2,1)S(1)} %copy-done.8, bf16[256,1024]{1,0:T(8,128)(2,1)S(1)} %copy-done.7, ...), custom_call_target="tpu_custom_call" | custom-call | flops 268435456 | bytes 8388608 | tf_op jit(solution)/shard_map/inner/pallas_call | solution.py:289
  34.8 2.2 %hidden.1 = (bf16[256,1024]{1,0:T(8,128)(2,1)S(1)}, bf16[256,512]{1,0:T(8,128)(2,1)S(1)}, bf16[128,1024]{1,0:T(8,128)(2,1)S(1)}, bf16[128,1024]{1,0:T(8,128)(2,1)S(1)}) custom-call(f32[256,1024]{1,0:T(8,128)S(1)} %get-tuple-element.40.refs_0_, bf16[256,1024]{1,0:T(8,128)(2,1)S(1)} %get-tuple-element.41.refs_1_, ...), custom_call_target="tpu_custom_call" | custom-call | tf_op jit(solution)/shard_map/hidden/pallas_call | solution.py:414
  38.4 2.5 %collective-permute-start.11 = (bf16[128,1024]{1,0:T(8,128)(2,1)S(1)}, bf16[128,1024]{1,0:T(8,128)(2,1)S(1)}, u32[]{:S(2)}, u32[]{:S(2)}) collective-permute-start(bf16[128,1024]{1,0:T(8,128)(2,1)S(1)} %get-tuple-element.53.refs_3_), channel_id=1, source_target_pairs={{0,4},{1,5},{2,6},{3,7},{4,8},{5,9},{6,10},{7,11},{8,12},{9,13},{1... | collective-permute-start | bytes 786440 | tf_op jit(solution)/shard_map/ppermute | solution.py:639
  41.4 2.4 %collective-permute-done.10.refs_6_.refs_2_ = bf16[128,1024]{1,0:T(8,128)(2,1)S(1)} collective-permute-done((bf16[128,1024]{1,0:T(8,128)(2,1)S(1)}, bf16[128,1024]{1,0:T(8,128)(2,1)S(1)}, u32[]{:S(2)}, u32[]{:S(2)}) %collective-permute-start.10) | collective-permute-done | bytes 262176 | tf_op jit(solution)/shard_map/ppermute | solution.py:639
  43.8 3.5 %collective-permute-start.12 = (bf16[128,1024]{1,0:T(8,128)(2,1)S(1)}, bf16[128,1024]{1,0:T(8,128)(2,1)S(1)}, u32[]{:S(2)}, u32[]{:S(2)}) collective-permute-start(bf16[128,1024]{1,0:T(8,128)(2,1)S(1)} %collective-permute-done.10.refs_6_.refs_2_), channel_id=1, source_target_pairs={{0,1},{1,0},{2,3},{3,2},{4,5},{5,4},{6,7},{7,6},{8,9},{9,8},{10,11... | collective-permute-start | bytes 786440 | tf_op jit(solution)/shard_map/ppermute | solution.py:598
  47.3 2.1 %collective-permute-start.14 = (bf16[128,1024]{1,0:T(8,128)(2,1)S(1)}, bf16[128,1024]{1,0:T(8,128)(2,1)S(1)}, u32[]{:S(2)}, u32[]{:S(2)}) collective-permute-start(bf16[128,1024]{1,0:T(8,128)(2,1)S(1)} %collective-permute-done.10.refs_6_.refs_2_), channel_id=1, source_target_pairs={{4,8},{5,9},{6,10},{7,11},{8,12},{9,13},{10,14},{11,15},{0,0},{1,1... | collective-permute-start | bytes 786440 | tf_op jit(solution)/shard_map/ppermute | solution.py:639
  49.5 4.1 %collective-permute-start.15 = (bf16[128,1024]{1,0:T(8,128)(2,1)S(1)}, bf16[128,1024]{1,0:T(8,128)(2,1)S(1)}, u32[]{:S(2)}, u32[]{:S(2)}) collective-permute-start(bf16[128,1024]{1,0:T(8,128)(2,1)S(1)} %collective-permute-done.11.refs_7_.refs_3_), channel_id=1, source_target_pairs={{4,8},{5,9},{6,10},{7,11},{8,12},{9,13},{10,14},{11,15},{0,0},{1,1... | collective-permute-start | bytes 786440 | tf_op jit(solution)/shard_map/ppermute | solution.py:639
  55.7 2.3 %collective-permute-done.14.refs_5_ = bf16[128,1024]{1,0:T(8,128)(2,1)S(1)} collective-permute-done((bf16[128,1024]{1,0:T(8,128)(2,1)S(1)}, bf16[128,1024]{1,0:T(8,128)(2,1)S(1)}, u32[]{:S(2)}, u32[]{:S(2)}) %collective-permute-start.14) | collective-permute-done | bytes 262176 | tf_op jit(solution)/shard_map/ppermute | solution.py:639
  59.3 4.3 %collective-permute-done.15.refs_6_ = bf16[128,1024]{1,0:T(8,128)(2,1)S(1)} collective-permute-done((bf16[128,1024]{1,0:T(8,128)(2,1)S(1)}, bf16[128,1024]{1,0:T(8,128)(2,1)S(1)}, u32[]{:S(2)}, u32[]{:S(2)}) %collective-permute-start.15) | collective-permute-done | bytes 262176 | tf_op jit(solution)/shard_map/ppermute | solution.py:639
  65.8 1.8 %collective-permute-done.24.refs_7_ = bf16[128,1024]{1,0:T(8,128)(2,1)S(1)} collective-permute-done((bf16[128,1024]{1,0:T(8,128)(2,1)S(1)}, bf16[128,1024]{1,0:T(8,128)(2,1)S(1)}, u32[]{:S(2)}, u32[]{:S(2)}) %collective-permute-start.24) | collective-permute-done | bytes 262176 | tf_op jit(solution)/shard_map/ppermute | solution.py:598
  68.6 3.2 %attend.3 = (f32[256,512]{1,0:T(8,128)S(1)}, f32[1024,128]{1,0:T(8,128)S(1)}, f32[1024,128]{1,0:T(8,128)S(1)}) custom-call(s32[4,8]{1,0:T(4,128)S(1)} %get-tuple-element.51.refs_0_, bf16[256,512]{1,0:T(8,128)(2,1)S(1)} %collective-permute-done.18.refs_1_, bf16[128,1024]{1,0:T(8,128)(2,1)S(1)} %get-tuple-element.52.refs_2_, ...), custom_call_target="tpu_custom_call" | custom-call | flops 536870912 | bytes 2097152 | tf_op jit(solution)/shard_map/attend/pallas_call | solution.py:542
  73.1 2.5 %attend_last.3 = (bf16[256,512]{1,0:T(8,128)(2,1)S(1)}, f32[8,256]{1,0:T(8,128)S(1)}) custom-call(s32[4,4]{1,0:T(4,128)S(1)} %get-tuple-element.39.refs_0_, bf16[256,512]{1,0:T(8,128)(2,1)S(1)} %collective-permute-done.18.refs_1_, f32[256,512]{1,0:T(8,128)S(1)} %get-tuple-element.59.refs_2_, f32[1024,128]{1,0:T(8,128)S(1)} %get-tuple-element.60.refs_3_, ...), custom_call_target="tpu_custom_call" | custom-call | flops 268435456 | bytes 1048576 | tf_op jit(solution)/shard_map/attend_last/pallas_call | solution.py:542
  77.0 3.9 %assist.1 = (bf16[256,512]{1,0:T(8,128)(2,1)S(1)}, f32[8,256]{1,0:T(8,128)S(1)}) custom-call(s32[2,9]{1,0:T(2,128)S(1)} %collective-permute-done.21.refs_0_, bf16[256,512]{1,0:T(8,128)(2,1)S(1)} %collective-permute-done.22.refs_1_, bf16[128,1024]{1,0:T(8,128)(2,1)S(1)} %collective-permute-done.10.refs_6_.refs_2_, ...), custom_call_target="tpu_custom_call" | custom-call | flops 536870912 | bytes 2097152 | tf_op jit(solution)/shard_map/assist/pallas_call | solution.py:542
  80.9 1.4 %collective-permute-start.27 = (bf16[256,512]{1,0:T(8,128)(2,1)S(1)}, bf16[256,512]{1,0:T(8,128)(2,1)S(1)}, u32[]{:S(2)}, u32[]{:S(2)}) collective-permute-start(bf16[256,512]{1,0:T(8,128)(2,1)S(1)} %get-tuple-element.64), channel_id=1, source_target_pairs={{4,12},{5,13},{6,14},{7,15},{20,28},{21,29},{22,30},{23,31}} | collective-permute-start | bytes 786440 | tf_op jit(solution)/shard_map/ppermute | solution.py:639
  82.3 3.2 %attend.2 = (f32[256,512]{1,0:T(8,128)S(1)}, f32[1024,128]{1,0:T(8,128)S(1)}, f32[1024,128]{1,0:T(8,128)S(1)}) custom-call(s32[4,8]{1,0:T(4,128)S(1)} %get-tuple-element.51.refs_0_, bf16[256,512]{1,0:T(8,128)(2,1)S(1)} %get-tuple-element.50.refs_1_, bf16[128,1024]{1,0:T(8,128)(2,1)S(1)} %get-tuple-element.52.refs_2_, ...), custom_call_target="tpu_custom_call" | custom-call | flops 536870912 | bytes 2097152 | tf_op jit(solution)/shard_map/attend/pallas_call | solution.py:542
  87.5 2.5 %attend_last.2 = (f32[256,512]{1,0:T(8,128)S(1)}, f32[8,256]{1,0:T(8,128)S(1)}) custom-call(s32[4,4]{1,0:T(4,128)S(1)} %get-tuple-element.39.refs_0_, bf16[256,512]{1,0:T(8,128)(2,1)S(1)} %get-tuple-element.50.refs_1_, f32[256,512]{1,0:T(8,128)S(1)} %get-tuple-element.54.refs_2_, f32[1024,128]{1,0:T(8,128)S(1)} %get-tuple-element.55.refs_3_, ...), custom_call_target="tpu_custom_call" | custom-call | flops 268435456 | bytes 1048576 | tf_op jit(solution)/shard_map/attend_last/pallas_call | solution.py:542
  90.0 1.9 %output.1 = bf16[256,1024]{1,0:T(8,128)(2,1)} custom-call(f32[256,512]{1,0:T(8,128)S(1)} %get-tuple-element.57.refs_0_, f32[8,256]{1,0:T(8,128)S(1)} %get-tuple-element.58.refs_1_, bf16[256,512]{1,0:T(8,128)(2,1)S(1)} %collective-permute-done.19.refs_2_, f32[8,256]{1,0:T(8,128)S(1)} %collective-permute-done.20.refs_3_, ...), custom_call_target="tpu_custom_call" | custom-call | tf_op jit(solution)/shard_map/output/pallas_call | solution.py:579
  (73 shorter events, 25.7 us)
Async XLA Ops:
  10.2 3.8 %collective-permute-start.3 = (bf16[272,128]{1,0:T(8,128)(2,1)S(1)}, bf16[272,128]{1,0:T(8,128)(2,1)S(1)}, u32[]{:S(2)}, u32[]{:S(2)}) collective-permute-start(bf16[272,128]{1,0:T(8,128)(2,1)S(1)} %shard_map.119), channel_id=1, source_target_pairs={{0,4},{1,5},{2,6},{3,7},{4,8},{5,9},{6,10},{7,11},{8,12},{9,13},{1... | collective-permute-start | bytes 208904 | tf_op jit(solution)/shard_map/ppermute | solution.py:602
  11.6 4.3 %collective-permute-start.4 = (bf16[272,128]{1,0:T(8,128)(2,1)S(1)}, bf16[272,128]{1,0:T(8,128)(2,1)S(1)}, u32[]{:S(2)}, u32[]{:S(2)}) collective-permute-start(bf16[272,128]{1,0:T(8,128)(2,1)S(1)} %shard_map.119), channel_id=1, source_target_pairs={{0,8},{1,9},{2,10},{3,11},{4,12},{5,13},{6,14},{7,15},{8,0},{9,1},... | collective-permute-start | bytes 208904 | tf_op jit(solution)/shard_map/ppermute | solution.py:602
  12.7 6.1 %collective-permute-start.5 = (bf16[272,128]{1,0:T(8,128)(2,1)S(1)}, bf16[272,128]{1,0:T(8,128)(2,1)S(1)}, u32[]{:S(2)}, u32[]{:S(2)}) collective-permute-start(bf16[272,128]{1,0:T(8,128)(2,1)S(1)} %shard_map.119), channel_id=1, source_target_pairs={{0,12},{1,13},{2,14},{3,15},{4,0},{5,1},{6,2},{7,3},{8,4},{9,5},{1... | collective-permute-start | bytes 208904 | tf_op jit(solution)/shard_map/ppermute | solution.py:602
  23.1 11.7 %collective-permute-start.7 = (bf16[2,256,128]{2,1,0:T(8,128)(2,1)S(1)}, bf16[2,256,128]{2,1,0:T(8,128)(2,1)S(1)}, u32[]{:S(2)}, u32[]{:S(2)}) collective-permute-start(bf16[2,256,128]{2,1,0:T(8,128)(2,1)S(1)} %get-tuple-element.49), channel_id=1, source_target_pairs={{0,1},{1,0},{2,3},{3,2},{4,5},{5,4},{6,7},{7,6},{8,9},{9,8},{10,11... | collective-permute-start | bytes 393224 | tf_op jit(solution)/shard_map/ppermute | solution.py:598
  37.0 6.8 %collective-permute-start.10 = (bf16[128,1024]{1,0:T(8,128)(2,1)S(1)}, bf16[128,1024]{1,0:T(8,128)(2,1)S(1)}, u32[]{:S(2)}, u32[]{:S(2)}) collective-permute-start(bf16[128,1024]{1,0:T(8,128)(2,1)S(1)} %get-tuple-element.52.refs_2_), channel_id=1, source_target_pairs={{0,4},{1,5},{2,6},{3,7},{4,8},{5,9},{6,10},{7,11},{8,12},{9,13},{1... | collective-permute-start | bytes 786440 | tf_op jit(solution)/shard_map/ppermute | solution.py:639
  37.1 10.3 %collective-permute-start.8 = (bf16[128,1024]{1,0:T(8,128)(2,1)S(1)}, bf16[128,1024]{1,0:T(8,128)(2,1)S(1)}, u32[]{:S(2)}, u32[]{:S(2)}) collective-permute-start(bf16[128,1024]{1,0:T(8,128)(2,1)S(1)} %get-tuple-element.52.refs_2_), channel_id=1, source_target_pairs={{0,1},{1,0},{2,3},{3,2},{4,5},{5,4},{6,7},{7,6},{8,9},{9,8},{10,11... | collective-permute-start | bytes 786440 | tf_op jit(solution)/shard_map/ppermute | solution.py:598
  38.4 11.1 %collective-permute-start.11 = (bf16[128,1024]{1,0:T(8,128)(2,1)S(1)}, bf16[128,1024]{1,0:T(8,128)(2,1)S(1)}, u32[]{:S(2)}, u32[]{:S(2)}) collective-permute-start(bf16[128,1024]{1,0:T(8,128)(2,1)S(1)} %get-tuple-element.53.refs_3_), channel_id=1, source_target_pairs={{0,4},{1,5},{2,6},{3,7},{4,8},{5,9},{6,10},{7,11},{8,12},{9,13},{1... | collective-permute-start | bytes 786440 | tf_op jit(solution)/shard_map/ppermute | solution.py:639
  40.9 12.7 %collective-permute-start.9 = (bf16[128,1024]{1,0:T(8,128)(2,1)S(1)}, bf16[128,1024]{1,0:T(8,128)(2,1)S(1)}, u32[]{:S(2)}, u32[]{:S(2)}) collective-permute-start(bf16[128,1024]{1,0:T(8,128)(2,1)S(1)} %get-tuple-element.53.refs_3_), channel_id=1, source_target_pairs={{0,1},{1,0},{2,3},{3,2},{4,5},{5,4},{6,7},{7,6},{8,9},{9,8},{10,11... | collective-permute-start | bytes 786440 | tf_op jit(solution)/shard_map/ppermute | solution.py:598
  41.1 13.1 %collective-permute-start.18 = (bf16[256,512]{1,0:T(8,128)(2,1)S(1)}, bf16[256,512]{1,0:T(8,128)(2,1)S(1)}, u32[]{:S(2)}, u32[]{:S(2)}) collective-permute-start(bf16[256,512]{1,0:T(8,128)(2,1)S(1)} %get-tuple-element.50.refs_1_), channel_id=1, source_target_pairs={{0,2},{1,3},{2,0},{3,1},{4,6},{5,7},{6,4},{7,5},{8,10},{9,11},{10,... | collective-permute-start | bytes 786440 | tf_op jit(solution)/shard_map/ppermute | solution.py:598
  43.8 10.7 %collective-permute-start.12 = (bf16[128,1024]{1,0:T(8,128)(2,1)S(1)}, bf16[128,1024]{1,0:T(8,128)(2,1)S(1)}, u32[]{:S(2)}, u32[]{:S(2)}) collective-permute-start(bf16[128,1024]{1,0:T(8,128)(2,1)S(1)} %collective-permute-done.10.refs_6_.refs_2_), channel_id=1, source_target_pairs={{0,1},{1,0},{2,3},{3,2},{4,5},{5,4},{6,7},{7,6},{8,9},{9,8},{10,11... | collective-permute-start | bytes 786440 | tf_op jit(solution)/shard_map/ppermute | solution.py:598
  47.3 10.6 %collective-permute-start.14 = (bf16[128,1024]{1,0:T(8,128)(2,1)S(1)}, bf16[128,1024]{1,0:T(8,128)(2,1)S(1)}, u32[]{:S(2)}, u32[]{:S(2)}) collective-permute-start(bf16[128,1024]{1,0:T(8,128)(2,1)S(1)} %collective-permute-done.10.refs_6_.refs_2_), channel_id=1, source_target_pairs={{4,8},{5,9},{6,10},{7,11},{8,12},{9,13},{10,14},{11,15},{0,0},{1,1... | collective-permute-start | bytes 786440 | tf_op jit(solution)/shard_map/ppermute | solution.py:639
  49.5 14.1 %collective-permute-start.15 = (bf16[128,1024]{1,0:T(8,128)(2,1)S(1)}, bf16[128,1024]{1,0:T(8,128)(2,1)S(1)}, u32[]{:S(2)}, u32[]{:S(2)}) collective-permute-start(bf16[128,1024]{1,0:T(8,128)(2,1)S(1)} %collective-permute-done.11.refs_7_.refs_3_), channel_id=1, source_target_pairs={{4,8},{5,9},{6,10},{7,11},{8,12},{9,13},{10,14},{11,15},{0,0},{1,1... | collective-permute-start | bytes 786440 | tf_op jit(solution)/shard_map/ppermute | solution.py:639
  53.6 10.8 %collective-permute-start.13 = (bf16[128,1024]{1,0:T(8,128)(2,1)S(1)}, bf16[128,1024]{1,0:T(8,128)(2,1)S(1)}, u32[]{:S(2)}, u32[]{:S(2)}) collective-permute-start(bf16[128,1024]{1,0:T(8,128)(2,1)S(1)} %collective-permute-done.11.refs_7_.refs_3_), channel_id=1, source_target_pairs={{0,1},{1,0},{2,3},{3,2},{4,5},{5,4},{6,7},{7,6},{8,9},{9,8},{10,11... | collective-permute-start | bytes 786440 | tf_op jit(solution)/shard_map/ppermute | solution.py:598
  54.2 11.5 %collective-permute-start.23 = (bf16[128,1024]{1,0:T(8,128)(2,1)S(1)}, bf16[128,1024]{1,0:T(8,128)(2,1)S(1)}, u32[]{:S(2)}, u32[]{:S(2)}) collective-permute-start(bf16[128,1024]{1,0:T(8,128)(2,1)S(1)} %collective-permute-done.10.refs_6_.refs_2_), channel_id=1, source_target_pairs={{0,2},{1,3},{2,0},{3,1},{4,6},{5,7},{6,4},{7,5},{8,10},{9,11},{10,... | collective-permute-start | bytes 786440 | tf_op jit(solution)/shard_map/ppermute | solution.py:598
  54.5 13.2 %collective-permute-start.24 = (bf16[128,1024]{1,0:T(8,128)(2,1)S(1)}, bf16[128,1024]{1,0:T(8,128)(2,1)S(1)}, u32[]{:S(2)}, u32[]{:S(2)}) collective-permute-start(bf16[128,1024]{1,0:T(8,128)(2,1)S(1)} %collective-permute-done.11.refs_7_.refs_3_), channel_id=1, source_target_pairs={{0,2},{1,3},{2,0},{3,1},{4,6},{5,7},{6,4},{7,5},{8,10},{9,11},{10,... | collective-permute-start | bytes 786440 | tf_op jit(solution)/shard_map/ppermute | solution.py:598
  58.0 13.8 %collective-permute-start.16 = (bf16[128,1024]{1,0:T(8,128)(2,1)S(1)}, bf16[128,1024]{1,0:T(8,128)(2,1)S(1)}, u32[]{:S(2)}, u32[]{:S(2)}) collective-permute-start(bf16[128,1024]{1,0:T(8,128)(2,1)S(1)} %collective-permute-done.14.refs_5_), channel_id=1, source_target_pairs={{0,1},{1,0},{2,3},{3,2},{4,5},{5,4},{6,7},{7,6},{8,9},{9,8},{10,11... | collective-permute-start | bytes 786440 | tf_op jit(solution)/shard_map/ppermute | solution.py:598
  63.6 9.5 %collective-permute-start.17 = (bf16[128,1024]{1,0:T(8,128)(2,1)S(1)}, bf16[128,1024]{1,0:T(8,128)(2,1)S(1)}, u32[]{:S(2)}, u32[]{:S(2)}) collective-permute-start(bf16[128,1024]{1,0:T(8,128)(2,1)S(1)} %collective-permute-done.15.refs_6_), channel_id=1, source_target_pairs={{0,1},{1,0},{2,3},{3,2},{4,5},{5,4},{6,7},{7,6},{8,9},{9,8},{10,11... | collective-permute-start | bytes 786440 | tf_op jit(solution)/shard_map/ppermute | solution.py:598
  64.4 12.6 %collective-permute-start.22 = (bf16[256,512]{1,0:T(8,128)(2,1)S(1)}, bf16[256,512]{1,0:T(8,128)(2,1)S(1)}, u32[]{:S(2)}, u32[]{:S(2)}) collective-permute-start(bf16[256,512]{1,0:T(8,128)(2,1)S(1)} %get-tuple-element.50.refs_1_), channel_id=1, source_target_pairs={{12,4},{13,5},{14,6},{15,7},{28,20},{29,21},{30,22},{31,23}} | collective-permute-start | bytes 786440 | tf_op jit(solution)/shard_map/ppermute | solution.py:639
  65.7 11.3 %collective-permute-start.25 = (bf16[128,1024]{1,0:T(8,128)(2,1)S(1)}, bf16[128,1024]{1,0:T(8,128)(2,1)S(1)}, u32[]{:S(2)}, u32[]{:S(2)}) collective-permute-start(bf16[128,1024]{1,0:T(8,128)(2,1)S(1)} %collective-permute-done.23.refs_6_), channel_id=1, source_target_pairs={{0,1},{1,0},{2,3},{3,2},{4,5},{5,4},{6,7},{7,6},{8,9},{9,8},{10,11... | collective-permute-start | bytes 786440 | tf_op jit(solution)/shard_map/ppermute | solution.py:598
  67.6 9.4 %collective-permute-start.26 = (bf16[128,1024]{1,0:T(8,128)(2,1)S(1)}, bf16[128,1024]{1,0:T(8,128)(2,1)S(1)}, u32[]{:S(2)}, u32[]{:S(2)}) collective-permute-start(bf16[128,1024]{1,0:T(8,128)(2,1)S(1)} %collective-permute-done.24.refs_7_), channel_id=1, source_target_pairs={{0,1},{1,0},{2,3},{3,2},{4,5},{5,4},{6,7},{7,6},{8,9},{9,8},{10,11... | collective-permute-start | bytes 786440 | tf_op jit(solution)/shard_map/ppermute | solution.py:598
  71.8 5.2 %collective-permute-start.21 = (s32[2,9]{1,0:T(2,128)S(1)}, s32[2,9]{1,0:T(2,128)S(1)}, u32[]{:S(2)}, u32[]{:S(2)}) collective-permute-start(s32[2,9]{1,0:T(2,128)S(1)} %copy-done.12), channel_id=1, source_target_pairs={{12,4},{13,5},{14,6},{15,7},{28,20},{29,21},{30,22},{31,23}} | collective-permute-start | bytes 224 | tf_op jit(solution)/shard_map/ppermute | solution.py:639
  75.6 14.4 %collective-permute-start.19 = (bf16[256,512]{1,0:T(8,128)(2,1)S(1)}, bf16[256,512]{1,0:T(8,128)(2,1)S(1)}, u32[]{:S(2)}, u32[]{:S(2)}) collective-permute-start(bf16[256,512]{1,0:T(8,128)(2,1)S(1)} %get-tuple-element.62), channel_id=1, source_target_pairs={{0,2},{1,3},{2,0},{3,1},{4,6},{5,7},{6,4},{7,5},{8,10},{9,11},{10,... | collective-permute-start | bytes 786440 | tf_op jit(solution)/shard_map/ppermute | solution.py:598
  80.9 9.1 %collective-permute-start.27 = (bf16[256,512]{1,0:T(8,128)(2,1)S(1)}, bf16[256,512]{1,0:T(8,128)(2,1)S(1)}, u32[]{:S(2)}, u32[]{:S(2)}) collective-permute-start(bf16[256,512]{1,0:T(8,128)(2,1)S(1)} %get-tuple-element.64), channel_id=1, source_target_pairs={{4,12},{5,13},{6,14},{7,15},{20,28},{21,29},{22,30},{23,31}} | collective-permute-start | bytes 786440 | tf_op jit(solution)/shard_map/ppermute | solution.py:639
  85.5 4.4 %collective-permute-start.20 = (f32[8,256]{1,0:T(8,128)S(1)}, f32[8,256]{1,0:T(8,128)S(1)}, u32[]{:S(2)}, u32[]{:S(2)}) collective-permute-start(f32[8,256]{1,0:T(8,128)S(1)} %get-tuple-element.63), channel_id=1, source_target_pairs={{0,2},{1,3},{2,0},{3,1},{4,6},{5,7},{6,4},{7,5},{8,10},{9,11},{10,... | collective-permute-start | bytes 24584 | tf_op jit(solution)/shard_map/ppermute | solution.py:598
  (18 other events, 244.6 us)

commit v6 on v5

--- a/solution.py
+++ b/solution.py
@@ -428,15 +428,17 @@
     )(inner_out, qq, *states, tokens, gain.reshape(1, d), w_mq, w_mk, w_mv)
 
 
-def list_assist(frames, at, steps, planes, index, flags):
+def list_assist(frames, at, half, steps, planes, index, flags):
     me = lax.axis_index("tm")
     clear(flags)
     for f in range(frames):
 
         def act(distance, its, place, f=f):
-            @pl.when((distance == at) & (me // LANES + steps < planes))
+            apart = its ^ lax.rem(me, LANES)
+
+            @pl.when((distance == at) & (apart // 2 == half) & (me // LANES + steps < planes))
             def _():
-                flags[f, (its ^ lax.rem(me, LANES)) * frames + place] = jnp.int32(1)
+                flags[f, (apart & 1) * frames + place] = jnp.int32(1)
 
         each_live(frames, f, index, act)
 
@@ -517,7 +519,7 @@
     if assist is None:
         run()
     else:
-        _, steps, planes = assist
+        steps, planes = assist[2:]
         plane = lax.axis_index("tm") // LANES
         pl.when((plane >= 1) & (plane + steps < planes))(run)
 
@@ -642,7 +644,7 @@
 
     def onward(x, distance):
         pairs = [(p, p + 1) for p in range(distance - 1, planes - 1)]
-        return between(x, pairs + [(p, p) for p in range(distance - 1)] + [(planes - 1, distance - 1)])
+        return between(x, pairs + [(planes - 1, 0)] * (distance == 1))
 
     frames = len(kv)
     partner_q = flip(q, 2)
@@ -655,7 +657,7 @@
         if 1 <= distance <= reach:
             column = [flip(x, 2) for x in kv]
             both = [flip(x, 1) for x in column]
-            across.append(kv + near + column + both)
+            across += [(distance, 0, kv + near), (distance, 1, column + both)]
     parts = []
     if reach:
         helped = [(p, p + steps) for p in range(1, planes - steps)]
@@ -663,8 +665,11 @@
         far_q = between(q, down)
         far_pack = between(pack, down)
         far = None
-        for at, blocks in enumerate(across, 1):
-            far = attend(far_pack, 0, far_q, blocks, far, at == reach, BF16, (at, steps, planes))
+        for at, half, blocks in across:
+            last = at == reach and half == 1
+            far = attend(
+                far_pack, 0, far_q, blocks, far, last, BF16, (at, half, steps, planes)
+            )
         parts = [[between(x, helped) for x in far]]
 
     def attended(row, asked, dtype):

time: 93.6 us -> 102 us (1.090)
  starting transfers between devices: 34.8 us -> 41.6 us
  Pallas kernels: 27.3 us -> 29.4 us
    ppermute x18, starting transfers between devices: 16.9 us -> 22.7 us  [flip(): return lax.ppermute(x, 'tm', [(i, i ^ bits) for i in range(size)])]
    pallas_call x5 -> x6, Pallas kernels: 15.2 us -> 17.4 us  [attend(): pl.pallas_call(functools.partial(attend_kernel, frames, blocks, row, firs...]
    ppermute x8, waiting for transfers between devices: 10.1 us -> 8.86 us  [between(): lax.ppermute(x, 'tm', [(a * LANES + i, b * LANES + i) for a, b in pairs f...]
    ppermute x8, starting transfers between devices: 14 us -> 15.1 us  [between(): lax.ppermute(x, 'tm', [(a * LANES + i, b * LANES + i) for a, b in pairs f...]
    unnamed x26 -> x24, local copies, waits for them, and re-layouts: 4.5 us -> 4.5 us
  transfers between devices with their start and end apart: 29 -> 29, of which waited for: 11 -> 10; matrix products, arithmetic and copies ran while one was open for 0% -> 0% of each run, Pallas kernels for 21% -> 21%
where the time goes in v6:
time: 102 us; the launch traced here: 101 us
  starting transfers between devices  41.6 us (41%)
  Pallas kernels  29.4 us (29%)
  waiting for transfers between devices  24.7 us (24%)
  local copies, waits for them, and re-layouts  4.5 us (4%)
    ppermute x18, starting transfers between devices, flip(): return lax.ppermute(x, 'tm', [(i, i ^ bits) for i in range(size)])  22.7 us
    pallas_call x6, Pallas kernels, attend(): pl.pallas_call(functools.partial(attend_kernel, frames, blocks, row, firs...  17.4 us
    ppermute x8, starting transfers between devices, between(): lax.ppermute(x, 'tm', [(a * LANES + i, b * LANES + i) for a, b in pairs f...  15.1 us
    ppermute x18, waiting for transfers between devices, flip(): return lax.ppermute(x, 'tm', [(i, i ^ bits) for i in range(size)])  11.2 us
    ppermute x8, waiting for transfers between devices, between(): lax.ppermute(x, 'tm', [(a * LANES + i, b * LANES + i) for a, b in pairs f...  8.86 us
    ppermute x3, waiting for transfers between devices, up(): return lax.ppermute(x, 'tm', [(i, (i + step) % size) for i in range(size)])  4.7 us
    unnamed x24, local copies, waits for them, and re-layouts  4.5 us
    pallas_call x1, Pallas kernels, local(): pl.pallas_call(local_kernel, in_specs=[HBM] * 6, out_specs=[VMEM] * 4 + [...  3.94 us
  transfers between devices with their start and end apart: 29, of which 10 were waited for; matrix products, arithmetic and copies ran while one was open for 0% of the time, Pallas kernels for 21%

profile of v6, /device:TPU:13, one launch (start us, length us, event | category | flops | bytes accessed | tf_op | source)
XLA Modules:
  0.0 100.6 jit_solution(18293083164821553568)
XLA Ops:
  0.0 3.9 %local.1 = (bf16[256,512]{1,0:T(8,128)(2,1)}, bf16[256,1024]{1,0:T(8,128)(2,1)}, bf16[2,272,128]{2,1,0:T(8,128)(2,1)}, bf16[2,272,128]{2,1,0:T(8,128)(2,1)}, s32[2,9]{1,0:T(2,128)}) custom-call(bf16[256,1024]{1,0:T(8,128)(2,1)} %refs_4_.1, f32[8,256]{1,0:T(8,128)} %refs_1_.1, bf16[1024,512]{1,0:T(8,128)(2,1)} %wk_in.1, bf16[1024,1024]{1,0:T(8,128)(2,1)} %wv_in.1, ...), custom_call_target="tpu_custom_call" | custom-call | tf_op jit(solution)/shard_map/local/pallas_call | solution.py:174
  7.2 2.9 %collective-permute-done.2.got.refs_1_ = bf16[272,128]{1,0:T(8,128)(2,1)S(1)} collective-permute-done((bf16[272,128]{1,0:T(8,128)(2,1)S(1)}, bf16[272,128]{1,0:T(8,128)(2,1)S(1)}, u32[]{:S(2)}, u32[]{:S(2)}) %collective-permute-start.2) | collective-permute-done | bytes 69664 | tf_op jit(solution)/shard_map/ppermute | solution.py:600
  14.1 1.9 %collective-permute-done.4.refs_3_ = bf16[272,128]{1,0:T(8,128)(2,1)S(1)} collective-permute-done((bf16[272,128]{1,0:T(8,128)(2,1)S(1)}, bf16[272,128]{1,0:T(8,128)(2,1)S(1)}, u32[]{:S(2)}, u32[]{:S(2)}) %collective-permute-start.4) | collective-permute-done | bytes 69664 | tf_op jit(solution)/shard_map/ppermute | solution.py:604
  15.9 2.8 %collective-permute-done.5.refs_4_ = bf16[272,128]{1,0:T(8,128)(2,1)S(1)} collective-permute-done((bf16[272,128]{1,0:T(8,128)(2,1)S(1)}, bf16[272,128]{1,0:T(8,128)(2,1)S(1)}, u32[]{:S(2)}, u32[]{:S(2)}) %collective-permute-start.5) | collective-permute-done | bytes 69664 | tf_op jit(solution)/shard_map/ppermute | solution.py:604
  20.0 2.0 %collective-permute-done.6.got = bf16[256,128]{1,0:T(8,128)(2,1)S(1)} collective-permute-done((bf16[256,128]{1,0:T(8,128)(2,1)S(1)}, bf16[256,128]{1,0:T(8,128)(2,1)S(1)}, u32[]{:S(2)}, u32[]{:S(2)}) %collective-permute-start.6) | collective-permute-done | bytes 65568 | tf_op jit(solution)/shard_map/ppermute | solution.py:600
  23.1 2.7 %collective-permute-start.7 = (bf16[2,256,128]{2,1,0:T(8,128)(2,1)S(1)}, bf16[2,256,128]{2,1,0:T(8,128)(2,1)S(1)}, u32[]{:S(2)}, u32[]{:S(2)}) collective-permute-start(bf16[2,256,128]{2,1,0:T(8,128)(2,1)S(1)} %get-tuple-element.52), channel_id=1, source_target_pairs={{0,1},{1,0},{2,3},{3,2},{4,5},{5,4},{6,7},{7,6},{8,9},{9,8},{10,11... | collective-permute-start | bytes 393224 | tf_op jit(solution)/shard_map/ppermute | solution.py:600
  26.2 2.2 %collective-permute-done.refs_5_ = s32[2,9]{1,0:T(2,128)S(1)} collective-permute-done((s32[2,9]{1,0:T(2,128)}, s32[2,9]{1,0:T(2,128)S(1)}, u32[]{:S(2)}, u32[]{:S(2)}) %collective-permute-start) | collective-permute-done | bytes 104 | tf_op jit(solution)/shard_map/ppermute | solution.py:600
  31.0 3.7 %inner.1 = (f32[256,1024]{1,0:T(8,128)S(1)}, bf16[256,1024]{1,0:T(8,128)(2,1)S(1)}, s32[4,8]{1,0:T(4,128)S(1)}, s32[4,4]{1,0:T(4,128)S(1)}) custom-call(bf16[256,1024]{1,0:T(8,128)(2,1)S(1)} %copy-done, f32[8,256]{1,0:T(8,128)S(1)} %copy-done.9, bf16[256,512]{1,0:T(8,128)(2,1)S(1)} %copy-done.8, bf16[256,1024]{1,0:T(8,128)(2,1)S(1)} %copy-done.7, ...), custom_call_target="tpu_custom_call" | custom-call | flops 268435456 | bytes 8388608 | tf_op jit(solution)/shard_map/inner/pallas_call | solution.py:289
  34.8 2.2 %hidden.1 = (bf16[256,1024]{1,0:T(8,128)(2,1)S(1)}, bf16[256,512]{1,0:T(8,128)(2,1)S(1)}, bf16[128,1024]{1,0:T(8,128)(2,1)S(1)}, bf16[128,1024]{1,0:T(8,128)(2,1)S(1)}) custom-call(f32[256,1024]{1,0:T(8,128)S(1)} %get-tuple-element.43.refs_0_, bf16[256,1024]{1,0:T(8,128)(2,1)S(1)} %get-tuple-element.44.refs_1_, ...), custom_call_target="tpu_custom_call" | custom-call | tf_op jit(solution)/shard_map/hidden/pallas_call | solution.py:414
  37.0 2.4 %collective-permute-start.11 = (bf16[128,1024]{1,0:T(8,128)(2,1)S(1)}, bf16[128,1024]{1,0:T(8,128)(2,1)S(1)}, u32[]{:S(2)}, u32[]{:S(2)}) collective-permute-start(bf16[128,1024]{1,0:T(8,128)(2,1)S(1)} %get-tuple-element.56.refs_3_), channel_id=1, source_target_pairs={{0,4},{1,5},{2,6},{3,7},{4,8},{5,9},{6,10},{7,11},{8,12},{9,13},{1... | collective-permute-start | bytes 786440 | tf_op jit(solution)/shard_map/ppermute | solution.py:641
  42.4 7.5 %collective-permute-done.21.refs_0_ = s32[2,9]{1,0:T(2,128)S(1)} collective-permute-done((s32[2,9]{1,0:T(2,128)S(1)}, s32[2,9]{1,0:T(2,128)S(1)}, u32[]{:S(2)}, u32[]{:S(2)}) %collective-permute-start.21) | collective-permute-done | bytes 104 | tf_op jit(solution)/shard_map/ppermute | solution.py:641
  51.2 2.3 %collective-permute-start.12 = (bf16[128,1024]{1,0:T(8,128)(2,1)S(1)}, bf16[128,1024]{1,0:T(8,128)(2,1)S(1)}, u32[]{:S(2)}, u32[]{:S(2)}) collective-permute-start(bf16[128,1024]{1,0:T(8,128)(2,1)S(1)} %collective-permute-done.10.refs_6_.refs_2_), channel_id=1, source_target_pairs={{0,1},{1,0},{2,3},{3,2},{4,5},{5,4},{6,7},{7,6},{8,9},{9,8},{10,11... | collective-permute-start | bytes 786440 | tf_op jit(solution)/shard_map/ppermute | solution.py:600
  54.9 6.1 %collective-permute-start.15 = (bf16[128,1024]{1,0:T(8,128)(2,1)S(1)}, bf16[128,1024]{1,0:T(8,128)(2,1)S(1)}, u32[]{:S(2)}, u32[]{:S(2)}) collective-permute-start(bf16[128,1024]{1,0:T(8,128)(2,1)S(1)} %collective-permute-done.11.refs_7_.refs_3_), channel_id=1, source_target_pairs={{4,8},{5,9},{6,10},{7,11},{8,12},{9,13},{10,14},{11,15},{20,24},{2... | collective-permute-start | bytes 786440 | tf_op jit(solution)/shard_map/ppermute | solution.py:641
  62.7 1.8 %collective-permute-start.16 = (bf16[128,1024]{1,0:T(8,128)(2,1)S(1)}, bf16[128,1024]{1,0:T(8,128)(2,1)S(1)}, u32[]{:S(2)}, u32[]{:S(2)}) collective-permute-start(bf16[128,1024]{1,0:T(8,128)(2,1)S(1)} %collective-permute-done.14.refs_5_), channel_id=1, source_target_pairs={{0,1},{1,0},{2,3},{3,2},{4,5},{5,4},{6,7},{7,6},{8,9},{9,8},{10,11... | collective-permute-start | bytes 786440 | tf_op jit(solution)/shard_map/ppermute | solution.py:600
  68.0 3.3 %collective-permute-start.25 = (bf16[128,1024]{1,0:T(8,128)(2,1)S(1)}, bf16[128,1024]{1,0:T(8,128)(2,1)S(1)}, u32[]{:S(2)}, u32[]{:S(2)}) collective-permute-start(bf16[128,1024]{1,0:T(8,128)(2,1)S(1)} %collective-permute-done.23.refs_5_), channel_id=1, source_target_pairs={{0,1},{1,0},{2,3},{3,2},{4,5},{5,4},{6,7},{7,6},{8,9},{9,8},{10,11... | collective-permute-start | bytes 786440 | tf_op jit(solution)/shard_map/ppermute | solution.py:600
  71.3 2.3 %collective-permute-done.24.refs_6_ = bf16[128,1024]{1,0:T(8,128)(2,1)S(1)} collective-permute-done((bf16[128,1024]{1,0:T(8,128)(2,1)S(1)}, bf16[128,1024]{1,0:T(8,128)(2,1)S(1)}, u32[]{:S(2)}, u32[]{:S(2)}) %collective-permute-start.24) | collective-permute-done | bytes 262176 | tf_op jit(solution)/shard_map/ppermute | solution.py:600
  73.6 3.3 %collective-permute-start.26 = (bf16[128,1024]{1,0:T(8,128)(2,1)S(1)}, bf16[128,1024]{1,0:T(8,128)(2,1)S(1)}, u32[]{:S(2)}, u32[]{:S(2)}) collective-permute-start(bf16[128,1024]{1,0:T(8,128)(2,1)S(1)} %collective-permute-done.24.refs_6_), channel_id=1, source_target_pairs={{0,1},{1,0},{2,3},{3,2},{4,5},{5,4},{6,7},{7,6},{8,9},{9,8},{10,11... | collective-permute-start | bytes 786440 | tf_op jit(solution)/shard_map/ppermute | solution.py:600
  76.9 3.1 %assist.2 = (f32[256,512]{1,0:T(8,128)S(1)}, f32[1024,128]{1,0:T(8,128)S(1)}, f32[1024,128]{1,0:T(8,128)S(1)}) custom-call(s32[2,9]{1,0:T(2,128)S(1)} %collective-permute-done.21.refs_0_, bf16[256,512]{1,0:T(8,128)(2,1)S(1)} %collective-permute-done.22.refs_1_, bf16[128,1024]{1,0:T(8,128)(2,1)S(1)} %collective-permute-done.10.refs_6_.refs_2_, ...), custom_call_target="tpu_custom_call" | custom-call | flops 268435456 | bytes 1048576 | tf_op jit(solution)/shard_map/assist/pallas_call | solution.py:544
  80.0 3.2 %attend.3 = (f32[256,512]{1,0:T(8,128)S(1)}, f32[1024,128]{1,0:T(8,128)S(1)}, f32[1024,128]{1,0:T(8,128)S(1)}) custom-call(s32[4,8]{1,0:T(4,128)S(1)} %get-tuple-element.54.refs_0_, bf16[256,512]{1,0:T(8,128)(2,1)S(1)} %collective-permute-done.18.refs_1_, bf16[128,1024]{1,0:T(8,128)(2,1)S(1)} %get-tuple-element.55.refs_2_, ...), custom_call_target="tpu_custom_call" | custom-call | flops 536870912 | bytes 2097152 | tf_op jit(solution)/shard_map/attend/pallas_call | solution.py:544
  83.2 2.5 %attend_last.3 = (bf16[256,512]{1,0:T(8,128)(2,1)S(1)}, f32[8,256]{1,0:T(8,128)S(1)}) custom-call(s32[4,4]{1,0:T(4,128)S(1)} %get-tuple-element.42.refs_0_, bf16[256,512]{1,0:T(8,128)(2,1)S(1)} %collective-permute-done.18.refs_1_, f32[256,512]{1,0:T(8,128)S(1)} %get-tuple-element.62.refs_2_, f32[1024,128]{1,0:T(8,128)S(1)} %get-tuple-element.63.refs_3_, ...), custom_call_target="tpu_custom_call" | custom-call | flops 268435456 | bytes 1048576 | tf_op jit(solution)/shard_map/attend_last/pallas_call | solution.py:544
  85.9 3.0 %assist.3 = (bf16[256,512]{1,0:T(8,128)(2,1)S(1)}, f32[8,256]{1,0:T(8,128)S(1)}) custom-call(s32[2,9]{1,0:T(2,128)S(1)} %collective-permute-done.21.refs_0_, bf16[256,512]{1,0:T(8,128)(2,1)S(1)} %collective-permute-done.22.refs_1_, f32[256,512]{1,0:T(8,128)S(1)} %get-tuple-element.67.refs_2_, f32[1024,128]{1,0:T(8,128)S(1)} %get-tuple-element.68.refs_3_, ...), custom_call_target="tpu_custom_call" | custom-call | flops 268435456 | bytes 1048576 | tf_op jit(solution)/shard_map/assist/pallas_call | solution.py:544
  90.4 3.2 %attend.2 = (f32[256,512]{1,0:T(8,128)S(1)}, f32[1024,128]{1,0:T(8,128)S(1)}, f32[1024,128]{1,0:T(8,128)S(1)}) custom-call(s32[4,8]{1,0:T(4,128)S(1)} %get-tuple-element.54.refs_0_, bf16[256,512]{1,0:T(8,128)(2,1)S(1)} %get-tuple-element.53.refs_1_, bf16[128,1024]{1,0:T(8,128)(2,1)S(1)} %get-tuple-element.55.refs_2_, ...), custom_call_target="tpu_custom_call" | custom-call | flops 536870912 | bytes 2097152 | tf_op jit(solution)/shard_map/attend/pallas_call | solution.py:544
  96.2 2.5 %attend_last.2 = (f32[256,512]{1,0:T(8,128)S(1)}, f32[8,256]{1,0:T(8,128)S(1)}) custom-call(s32[4,4]{1,0:T(4,128)S(1)} %get-tuple-element.42.refs_0_, bf16[256,512]{1,0:T(8,128)(2,1)S(1)} %get-tuple-element.53.refs_1_, f32[256,512]{1,0:T(8,128)S(1)} %get-tuple-element.57.refs_2_, f32[1024,128]{1,0:T(8,128)S(1)} %get-tuple-element.58.refs_3_, ...), custom_call_target="tpu_custom_call" | custom-call | flops 268435456 | bytes 1048576 | tf_op jit(solution)/shard_map/attend_last/pallas_call | solution.py:544
  98.7 1.9 %output.1 = bf16[256,1024]{1,0:T(8,128)(2,1)} custom-call(f32[256,512]{1,0:T(8,128)S(1)} %get-tuple-element.60.refs_0_, f32[8,256]{1,0:T(8,128)S(1)} %get-tuple-element.61.refs_1_, bf16[256,512]{1,0:T(8,128)(2,1)S(1)} %collective-permute-done.19.refs_2_, f32[8,256]{1,0:T(8,128)S(1)} %collective-permute-done.20.refs_3_, ...), custom_call_target="tpu_custom_call" | custom-call | tf_op jit(solution)/shard_map/output/pallas_call | solution.py:581
  (72 shorter events, 27.7 us)
Async XLA Ops:
  10.2 3.8 %collective-permute-start.3 = (bf16[272,128]{1,0:T(8,128)(2,1)S(1)}, bf16[272,128]{1,0:T(8,128)(2,1)S(1)}, u32[]{:S(2)}, u32[]{:S(2)}) collective-permute-start(bf16[272,128]{1,0:T(8,128)(2,1)S(1)} %shard_map.119), channel_id=1, source_target_pairs={{0,4},{1,5},{2,6},{3,7},{4,8},{5,9},{6,10},{7,11},{8,12},{9,13},{1... | collective-permute-start | bytes 208904 | tf_op jit(solution)/shard_map/ppermute | solution.py:604
  11.6 4.3 %collective-permute-start.4 = (bf16[272,128]{1,0:T(8,128)(2,1)S(1)}, bf16[272,128]{1,0:T(8,128)(2,1)S(1)}, u32[]{:S(2)}, u32[]{:S(2)}) collective-permute-start(bf16[272,128]{1,0:T(8,128)(2,1)S(1)} %shard_map.119), channel_id=1, source_target_pairs={{0,8},{1,9},{2,10},{3,11},{4,12},{5,13},{6,14},{7,15},{8,0},{9,1},... | collective-permute-start | bytes 208904 | tf_op jit(solution)/shard_map/ppermute | solution.py:604
  12.7 6.1 %collective-permute-start.5 = (bf16[272,128]{1,0:T(8,128)(2,1)S(1)}, bf16[272,128]{1,0:T(8,128)(2,1)S(1)}, u32[]{:S(2)}, u32[]{:S(2)}) collective-permute-start(bf16[272,128]{1,0:T(8,128)(2,1)S(1)} %shard_map.119), channel_id=1, source_target_pairs={{0,12},{1,13},{2,14},{3,15},{4,0},{5,1},{6,2},{7,3},{8,4},{9,5},{1... | collective-permute-start | bytes 208904 | tf_op jit(solution)/shard_map/ppermute | solution.py:604
  23.1 11.7 %collective-permute-start.7 = (bf16[2,256,128]{2,1,0:T(8,128)(2,1)S(1)}, bf16[2,256,128]{2,1,0:T(8,128)(2,1)S(1)}, u32[]{:S(2)}, u32[]{:S(2)}) collective-permute-start(bf16[2,256,128]{2,1,0:T(8,128)(2,1)S(1)} %get-tuple-element.52), channel_id=1, source_target_pairs={{0,1},{1,0},{2,3},{3,2},{4,5},{5,4},{6,7},{7,6},{8,9},{9,8},{10,11... | collective-permute-start | bytes 393224 | tf_op jit(solution)/shard_map/ppermute | solution.py:600
  37.0 14.2 %collective-permute-start.10 = (bf16[128,1024]{1,0:T(8,128)(2,1)S(1)}, bf16[128,1024]{1,0:T(8,128)(2,1)S(1)}, u32[]{:S(2)}, u32[]{:S(2)}) collective-permute-start(bf16[128,1024]{1,0:T(8,128)(2,1)S(1)} %get-tuple-element.55.refs_2_), channel_id=1, source_target_pairs={{0,4},{1,5},{2,6},{3,7},{4,8},{5,9},{6,10},{7,11},{8,12},{9,13},{1... | collective-permute-start | bytes 786440 | tf_op jit(solution)/shard_map/ppermute | solution.py:641
  37.0 16.5 %collective-permute-start.11 = (bf16[128,1024]{1,0:T(8,128)(2,1)S(1)}, bf16[128,1024]{1,0:T(8,128)(2,1)S(1)}, u32[]{:S(2)}, u32[]{:S(2)}) collective-permute-start(bf16[128,1024]{1,0:T(8,128)(2,1)S(1)} %get-tuple-element.56.refs_3_), channel_id=1, source_target_pairs={{0,4},{1,5},{2,6},{3,7},{4,8},{5,9},{6,10},{7,11},{8,12},{9,13},{1... | collective-permute-start | bytes 786440 | tf_op jit(solution)/shard_map/ppermute | solution.py:641
  39.5 14.1 %collective-permute-start.8 = (bf16[128,1024]{1,0:T(8,128)(2,1)S(1)}, bf16[128,1024]{1,0:T(8,128)(2,1)S(1)}, u32[]{:S(2)}, u32[]{:S(2)}) collective-permute-start(bf16[128,1024]{1,0:T(8,128)(2,1)S(1)} %get-tuple-element.55.refs_2_), channel_id=1, source_target_pairs={{0,1},{1,0},{2,3},{3,2},{4,5},{5,4},{6,7},{7,6},{8,9},{9,8},{10,11... | collective-permute-start | bytes 786440 | tf_op jit(solution)/shard_map/ppermute | solution.py:600
  41.1 13.8 %collective-permute-start.9 = (bf16[128,1024]{1,0:T(8,128)(2,1)S(1)}, bf16[128,1024]{1,0:T(8,128)(2,1)S(1)}, u32[]{:S(2)}, u32[]{:S(2)}) collective-permute-start(bf16[128,1024]{1,0:T(8,128)(2,1)S(1)} %get-tuple-element.56.refs_3_), channel_id=1, source_target_pairs={{0,1},{1,0},{2,3},{3,2},{4,5},{5,4},{6,7},{7,6},{8,9},{9,8},{10,11... | collective-permute-start | bytes 786440 | tf_op jit(solution)/shard_map/ppermute | solution.py:600
  41.1 8.8 %collective-permute-start.21 = (s32[2,9]{1,0:T(2,128)S(1)}, s32[2,9]{1,0:T(2,128)S(1)}, u32[]{:S(2)}, u32[]{:S(2)}) collective-permute-start(s32[2,9]{1,0:T(2,128)S(1)} %copy-done.11), channel_id=1, source_target_pairs={{12,4},{13,5},{14,6},{15,7},{28,20},{29,21},{30,22},{31,23}} | collective-permute-start | bytes 224 | tf_op jit(solution)/shard_map/ppermute | solution.py:641
  49.9 11.1 %collective-permute-start.22 = (bf16[256,512]{1,0:T(8,128)(2,1)S(1)}, bf16[256,512]{1,0:T(8,128)(2,1)S(1)}, u32[]{:S(2)}, u32[]{:S(2)}) collective-permute-start(bf16[256,512]{1,0:T(8,128)(2,1)S(1)} %get-tuple-element.53.refs_1_), channel_id=1, source_target_pairs={{12,4},{13,5},{14,6},{15,7},{28,20},{29,21},{30,22},{31,23}} | collective-permute-start | bytes 786440 | tf_op jit(solution)/shard_map/ppermute | solution.py:641
  51.2 10.1 %collective-permute-start.12 = (bf16[128,1024]{1,0:T(8,128)(2,1)S(1)}, bf16[128,1024]{1,0:T(8,128)(2,1)S(1)}, u32[]{:S(2)}, u32[]{:S(2)}) collective-permute-start(bf16[128,1024]{1,0:T(8,128)(2,1)S(1)} %collective-permute-done.10.refs_6_.refs_2_), channel_id=1, source_target_pairs={{0,1},{1,0},{2,3},{3,2},{4,5},{5,4},{6,7},{7,6},{8,9},{9,8},{10,11... | collective-permute-start | bytes 786440 | tf_op jit(solution)/shard_map/ppermute | solution.py:600
  53.5 9.0 %collective-permute-start.13 = (bf16[128,1024]{1,0:T(8,128)(2,1)S(1)}, bf16[128,1024]{1,0:T(8,128)(2,1)S(1)}, u32[]{:S(2)}, u32[]{:S(2)}) collective-permute-start(bf16[128,1024]{1,0:T(8,128)(2,1)S(1)} %collective-permute-done.11.refs_7_.refs_3_), channel_id=1, source_target_pairs={{0,1},{1,0},{2,3},{3,2},{4,5},{5,4},{6,7},{7,6},{8,9},{9,8},{10,11... | collective-permute-start | bytes 786440 | tf_op jit(solution)/shard_map/ppermute | solution.py:600
  53.6 9.1 %collective-permute-start.14 = (bf16[128,1024]{1,0:T(8,128)(2,1)S(1)}, bf16[128,1024]{1,0:T(8,128)(2,1)S(1)}, u32[]{:S(2)}, u32[]{:S(2)}) collective-permute-start(bf16[128,1024]{1,0:T(8,128)(2,1)S(1)} %collective-permute-done.10.refs_6_.refs_2_), channel_id=1, source_target_pairs={{4,8},{5,9},{6,10},{7,11},{8,12},{9,13},{10,14},{11,15},{20,24},{2... | collective-permute-start | bytes 786440 | tf_op jit(solution)/shard_map/ppermute | solution.py:641
  54.9 11.0 %collective-permute-start.15 = (bf16[128,1024]{1,0:T(8,128)(2,1)S(1)}, bf16[128,1024]{1,0:T(8,128)(2,1)S(1)}, u32[]{:S(2)}, u32[]{:S(2)}) collective-permute-start(bf16[128,1024]{1,0:T(8,128)(2,1)S(1)} %collective-permute-done.11.refs_7_.refs_3_), channel_id=1, source_target_pairs={{4,8},{5,9},{6,10},{7,11},{8,12},{9,13},{10,14},{11,15},{20,24},{2... | collective-permute-start | bytes 786440 | tf_op jit(solution)/shard_map/ppermute | solution.py:641
  61.0 6.9 %collective-permute-start.23 = (bf16[128,1024]{1,0:T(8,128)(2,1)S(1)}, bf16[128,1024]{1,0:T(8,128)(2,1)S(1)}, u32[]{:S(2)}, u32[]{:S(2)}) collective-permute-start(bf16[128,1024]{1,0:T(8,128)(2,1)S(1)} %collective-permute-done.10.refs_6_.refs_2_), channel_id=1, source_target_pairs={{0,2},{1,3},{2,0},{3,1},{4,6},{5,7},{6,4},{7,5},{8,10},{9,11},{10,... | collective-permute-start | bytes 786440 | tf_op jit(solution)/shard_map/ppermute | solution.py:600
  61.3 12.3 %collective-permute-start.24 = (bf16[128,1024]{1,0:T(8,128)(2,1)S(1)}, bf16[128,1024]{1,0:T(8,128)(2,1)S(1)}, u32[]{:S(2)}, u32[]{:S(2)}) collective-permute-start(bf16[128,1024]{1,0:T(8,128)(2,1)S(1)} %collective-permute-done.11.refs_7_.refs_3_), channel_id=1, source_target_pairs={{0,2},{1,3},{2,0},{3,1},{4,6},{5,7},{6,4},{7,5},{8,10},{9,11},{10,... | collective-permute-start | bytes 786440 | tf_op jit(solution)/shard_map/ppermute | solution.py:600
  62.6 17.4 %collective-permute-start.18 = (bf16[256,512]{1,0:T(8,128)(2,1)S(1)}, bf16[256,512]{1,0:T(8,128)(2,1)S(1)}, u32[]{:S(2)}, u32[]{:S(2)}) collective-permute-start(bf16[256,512]{1,0:T(8,128)(2,1)S(1)} %get-tuple-element.53.refs_1_), channel_id=1, source_target_pairs={{0,2},{1,3},{2,0},{3,1},{4,6},{5,7},{6,4},{7,5},{8,10},{9,11},{10,... | collective-permute-start | bytes 786440 | tf_op jit(solution)/shard_map/ppermute | solution.py:600
  62.7 20.4 %collective-permute-start.16 = (bf16[128,1024]{1,0:T(8,128)(2,1)S(1)}, bf16[128,1024]{1,0:T(8,128)(2,1)S(1)}, u32[]{:S(2)}, u32[]{:S(2)}) collective-permute-start(bf16[128,1024]{1,0:T(8,128)(2,1)S(1)} %collective-permute-done.14.refs_5_), channel_id=1, source_target_pairs={{0,1},{1,0},{2,3},{3,2},{4,5},{5,4},{6,7},{7,6},{8,9},{9,8},{10,11... | collective-permute-start | bytes 786440 | tf_op jit(solution)/shard_map/ppermute | solution.py:600
  65.9 17.2 %collective-permute-start.17 = (bf16[128,1024]{1,0:T(8,128)(2,1)S(1)}, bf16[128,1024]{1,0:T(8,128)(2,1)S(1)}, u32[]{:S(2)}, u32[]{:S(2)}) collective-permute-start(bf16[128,1024]{1,0:T(8,128)(2,1)S(1)} %collective-permute-done.15.refs_6_), channel_id=1, source_target_pairs={{0,1},{1,0},{2,3},{3,2},{4,5},{5,4},{6,7},{7,6},{8,9},{9,8},{10,11... | collective-permute-start | bytes 786440 | tf_op jit(solution)/shard_map/ppermute | solution.py:600
  68.0 18.0 %collective-permute-start.25 = (bf16[128,1024]{1,0:T(8,128)(2,1)S(1)}, bf16[128,1024]{1,0:T(8,128)(2,1)S(1)}, u32[]{:S(2)}, u32[]{:S(2)}) collective-permute-start(bf16[128,1024]{1,0:T(8,128)(2,1)S(1)} %collective-permute-done.23.refs_5_), channel_id=1, source_target_pairs={{0,1},{1,0},{2,3},{3,2},{4,5},{5,4},{6,7},{7,6},{8,9},{9,8},{10,11... | collective-permute-start | bytes 786440 | tf_op jit(solution)/shard_map/ppermute | solution.py:600
  73.6 12.4 %collective-permute-start.26 = (bf16[128,1024]{1,0:T(8,128)(2,1)S(1)}, bf16[128,1024]{1,0:T(8,128)(2,1)S(1)}, u32[]{:S(2)}, u32[]{:S(2)}) collective-permute-start(bf16[128,1024]{1,0:T(8,128)(2,1)S(1)} %collective-permute-done.24.refs_6_), channel_id=1, source_target_pairs={{0,1},{1,0},{2,3},{3,2},{4,5},{5,4},{6,7},{7,6},{8,9},{9,8},{10,11... | collective-permute-start | bytes 786440 | tf_op jit(solution)/shard_map/ppermute | solution.py:600
  85.7 13.0 %collective-permute-start.19 = (bf16[256,512]{1,0:T(8,128)(2,1)S(1)}, bf16[256,512]{1,0:T(8,128)(2,1)S(1)}, u32[]{:S(2)}, u32[]{:S(2)}) collective-permute-start(bf16[256,512]{1,0:T(8,128)(2,1)S(1)} %get-tuple-element.65), channel_id=1, source_target_pairs={{0,2},{1,3},{2,0},{3,1},{4,6},{5,7},{6,4},{7,5},{8,10},{9,11},{10,... | collective-permute-start | bytes 786440 | tf_op jit(solution)/shard_map/ppermute | solution.py:600
  88.9 9.8 %collective-permute-start.27 = (bf16[256,512]{1,0:T(8,128)(2,1)S(1)}, bf16[256,512]{1,0:T(8,128)(2,1)S(1)}, u32[]{:S(2)}, u32[]{:S(2)}) collective-permute-start(bf16[256,512]{1,0:T(8,128)(2,1)S(1)} %get-tuple-element.70), channel_id=1, source_target_pairs={{4,12},{5,13},{6,14},{7,15},{20,28},{21,29},{22,30},{23,31}} | collective-permute-start | bytes 786440 | tf_op jit(solution)/shard_map/ppermute | solution.py:641
  93.6 5.1 %collective-permute-start.20 = (f32[8,256]{1,0:T(8,128)S(1)}, f32[8,256]{1,0:T(8,128)S(1)}, u32[]{:S(2)}, u32[]{:S(2)}) collective-permute-start(f32[8,256]{1,0:T(8,128)S(1)} %get-tuple-element.66), channel_id=1, source_target_pairs={{0,2},{1,3},{2,0},{3,1},{4,6},{5,7},{6,4},{7,5},{8,10},{9,11},{10,... | collective-permute-start | bytes 24584 | tf_op jit(solution)/shard_map/ppermute | solution.py:600
  (17 other events, 210.5 us)

commit v7 on v6

--- a/solution.py
+++ b/solution.py
@@ -198,13 +198,9 @@
 
 
 def clear(flags):
-    rows, blocks = flags.shape
-
-    def one(i, _):
-        flags[i // blocks, lax.rem(i, blocks)] = jnp.int32(0)
-        return 0
-
-    lax.fori_loop(0, rows * blocks, one, 0)
+    for row in range(flags.shape[0]):
+        for block in range(flags.shape[1]):
+            flags[row, block] = jnp.int32(0)
 
 
 def each_live(frames, f, index, act):
@@ -464,8 +460,7 @@
         if assist is not None:
             list_assist(frames, *assist, index, live)
         lane = lax.broadcasted_iota(jnp.int32, (rows, 128), 1)
-        if last:
-            stat[...] = jnp.zeros_like(stat)
+        kept = []
         for e in range(MH):
             cols, vcols = slice(e * MD, (e + 1) * MD), slice(MC + e * MD, MC + (e + 1) * MD)
             held = slice(e * rows, (e + 1) * rows)
@@ -477,7 +472,7 @@
                     for f in range(frames):
                         part = s[spans[f], j * P_SIZE : (j + 1) * P_SIZE]
                         part = jnp.where(live[row + f, b] == 1, part, NEG)
-                        scores[spans[f], b * P_SIZE : (b + 1) * P_SIZE] = part
+                        scores[e, spans[f], b * P_SIZE : (b + 1) * P_SIZE] = part
                         tops[f] = part if tops[f] is None else jnp.maximum(tops[f], part)
             top = jnp.concatenate([jnp.max(t, axis=1, keepdims=True) for t in tops], axis=0)
             top = jnp.broadcast_to(jnp.maximum(top, 0.1 * NEG), (rows, 128))
@@ -489,7 +484,7 @@
             for pair in pairs:
                 ps = []
                 for b in pair:
-                    p = jnp.exp2((scores[:, b * P_SIZE : (b + 1) * P_SIZE] - top) * base2)
+                    p = jnp.exp2((scores[e, :, b * P_SIZE : (b + 1) * P_SIZE] - top) * base2)
                     total = p if total is None else total + p
                     ps.append(p.astype(BF16))
                 part = nn(
@@ -504,14 +499,16 @@
                 whole = jnp.broadcast_to(jnp.sum(total, axis=1, keepdims=True), (rows, 128))
                 whole = jnp.maximum(whole, 1e-30)
                 outs[0][:, cols] = (acc / whole).astype(outs[0].dtype)
-                stat[...] = jnp.where(
-                    lane == e, top, jnp.where(lane == MH + e, whole, stat[...])
-                )
+                kept.append((top, whole))
             else:
                 outs[0][:, cols] = acc
                 outs[1][held, :] = top
                 outs[2][held, :] = total
         if last:
+            merged = jnp.zeros((rows, 128), F32)
+            for e, (top, whole) in enumerate(kept):
+                merged = jnp.where(lane == e, top, jnp.where(lane == MH + e, whole, merged))
+            stat[...] = merged
             flat = jnp.transpose(stat[...])
             low = jnp.log(flat[MH : 2 * MH])
             outs[1][...] = jnp.concatenate([flat[:MH] * scale + low, low], axis=0)
@@ -538,7 +535,7 @@
     else:
         out_shape = [jax.ShapeDtypeStruct((rows, MC), F32)]
         out_shape += [jax.ShapeDtypeStruct((MH * rows, 128), F32)] * 2
-    scratch = [pltpu.VMEM((rows, blocks * P_SIZE), F32), pltpu.VMEM((rows, 128), F32)]
+    scratch = [pltpu.VMEM((MH, rows, blocks * P_SIZE), F32), pltpu.VMEM((rows, 128), F32)]
     if assist is not None:
         scratch.append(pltpu.SMEM((frames, blocks), jnp.int32))
     return pl.pallas_call(

time: 102 us -> 101 us (level)
  transfers between devices with their start and end apart: 29 -> 29, of which waited for: 10 -> 10; matrix products, arithmetic and copies ran while one was open for 0% -> 0% of each run, Pallas kernels for 21% -> 20%
where the time goes in v7:
time: 101 us; the launch traced here: 100 us
  starting transfers between devices  41.6 us (41%)
  Pallas kernels  28.8 us (29%)
  waiting for transfers between devices  24.7 us (24%)
  local copies, waits for them, and re-layouts  4.5 us (4%)
    ppermute x18, starting transfers between devices, flip(): return lax.ppermute(x, 'tm', [(i, i ^ bits) for i in range(size)])  22.7 us
    pallas_call x6, Pallas kernels, attend(): pl.pallas_call(functools.partial(attend_kernel, frames, blocks, row, firs...  17.2 us
    ppermute x8, starting transfers between devices, between(): lax.ppermute(x, 'tm', [(a * LANES + i, b * LANES + i) for a, b in pairs f...  15.1 us
    ppermute x18, waiting for transfers between devices, flip(): return lax.ppermute(x, 'tm', [(i, i ^ bits) for i in range(size)])  11.2 us
    ppermute x8, waiting for transfers between devices, between(): lax.ppermute(x, 'tm', [(a * LANES + i, b * LANES + i) for a, b in pairs f...  8.86 us
    ppermute x3, waiting for transfers between devices, up(): return lax.ppermute(x, 'tm', [(i, (i + step) % size) for i in range(size)])  4.7 us
    unnamed x24, local copies, waits for them, and re-layouts  4.5 us
    pallas_call x1, Pallas kernels, local(): pl.pallas_call(local_kernel, in_specs=[HBM] * 6, out_specs=[VMEM] * 4 + [...  3.94 us
  transfers between devices with their start and end apart: 29, of which 10 were waited for; matrix products, arithmetic and copies ran while one was open for 0% of the time, Pallas kernels for 20%

profile of v7, /device:TPU:13, one launch (start us, length us, event | category | flops | bytes accessed | tf_op | source)
XLA Modules:
  0.0 100.0 jit_solution(3113209159885501337)
XLA Ops:
  0.0 3.9 %local.1 = (bf16[256,512]{1,0:T(8,128)(2,1)}, bf16[256,1024]{1,0:T(8,128)(2,1)}, bf16[2,272,128]{2,1,0:T(8,128)(2,1)}, bf16[2,272,128]{2,1,0:T(8,128)(2,1)}, s32[2,9]{1,0:T(2,128)}) custom-call(bf16[256,1024]{1,0:T(8,128)(2,1)} %refs_4_.1, f32[8,256]{1,0:T(8,128)} %refs_1_.1, bf16[1024,512]{1,0:T(8,128)(2,1)} %wk_in.1, bf16[1024,1024]{1,0:T(8,128)(2,1)} %wv_in.1, ...), custom_call_target="tpu_custom_call" | custom-call | tf_op jit(solution)/shard_map/local/pallas_call | solution.py:174
  7.2 2.9 %collective-permute-done.2.got.refs_1_ = bf16[272,128]{1,0:T(8,128)(2,1)S(1)} collective-permute-done((bf16[272,128]{1,0:T(8,128)(2,1)S(1)}, bf16[272,128]{1,0:T(8,128)(2,1)S(1)}, u32[]{:S(2)}, u32[]{:S(2)}) %collective-permute-start.2) | collective-permute-done | bytes 69664 | tf_op jit(solution)/shard_map/ppermute | solution.py:597
  14.1 1.9 %collective-permute-done.4.refs_3_ = bf16[272,128]{1,0:T(8,128)(2,1)S(1)} collective-permute-done((bf16[272,128]{1,0:T(8,128)(2,1)S(1)}, bf16[272,128]{1,0:T(8,128)(2,1)S(1)}, u32[]{:S(2)}, u32[]{:S(2)}) %collective-permute-start.4) | collective-permute-done | bytes 69664 | tf_op jit(solution)/shard_map/ppermute | solution.py:601
  15.9 2.8 %collective-permute-done.5.refs_4_ = bf16[272,128]{1,0:T(8,128)(2,1)S(1)} collective-permute-done((bf16[272,128]{1,0:T(8,128)(2,1)S(1)}, bf16[272,128]{1,0:T(8,128)(2,1)S(1)}, u32[]{:S(2)}, u32[]{:S(2)}) %collective-permute-start.5) | collective-permute-done | bytes 69664 | tf_op jit(solution)/shard_map/ppermute | solution.py:601
  20.0 2.0 %collective-permute-done.6.got = bf16[256,128]{1,0:T(8,128)(2,1)S(1)} collective-permute-done((bf16[256,128]{1,0:T(8,128)(2,1)S(1)}, bf16[256,128]{1,0:T(8,128)(2,1)S(1)}, u32[]{:S(2)}, u32[]{:S(2)}) %collective-permute-start.6) | collective-permute-done | bytes 65568 | tf_op jit(solution)/shard_map/ppermute | solution.py:597
  23.1 2.7 %collective-permute-start.7 = (bf16[2,256,128]{2,1,0:T(8,128)(2,1)S(1)}, bf16[2,256,128]{2,1,0:T(8,128)(2,1)S(1)}, u32[]{:S(2)}, u32[]{:S(2)}) collective-permute-start(bf16[2,256,128]{2,1,0:T(8,128)(2,1)S(1)} %get-tuple-element.52), channel_id=1, source_target_pairs={{0,1},{1,0},{2,3},{3,2},{4,5},{5,4},{6,7},{7,6},{8,9},{9,8},{10,11... | collective-permute-start | bytes 393224 | tf_op jit(solution)/shard_map/ppermute | solution.py:597
  26.2 2.2 %collective-permute-done.refs_5_ = s32[2,9]{1,0:T(2,128)S(1)} collective-permute-done((s32[2,9]{1,0:T(2,128)}, s32[2,9]{1,0:T(2,128)S(1)}, u32[]{:S(2)}, u32[]{:S(2)}) %collective-permute-start) | collective-permute-done | bytes 104 | tf_op jit(solution)/shard_map/ppermute | solution.py:597
  31.0 3.2 %inner.1 = (f32[256,1024]{1,0:T(8,128)S(1)}, bf16[256,1024]{1,0:T(8,128)(2,1)S(1)}, s32[4,8]{1,0:T(4,128)S(1)}, s32[4,4]{1,0:T(4,128)S(1)}) custom-call(bf16[256,1024]{1,0:T(8,128)(2,1)S(1)} %copy-done, f32[8,256]{1,0:T(8,128)S(1)} %copy-done.9, bf16[256,512]{1,0:T(8,128)(2,1)S(1)} %copy-done.8, bf16[256,1024]{1,0:T(8,128)(2,1)S(1)} %copy-done.7, ...), custom_call_target="tpu_custom_call" | custom-call | flops 268435456 | bytes 8388608 | tf_op jit(solution)/shard_map/inner/pallas_call | solution.py:285
  34.3 2.2 %hidden.1 = (bf16[256,1024]{1,0:T(8,128)(2,1)S(1)}, bf16[256,512]{1,0:T(8,128)(2,1)S(1)}, bf16[128,1024]{1,0:T(8,128)(2,1)S(1)}, bf16[128,1024]{1,0:T(8,128)(2,1)S(1)}) custom-call(f32[256,1024]{1,0:T(8,128)S(1)} %get-tuple-element.43.refs_0_, bf16[256,1024]{1,0:T(8,128)(2,1)S(1)} %get-tuple-element.44.refs_1_, ...), custom_call_target="tpu_custom_call" | custom-call | tf_op jit(solution)/shard_map/hidden/pallas_call | solution.py:410
  36.6 2.4 %collective-permute-start.11 = (bf16[128,1024]{1,0:T(8,128)(2,1)S(1)}, bf16[128,1024]{1,0:T(8,128)(2,1)S(1)}, u32[]{:S(2)}, u32[]{:S(2)}) collective-permute-start(bf16[128,1024]{1,0:T(8,128)(2,1)S(1)} %get-tuple-element.56.refs_3_), channel_id=1, source_target_pairs={{0,4},{1,5},{2,6},{3,7},{4,8},{5,9},{6,10},{7,11},{8,12},{9,13},{1... | collective-permute-start | bytes 786440 | tf_op jit(solution)/shard_map/ppermute | solution.py:638
  42.0 7.5 %collective-permute-done.21.refs_0_ = s32[2,9]{1,0:T(2,128)S(1)} collective-permute-done((s32[2,9]{1,0:T(2,128)S(1)}, s32[2,9]{1,0:T(2,128)S(1)}, u32[]{:S(2)}, u32[]{:S(2)}) %collective-permute-start.21) | collective-permute-done | bytes 104 | tf_op jit(solution)/shard_map/ppermute | solution.py:638
  50.7 2.3 %collective-permute-start.12 = (bf16[128,1024]{1,0:T(8,128)(2,1)S(1)}, bf16[128,1024]{1,0:T(8,128)(2,1)S(1)}, u32[]{:S(2)}, u32[]{:S(2)}) collective-permute-start(bf16[128,1024]{1,0:T(8,128)(2,1)S(1)} %collective-permute-done.10.refs_6_.refs_2_), channel_id=1, source_target_pairs={{0,1},{1,0},{2,3},{3,2},{4,5},{5,4},{6,7},{7,6},{8,9},{9,8},{10,11... | collective-permute-start | bytes 786440 | tf_op jit(solution)/shard_map/ppermute | solution.py:597
  54.5 6.1 %collective-permute-start.15 = (bf16[128,1024]{1,0:T(8,128)(2,1)S(1)}, bf16[128,1024]{1,0:T(8,128)(2,1)S(1)}, u32[]{:S(2)}, u32[]{:S(2)}) collective-permute-start(bf16[128,1024]{1,0:T(8,128)(2,1)S(1)} %collective-permute-done.11.refs_7_.refs_3_), channel_id=1, source_target_pairs={{4,8},{5,9},{6,10},{7,11},{8,12},{9,13},{10,14},{11,15},{20,24},{2... | collective-permute-start | bytes 786440 | tf_op jit(solution)/shard_map/ppermute | solution.py:638
  62.3 1.8 %collective-permute-start.16 = (bf16[128,1024]{1,0:T(8,128)(2,1)S(1)}, bf16[128,1024]{1,0:T(8,128)(2,1)S(1)}, u32[]{:S(2)}, u32[]{:S(2)}) collective-permute-start(bf16[128,1024]{1,0:T(8,128)(2,1)S(1)} %collective-permute-done.14.refs_5_), channel_id=1, source_target_pairs={{0,1},{1,0},{2,3},{3,2},{4,5},{5,4},{6,7},{7,6},{8,9},{9,8},{10,11... | collective-permute-start | bytes 786440 | tf_op jit(solution)/shard_map/ppermute | solution.py:597
  67.5 3.3 %collective-permute-start.25 = (bf16[128,1024]{1,0:T(8,128)(2,1)S(1)}, bf16[128,1024]{1,0:T(8,128)(2,1)S(1)}, u32[]{:S(2)}, u32[]{:S(2)}) collective-permute-start(bf16[128,1024]{1,0:T(8,128)(2,1)S(1)} %collective-permute-done.23.refs_5_), channel_id=1, source_target_pairs={{0,1},{1,0},{2,3},{3,2},{4,5},{5,4},{6,7},{7,6},{8,9},{9,8},{10,11... | collective-permute-start | bytes 786440 | tf_op jit(solution)/shard_map/ppermute | solution.py:597
  70.8 2.3 %collective-permute-done.24.refs_6_ = bf16[128,1024]{1,0:T(8,128)(2,1)S(1)} collective-permute-done((bf16[128,1024]{1,0:T(8,128)(2,1)S(1)}, bf16[128,1024]{1,0:T(8,128)(2,1)S(1)}, u32[]{:S(2)}, u32[]{:S(2)}) %collective-permute-start.24) | collective-permute-done | bytes 262176 | tf_op jit(solution)/shard_map/ppermute | solution.py:597
  73.1 3.3 %collective-permute-start.26 = (bf16[128,1024]{1,0:T(8,128)(2,1)S(1)}, bf16[128,1024]{1,0:T(8,128)(2,1)S(1)}, u32[]{:S(2)}, u32[]{:S(2)}) collective-permute-start(bf16[128,1024]{1,0:T(8,128)(2,1)S(1)} %collective-permute-done.24.refs_6_), channel_id=1, source_target_pairs={{0,1},{1,0},{2,3},{3,2},{4,5},{5,4},{6,7},{7,6},{8,9},{9,8},{10,11... | collective-permute-start | bytes 786440 | tf_op jit(solution)/shard_map/ppermute | solution.py:597
  76.4 3.0 %assist.2 = (f32[256,512]{1,0:T(8,128)S(1)}, f32[1024,128]{1,0:T(8,128)S(1)}, f32[1024,128]{1,0:T(8,128)S(1)}) custom-call(s32[2,9]{1,0:T(2,128)S(1)} %collective-permute-done.21.refs_0_, bf16[256,512]{1,0:T(8,128)(2,1)S(1)} %collective-permute-done.22.refs_1_, bf16[128,1024]{1,0:T(8,128)(2,1)S(1)} %collective-permute-done.10.refs_6_.refs_2_, ...), custom_call_target="tpu_custom_call" | custom-call | flops 268435456 | bytes 1048576 | tf_op jit(solution)/shard_map/assist/pallas_call | solution.py:541
  79.4 3.2 %attend.3 = (f32[256,512]{1,0:T(8,128)S(1)}, f32[1024,128]{1,0:T(8,128)S(1)}, f32[1024,128]{1,0:T(8,128)S(1)}) custom-call(s32[4,8]{1,0:T(4,128)S(1)} %get-tuple-element.54.refs_0_, bf16[256,512]{1,0:T(8,128)(2,1)S(1)} %collective-permute-done.18.refs_1_, bf16[128,1024]{1,0:T(8,128)(2,1)S(1)} %get-tuple-element.55.refs_2_, ...), custom_call_target="tpu_custom_call" | custom-call | flops 536870912 | bytes 2097152 | tf_op jit(solution)/shard_map/attend/pallas_call | solution.py:541
  82.6 2.5 %attend_last.3 = (bf16[256,512]{1,0:T(8,128)(2,1)S(1)}, f32[8,256]{1,0:T(8,128)S(1)}) custom-call(s32[4,4]{1,0:T(4,128)S(1)} %get-tuple-element.42.refs_0_, bf16[256,512]{1,0:T(8,128)(2,1)S(1)} %collective-permute-done.18.refs_1_, f32[256,512]{1,0:T(8,128)S(1)} %get-tuple-element.62.refs_2_, f32[1024,128]{1,0:T(8,128)S(1)} %get-tuple-element.63.refs_3_, ...), custom_call_target="tpu_custom_call" | custom-call | flops 268435456 | bytes 1048576 | tf_op jit(solution)/shard_map/attend_last/pallas_call | solution.py:541
  85.4 2.9 %assist.3 = (bf16[256,512]{1,0:T(8,128)(2,1)S(1)}, f32[8,256]{1,0:T(8,128)S(1)}) custom-call(s32[2,9]{1,0:T(2,128)S(1)} %collective-permute-done.21.refs_0_, bf16[256,512]{1,0:T(8,128)(2,1)S(1)} %collective-permute-done.22.refs_1_, f32[256,512]{1,0:T(8,128)S(1)} %get-tuple-element.67.refs_2_, f32[1024,128]{1,0:T(8,128)S(1)} %get-tuple-element.68.refs_3_, ...), custom_call_target="tpu_custom_call" | custom-call | flops 268435456 | bytes 1048576 | tf_op jit(solution)/shard_map/assist/pallas_call | solution.py:541
  89.7 3.2 %attend.2 = (f32[256,512]{1,0:T(8,128)S(1)}, f32[1024,128]{1,0:T(8,128)S(1)}, f32[1024,128]{1,0:T(8,128)S(1)}) custom-call(s32[4,8]{1,0:T(4,128)S(1)} %get-tuple-element.54.refs_0_, bf16[256,512]{1,0:T(8,128)(2,1)S(1)} %get-tuple-element.53.refs_1_, bf16[128,1024]{1,0:T(8,128)(2,1)S(1)} %get-tuple-element.55.refs_2_, ...), custom_call_target="tpu_custom_call" | custom-call | flops 536870912 | bytes 2097152 | tf_op jit(solution)/shard_map/attend/pallas_call | solution.py:541
  95.6 2.5 %attend_last.2 = (f32[256,512]{1,0:T(8,128)S(1)}, f32[8,256]{1,0:T(8,128)S(1)}) custom-call(s32[4,4]{1,0:T(4,128)S(1)} %get-tuple-element.42.refs_0_, bf16[256,512]{1,0:T(8,128)(2,1)S(1)} %get-tuple-element.53.refs_1_, f32[256,512]{1,0:T(8,128)S(1)} %get-tuple-element.57.refs_2_, f32[1024,128]{1,0:T(8,128)S(1)} %get-tuple-element.58.refs_3_, ...), custom_call_target="tpu_custom_call" | custom-call | flops 268435456 | bytes 1048576 | tf_op jit(solution)/shard_map/attend_last/pallas_call | solution.py:541
  98.1 1.9 %output.1 = bf16[256,1024]{1,0:T(8,128)(2,1)} custom-call(f32[256,512]{1,0:T(8,128)S(1)} %get-tuple-element.60.refs_0_, f32[8,256]{1,0:T(8,128)S(1)} %get-tuple-element.61.refs_1_, bf16[256,512]{1,0:T(8,128)(2,1)S(1)} %collective-permute-done.19.refs_2_, f32[8,256]{1,0:T(8,128)S(1)} %collective-permute-done.20.refs_3_, ...), custom_call_target="tpu_custom_call" | custom-call | tf_op jit(solution)/shard_map/output/pallas_call | solution.py:578
  (72 shorter events, 27.7 us)
Async XLA Ops:
  10.2 3.8 %collective-permute-start.3 = (bf16[272,128]{1,0:T(8,128)(2,1)S(1)}, bf16[272,128]{1,0:T(8,128)(2,1)S(1)}, u32[]{:S(2)}, u32[]{:S(2)}) collective-permute-start(bf16[272,128]{1,0:T(8,128)(2,1)S(1)} %shard_map.119), channel_id=1, source_target_pairs={{0,4},{1,5},{2,6},{3,7},{4,8},{5,9},{6,10},{7,11},{8,12},{9,13},{1... | collective-permute-start | bytes 208904 | tf_op jit(solution)/shard_map/ppermute | solution.py:601
  11.6 4.3 %collective-permute-start.4 = (bf16[272,128]{1,0:T(8,128)(2,1)S(1)}, bf16[272,128]{1,0:T(8,128)(2,1)S(1)}, u32[]{:S(2)}, u32[]{:S(2)}) collective-permute-start(bf16[272,128]{1,0:T(8,128)(2,1)S(1)} %shard_map.119), channel_id=1, source_target_pairs={{0,8},{1,9},{2,10},{3,11},{4,12},{5,13},{6,14},{7,15},{8,0},{9,1},... | collective-permute-start | bytes 208904 | tf_op jit(solution)/shard_map/ppermute | solution.py:601
  12.7 6.1 %collective-permute-start.5 = (bf16[272,128]{1,0:T(8,128)(2,1)S(1)}, bf16[272,128]{1,0:T(8,128)(2,1)S(1)}, u32[]{:S(2)}, u32[]{:S(2)}) collective-permute-start(bf16[272,128]{1,0:T(8,128)(2,1)S(1)} %shard_map.119), channel_id=1, source_target_pairs={{0,12},{1,13},{2,14},{3,15},{4,0},{5,1},{6,2},{7,3},{8,4},{9,5},{1... | collective-permute-start | bytes 208904 | tf_op jit(solution)/shard_map/ppermute | solution.py:601
  23.1 11.2 %collective-permute-start.7 = (bf16[2,256,128]{2,1,0:T(8,128)(2,1)S(1)}, bf16[2,256,128]{2,1,0:T(8,128)(2,1)S(1)}, u32[]{:S(2)}, u32[]{:S(2)}) collective-permute-start(bf16[2,256,128]{2,1,0:T(8,128)(2,1)S(1)} %get-tuple-element.52), channel_id=1, source_target_pairs={{0,1},{1,0},{2,3},{3,2},{4,5},{5,4},{6,7},{7,6},{8,9},{9,8},{10,11... | collective-permute-start | bytes 393224 | tf_op jit(solution)/shard_map/ppermute | solution.py:597
  36.5 14.2 %collective-permute-start.10 = (bf16[128,1024]{1,0:T(8,128)(2,1)S(1)}, bf16[128,1024]{1,0:T(8,128)(2,1)S(1)}, u32[]{:S(2)}, u32[]{:S(2)}) collective-permute-start(bf16[128,1024]{1,0:T(8,128)(2,1)S(1)} %get-tuple-element.55.refs_2_), channel_id=1, source_target_pairs={{0,4},{1,5},{2,6},{3,7},{4,8},{5,9},{6,10},{7,11},{8,12},{9,13},{1... | collective-permute-start | bytes 786440 | tf_op jit(solution)/shard_map/ppermute | solution.py:638
  36.6 16.5 %collective-permute-start.11 = (bf16[128,1024]{1,0:T(8,128)(2,1)S(1)}, bf16[128,1024]{1,0:T(8,128)(2,1)S(1)}, u32[]{:S(2)}, u32[]{:S(2)}) collective-permute-start(bf16[128,1024]{1,0:T(8,128)(2,1)S(1)} %get-tuple-element.56.refs_3_), channel_id=1, source_target_pairs={{0,4},{1,5},{2,6},{3,7},{4,8},{5,9},{6,10},{7,11},{8,12},{9,13},{1... | collective-permute-start | bytes 786440 | tf_op jit(solution)/shard_map/ppermute | solution.py:638
  39.0 14.1 %collective-permute-start.8 = (bf16[128,1024]{1,0:T(8,128)(2,1)S(1)}, bf16[128,1024]{1,0:T(8,128)(2,1)S(1)}, u32[]{:S(2)}, u32[]{:S(2)}) collective-permute-start(bf16[128,1024]{1,0:T(8,128)(2,1)S(1)} %get-tuple-element.55.refs_2_), channel_id=1, source_target_pairs={{0,1},{1,0},{2,3},{3,2},{4,5},{5,4},{6,7},{7,6},{8,9},{9,8},{10,11... | collective-permute-start | bytes 786440 | tf_op jit(solution)/shard_map/ppermute | solution.py:597
  40.7 13.8 %collective-permute-start.9 = (bf16[128,1024]{1,0:T(8,128)(2,1)S(1)}, bf16[128,1024]{1,0:T(8,128)(2,1)S(1)}, u32[]{:S(2)}, u32[]{:S(2)}) collective-permute-start(bf16[128,1024]{1,0:T(8,128)(2,1)S(1)} %get-tuple-element.56.refs_3_), channel_id=1, source_target_pairs={{0,1},{1,0},{2,3},{3,2},{4,5},{5,4},{6,7},{7,6},{8,9},{9,8},{10,11... | collective-permute-start | bytes 786440 | tf_op jit(solution)/shard_map/ppermute | solution.py:597
  40.7 8.8 %collective-permute-start.21 = (s32[2,9]{1,0:T(2,128)S(1)}, s32[2,9]{1,0:T(2,128)S(1)}, u32[]{:S(2)}, u32[]{:S(2)}) collective-permute-start(s32[2,9]{1,0:T(2,128)S(1)} %copy-done.11), channel_id=1, source_target_pairs={{12,4},{13,5},{14,6},{15,7},{28,20},{29,21},{30,22},{31,23}} | collective-permute-start | bytes 224 | tf_op jit(solution)/shard_map/ppermute | solution.py:638
  49.4 11.1 %collective-permute-start.22 = (bf16[256,512]{1,0:T(8,128)(2,1)S(1)}, bf16[256,512]{1,0:T(8,128)(2,1)S(1)}, u32[]{:S(2)}, u32[]{:S(2)}) collective-permute-start(bf16[256,512]{1,0:T(8,128)(2,1)S(1)} %get-tuple-element.53.refs_1_), channel_id=1, source_target_pairs={{12,4},{13,5},{14,6},{15,7},{28,20},{29,21},{30,22},{31,23}} | collective-permute-start | bytes 786440 | tf_op jit(solution)/shard_map/ppermute | solution.py:638
  50.7 10.1 %collective-permute-start.12 = (bf16[128,1024]{1,0:T(8,128)(2,1)S(1)}, bf16[128,1024]{1,0:T(8,128)(2,1)S(1)}, u32[]{:S(2)}, u32[]{:S(2)}) collective-permute-start(bf16[128,1024]{1,0:T(8,128)(2,1)S(1)} %collective-permute-done.10.refs_6_.refs_2_), channel_id=1, source_target_pairs={{0,1},{1,0},{2,3},{3,2},{4,5},{5,4},{6,7},{7,6},{8,9},{9,8},{10,11... | collective-permute-start | bytes 786440 | tf_op jit(solution)/shard_map/ppermute | solution.py:597
  53.1 9.0 %collective-permute-start.13 = (bf16[128,1024]{1,0:T(8,128)(2,1)S(1)}, bf16[128,1024]{1,0:T(8,128)(2,1)S(1)}, u32[]{:S(2)}, u32[]{:S(2)}) collective-permute-start(bf16[128,1024]{1,0:T(8,128)(2,1)S(1)} %collective-permute-done.11.refs_7_.refs_3_), channel_id=1, source_target_pairs={{0,1},{1,0},{2,3},{3,2},{4,5},{5,4},{6,7},{7,6},{8,9},{9,8},{10,11... | collective-permute-start | bytes 786440 | tf_op jit(solution)/shard_map/ppermute | solution.py:597
  53.1 9.1 %collective-permute-start.14 = (bf16[128,1024]{1,0:T(8,128)(2,1)S(1)}, bf16[128,1024]{1,0:T(8,128)(2,1)S(1)}, u32[]{:S(2)}, u32[]{:S(2)}) collective-permute-start(bf16[128,1024]{1,0:T(8,128)(2,1)S(1)} %collective-permute-done.10.refs_6_.refs_2_), channel_id=1, source_target_pairs={{4,8},{5,9},{6,10},{7,11},{8,12},{9,13},{10,14},{11,15},{20,24},{2... | collective-permute-start | bytes 786440 | tf_op jit(solution)/shard_map/ppermute | solution.py:638
  54.5 11.0 %collective-permute-start.15 = (bf16[128,1024]{1,0:T(8,128)(2,1)S(1)}, bf16[128,1024]{1,0:T(8,128)(2,1)S(1)}, u32[]{:S(2)}, u32[]{:S(2)}) collective-permute-start(bf16[128,1024]{1,0:T(8,128)(2,1)S(1)} %collective-permute-done.11.refs_7_.refs_3_), channel_id=1, source_target_pairs={{4,8},{5,9},{6,10},{7,11},{8,12},{9,13},{10,14},{11,15},{20,24},{2... | collective-permute-start | bytes 786440 | tf_op jit(solution)/shard_map/ppermute | solution.py:638
  60.6 6.9 %collective-permute-start.23 = (bf16[128,1024]{1,0:T(8,128)(2,1)S(1)}, bf16[128,1024]{1,0:T(8,128)(2,1)S(1)}, u32[]{:S(2)}, u32[]{:S(2)}) collective-permute-start(bf16[128,1024]{1,0:T(8,128)(2,1)S(1)} %collective-permute-done.10.refs_6_.refs_2_), channel_id=1, source_target_pairs={{0,2},{1,3},{2,0},{3,1},{4,6},{5,7},{6,4},{7,5},{8,10},{9,11},{10,... | collective-permute-start | bytes 786440 | tf_op jit(solution)/shard_map/ppermute | solution.py:597
  60.8 12.3 %collective-permute-start.24 = (bf16[128,1024]{1,0:T(8,128)(2,1)S(1)}, bf16[128,1024]{1,0:T(8,128)(2,1)S(1)}, u32[]{:S(2)}, u32[]{:S(2)}) collective-permute-start(bf16[128,1024]{1,0:T(8,128)(2,1)S(1)} %collective-permute-done.11.refs_7_.refs_3_), channel_id=1, source_target_pairs={{0,2},{1,3},{2,0},{3,1},{4,6},{5,7},{6,4},{7,5},{8,10},{9,11},{10,... | collective-permute-start | bytes 786440 | tf_op jit(solution)/shard_map/ppermute | solution.py:597
  62.1 17.3 %collective-permute-start.18 = (bf16[256,512]{1,0:T(8,128)(2,1)S(1)}, bf16[256,512]{1,0:T(8,128)(2,1)S(1)}, u32[]{:S(2)}, u32[]{:S(2)}) collective-permute-start(bf16[256,512]{1,0:T(8,128)(2,1)S(1)} %get-tuple-element.53.refs_1_), channel_id=1, source_target_pairs={{0,2},{1,3},{2,0},{3,1},{4,6},{5,7},{6,4},{7,5},{8,10},{9,11},{10,... | collective-permute-start | bytes 786440 | tf_op jit(solution)/shard_map/ppermute | solution.py:597
  62.3 20.3 %collective-permute-start.16 = (bf16[128,1024]{1,0:T(8,128)(2,1)S(1)}, bf16[128,1024]{1,0:T(8,128)(2,1)S(1)}, u32[]{:S(2)}, u32[]{:S(2)}) collective-permute-start(bf16[128,1024]{1,0:T(8,128)(2,1)S(1)} %collective-permute-done.14.refs_5_), channel_id=1, source_target_pairs={{0,1},{1,0},{2,3},{3,2},{4,5},{5,4},{6,7},{7,6},{8,9},{9,8},{10,11... | collective-permute-start | bytes 786440 | tf_op jit(solution)/shard_map/ppermute | solution.py:597
  65.5 17.2 %collective-permute-start.17 = (bf16[128,1024]{1,0:T(8,128)(2,1)S(1)}, bf16[128,1024]{1,0:T(8,128)(2,1)S(1)}, u32[]{:S(2)}, u32[]{:S(2)}) collective-permute-start(bf16[128,1024]{1,0:T(8,128)(2,1)S(1)} %collective-permute-done.15.refs_6_), channel_id=1, source_target_pairs={{0,1},{1,0},{2,3},{3,2},{4,5},{5,4},{6,7},{7,6},{8,9},{9,8},{10,11... | collective-permute-start | bytes 786440 | tf_op jit(solution)/shard_map/ppermute | solution.py:597
  67.5 17.9 %collective-permute-start.25 = (bf16[128,1024]{1,0:T(8,128)(2,1)S(1)}, bf16[128,1024]{1,0:T(8,128)(2,1)S(1)}, u32[]{:S(2)}, u32[]{:S(2)}) collective-permute-start(bf16[128,1024]{1,0:T(8,128)(2,1)S(1)} %collective-permute-done.23.refs_5_), channel_id=1, source_target_pairs={{0,1},{1,0},{2,3},{3,2},{4,5},{5,4},{6,7},{7,6},{8,9},{9,8},{10,11... | collective-permute-start | bytes 786440 | tf_op jit(solution)/shard_map/ppermute | solution.py:597
  73.1 12.3 %collective-permute-start.26 = (bf16[128,1024]{1,0:T(8,128)(2,1)S(1)}, bf16[128,1024]{1,0:T(8,128)(2,1)S(1)}, u32[]{:S(2)}, u32[]{:S(2)}) collective-permute-start(bf16[128,1024]{1,0:T(8,128)(2,1)S(1)} %collective-permute-done.24.refs_6_), channel_id=1, source_target_pairs={{0,1},{1,0},{2,3},{3,2},{4,5},{5,4},{6,7},{7,6},{8,9},{9,8},{10,11... | collective-permute-start | bytes 786440 | tf_op jit(solution)/shard_map/ppermute | solution.py:597
  85.1 13.0 %collective-permute-start.19 = (bf16[256,512]{1,0:T(8,128)(2,1)S(1)}, bf16[256,512]{1,0:T(8,128)(2,1)S(1)}, u32[]{:S(2)}, u32[]{:S(2)}) collective-permute-start(bf16[256,512]{1,0:T(8,128)(2,1)S(1)} %get-tuple-element.65), channel_id=1, source_target_pairs={{0,2},{1,3},{2,0},{3,1},{4,6},{5,7},{6,4},{7,5},{8,10},{9,11},{10,... | collective-permute-start | bytes 786440 | tf_op jit(solution)/shard_map/ppermute | solution.py:597
  88.3 9.8 %collective-permute-start.27 = (bf16[256,512]{1,0:T(8,128)(2,1)S(1)}, bf16[256,512]{1,0:T(8,128)(2,1)S(1)}, u32[]{:S(2)}, u32[]{:S(2)}) collective-permute-start(bf16[256,512]{1,0:T(8,128)(2,1)S(1)} %get-tuple-element.70), channel_id=1, source_target_pairs={{4,12},{5,13},{6,14},{7,15},{20,28},{21,29},{22,30},{23,31}} | collective-permute-start | bytes 786440 | tf_op jit(solution)/shard_map/ppermute | solution.py:638
  92.9 5.1 %collective-permute-start.20 = (f32[8,256]{1,0:T(8,128)S(1)}, f32[8,256]{1,0:T(8,128)S(1)}, u32[]{:S(2)}, u32[]{:S(2)}) collective-permute-start(f32[8,256]{1,0:T(8,128)S(1)} %get-tuple-element.66), channel_id=1, source_target_pairs={{0,2},{1,3},{2,0},{3,1},{4,6},{5,7},{6,4},{7,5},{8,10},{9,11},{10,... | collective-permute-start | bytes 24584 | tf_op jit(solution)/shard_map/ppermute | solution.py:597
  (17 other events, 209.1 us)
